TPU v7x, 256 devices: a whole 4x4x8 slice. The times are simulated.
256 devices in a mesh: dp: 64 (over x, y_hi, z), seq: 4 (over y_lo, core).
Axes of the slice: x: 4, y: 4 (y_hi: 2, y_lo: 2; y = y_hi * 2 + y_lo), z: 8, core: 2. Of those that a mesh axis runs over, the one named last changes fastest.
Arguments:
- queries: bfloat16 [64, 512, 768], P('dp', 'seq'), may hold values from -720 to 720
- key_rows: bfloat16 [64, 512, 768], P('dp', 'seq'), may hold values from -7 to 7
- value_rows: bfloat16 [64, 512, 768], P('dp', 'seq'), may hold values from -6 to 6
- conv_weight: bfloat16 [768, 3, 768], replicated, may hold values from -0.125 to 0.125
- output_gradient: bfloat16 [64, 512, 768], P('dp', 'seq'), may hold values from -16 to 16
Outputs:
- conv_out: bfloat16 [64, 512, 768], P('dp', 'seq')
- grad_queries: bfloat16 [64, 512, 768], P('dp', 'seq')
- grad_keys: bfloat16 [64, 512, 768], P('dp', 'seq')
- grad_values: bfloat16 [64, 512, 768], P('dp', 'seq')
- grad_weight: float32 [768, 3, 768], P('dp', None, 'seq')
All inputs are finite; a program needn't handle non-finite values.
Results may differ from a plain program's by a relative error of at most 0.014.
Values may be sent and summed in bfloat16 or wider, within the bound.
No kernel may reach another device: no remote copies, remote signals or barrier semaphores. Data moves between devices by JAX's collectives and lax.ppermute only.
A program may use at most 64 MiB of HBM per device.

v0:
```python
import math

import jax
import jax.numpy as jnp
from jax import lax
from jax.sharding import PartitionSpec as P

HEAD_DIM = 192
TAPS = 3
DILATION_STEP = 32


tanh_scale = 0.7978845608028654
cubic_term = 0.044715
norm_epsilon = 1e-06


def padded(block, sides, width):
    for axis, dim in sides:
        count = lax.axis_size(axis)
        forward = [(i, i + 1) for i in range(count - 1)]
        backward = [(target, source) for source, target in forward]
        low = lax.ppermute(
            lax.slice_in_dim(block, block.shape[dim] - width, None, axis=dim), axis, forward
        )
        high = lax.ppermute(lax.slice_in_dim(block, 0, width, axis=dim), axis, backward)
        block = jnp.concatenate([low, block, high], axis=dim)
    return block


def gelu_pair(value):
    inner = tanh_scale * (value + cubic_term * value * value * value)
    tangent = jnp.tanh(inner)
    result = 0.5 * value * (1.0 + tangent)
    slope = 0.5 * (1.0 + tangent) + 0.5 * value * (1.0 - tangent * tangent) * tanh_scale * (
        1.0 + 3.0 * cubic_term * value * value
    )
    return (result, slope)


def split_heads(matrix):
    return matrix.reshape(matrix.shape[0], matrix.shape[1] // HEAD_DIM, HEAD_DIM)


def attend_forward(query, keys, values):
    query_count, features = query.shape
    inverse = 1.0 / math.sqrt(HEAD_DIM)
    scores = (
        jnp.einsum(
            "qhd,khd->hqk",
            split_heads(query),
            split_heads(keys),
            preferred_element_type=jnp.float32,
        )
        * inverse
    )
    soft_exact = jax.nn.softmax(scores, axis=-1)
    soft_rounded = soft_exact.astype(jnp.bfloat16)
    attended = jnp.einsum(
        "hqk,khd->qhd", soft_rounded, split_heads(values), preferred_element_type=jnp.float32
    )
    return (soft_exact, soft_rounded, attended.reshape(query_count, features).astype(jnp.bfloat16))


def score_grads(values, soft_exact, grad_out):
    inverse = 1.0 / math.sqrt(HEAD_DIM)
    grad_soft = jnp.einsum(
        "qhd,khd->hqk",
        split_heads(grad_out),
        split_heads(values),
        preferred_element_type=jnp.float32,
    )
    row_inner = jnp.sum(grad_soft * soft_exact, axis=-1, keepdims=True)
    return (soft_exact * (grad_soft - row_inner) * inverse).astype(jnp.bfloat16)


def query_side(grad_scores, keys):
    features = keys.shape[1]
    grad_queries = jnp.einsum(
        "hqk,khd->qhd", grad_scores, split_heads(keys), preferred_element_type=jnp.float32
    )
    return grad_queries.reshape(grad_queries.shape[0], features)


def key_side(score_part, soft_part, query, grad_out):
    features = query.shape[1]
    grad_keys = jnp.einsum(
        "hqk,qhd->khd", score_part, split_heads(query), preferred_element_type=jnp.float32
    )
    grad_values = jnp.einsum(
        "hqk,qhd->khd", soft_part, split_heads(grad_out), preferred_element_type=jnp.float32
    )
    row_total = grad_keys.shape[0]
    return jnp.concatenate(
        [grad_keys.reshape(row_total, features), grad_values.reshape(row_total, features)], axis=1
    )


def body(queries, key_rows, value_rows, conv_weight, output_gradient):
    local_shard_rows = queries.shape[1]
    features = queries.shape[2]
    total_rows = lax.axis_size("dp") * lax.axis_size("seq") * local_shard_rows
    grad_scale = 1.0 / math.sqrt(total_rows)
    padded_gradient = padded(output_gradient, (("seq", 1),), DILATION_STEP)
    whole_keys, whole_values = (
        lax.all_gather(key_rows, "seq", axis=1, tiled=True),
        lax.all_gather(value_rows, "seq", axis=1, tiled=True),
    )
    soft_exact, soft_rounded, attended = attend_forward(queries[0], whole_keys[0], whole_values[0])
    att_full = attended.astype(jnp.float32)
    mean_square = jnp.mean(att_full * att_full, axis=-1, keepdims=True)
    norm_factor = lax.rsqrt(mean_square + norm_epsilon)
    normed = att_full * norm_factor
    gelu_value, gelu_slope = gelu_pair(normed)
    activation_output = gelu_value.astype(jnp.bfloat16)
    padded_input = padded(activation_output[None], (("seq", 1),), DILATION_STEP)[0]
    incoming_gradient = output_gradient[0]
    row_gradient = padded_gradient[0]
    conv_sum = jnp.zeros((local_shard_rows, conv_weight.shape[2]), jnp.float32)
    grad_acted = jnp.zeros((local_shard_rows, features), jnp.float32)
    for kernel_tap_index in range(TAPS):
        shifted_input = padded_input[
            kernel_tap_index * DILATION_STEP : kernel_tap_index * DILATION_STEP + local_shard_rows
        ]
        conv_sum = conv_sum + jnp.dot(
            shifted_input, conv_weight[:, kernel_tap_index, :], preferred_element_type=jnp.float32
        )
        reverse_rows = row_gradient[
            (2 - kernel_tap_index) * DILATION_STEP : (2 - kernel_tap_index) * DILATION_STEP
            + local_shard_rows
        ]
        grad_acted = grad_acted + jnp.einsum(
            "pc,dc->pd",
            reverse_rows,
            conv_weight[:, kernel_tap_index, :],
            preferred_element_type=jnp.float32,
        )
    conv_out = conv_sum.astype(jnp.bfloat16)
    grad_normed = grad_acted * gelu_slope
    mean_inner = jnp.mean(grad_normed * normed, axis=-1, keepdims=True)
    grad_attended = (norm_factor * (grad_normed - normed * mean_inner)).astype(jnp.bfloat16)
    grad_scores = score_grads(whole_values[0], soft_exact, grad_attended)
    grad_queries = query_side(grad_scores, whole_keys[0]).astype(jnp.bfloat16)
    grad_pair = lax.psum_scatter(
        key_side(grad_scores, soft_rounded, queries[0], grad_attended),
        "seq",
        scatter_dimension=0,
        tiled=True,
    )
    grad_keys = grad_pair[:, :features].astype(jnp.bfloat16)
    grad_values = grad_pair[:, features:].astype(jnp.bfloat16)
    grad_queries = grad_queries[None]
    grad_keys = grad_keys[None]
    grad_values = grad_values[None]
    tap_terms = [
        jnp.einsum(
            "pd,pc->dc",
            padded_input[
                kernel_tap_index * DILATION_STEP : kernel_tap_index * DILATION_STEP
                + local_shard_rows
            ],
            incoming_gradient,
            preferred_element_type=jnp.float32,
        )
        for kernel_tap_index in range(TAPS)
    ]
    partial_value = lax.psum_scatter(
        jnp.stack(tap_terms, axis=1) * grad_scale, "dp", scatter_dimension=0, tiled=True
    )
    grad_weight = lax.psum_scatter(
        partial_value.astype(jnp.bfloat16), "seq", scatter_dimension=2, tiled=True
    ).astype(jnp.float32)
    return (conv_out[None], grad_queries, grad_keys, grad_values, grad_weight)


def solution(mesh):
    return jax.shard_map(
        body,
        mesh=mesh,
        in_specs=(
            P("dp", "seq", None),
            P("dp", "seq", None),
            P("dp", "seq", None),
            P(),
            P("dp", "seq", None),
        ),
        out_specs=(
            P("dp", "seq", None),
            P("dp", "seq", None),
            P("dp", "seq", None),
            P("dp", "seq", None),
            P("dp", None, "seq"),
        ),
        check_vma=False,
    )
```

profile of v0, /device:TPU:1, one launch (start us, length us, event | category | flops | bytes accessed | tf_op | source)
XLA Modules:
  0.0 567.7 jit_solution(16866695206236518721)
XLA Ops:
  7.2 10.6 %all_gather.7 = bf16[1,512,768]{2,1,0:T(8,128)(2,1)S(1)} all-gather(bf16[1,128,768]{2,1,0:T(8,128)(2,1)} %param.7), channel_id=1, replica_groups=mesh['dp'=64,'seq'=4] {'seq'}, dimensions={1}, use_global_device_ids=true | all-gather | bytes 983040 | tf_op jit(solution)/shard_map/all_gather | solution.py:107
  18.3 9.0 %all_gather.6 = bf16[1,512,768]{2,1,0:T(8,128)(2,1)S(1)} all-gather(bf16[1,128,768]{2,1,0:T(8,128)(2,1)S(1)} %copy-done.13), channel_id=1, replica_groups=mesh['dp'=64,'seq'=4] {'seq'}, dimensions={1}, use_global_device_ids=true | all-gather | bytes 983040 | tf_op jit(solution)/shard_map/all_gather | solution.py:106
  27.6 1.5 fusion.93
  30.9 2.1 collective-permute-start.1
  33.0 3.5 collective-permute-start
  37.2 2.7 collective-permute-start.3
  39.9 2.4 collective-permute-start.2
  42.2 2.6 fusion.15
  46.8 1.8 fusion.11
  48.6 2.1 multiply_reduce_fusion.1
  50.7 1.9 multiply_convert_fusion
  52.6 1.7 copy.34
  54.3 2.6 fusion.94
  56.9 2.9 fusion.56
  59.9 6.0 %fusion.34 = f32[4,512,192]{1,2,0:T(8,128)} fusion(bf16[128,4,192]{0,2,1:T(8,128)(2,1)} %bitcast.121, f32[4,128,512]{2,1,0:T(8,128)} %fusion.94, f32[4,128,512]{2,1,0:T(8,128)} %get-tuple-element.27, f32[4,128]{1,0:T(4,128)S(1)} %get-tuple-element.26), kind=kOutput, calls=%fused_computation.40 | convolution fusion | flops 102499328 | bytes 3868672 | tf_op jit(solution)/shard_map/hqk,qhd->khd/dot_general | solution.py:87
  65.8 2.9 convolution_bitcast_fusion
  68.7 3.0 copy.36
  71.7 3.1 copy.35
  74.8 1.6 convolution_bitcast_fusion.2
  76.6 3.1 maximum_multiply_fusion
  79.7 373.2 %all-reduce.2 = bf16[768,3,768]{2,0,1:T(8,128)(2,1)} all-reduce(f32[768,3,768]{2,0,1:T(8,128)} %maximum_multiply_fusion), channel_id=3, replica_groups=mesh['dp'=64,'seq'=4] {'dp'}, use_global_device_ids=true, to_apply=%region_6.0.clone | all-reduce | flops 1769472 | bytes 10616832
  452.9 1.0 dynamic-slice_convert_fusion
  453.9 1.3 copy.41
  455.2 2.2 reshape.219
  457.7 2.1 pad_maximum_fusion
  460.8 1.7 fusion.17
  462.5 4.6 convolution_convert_fusion
  468.0 1.9 fusion.13
  469.8 2.5 fusion.25
  472.3 43.9 %reduce-scatter.8.cloned.1.call-done = bf16[192,36]{1,0:T(8,128)(2,1)} async-done(((bf16[768,36]{1,0:T(8,128)(2,1)}), bf16[192,36]{1,0:T(8,128)(2,1)}) %reduce-scatter.8.cloned.1.call-update) | async-done | bytes 13840
  517.9 41.0 %reduce-scatter.6.cloned.1.call-done = f32[128,1536]{1,0:T(8,128)} async-done(((f32[512,1536]{1,0:T(8,128)}), f32[128,1536]{1,0:T(8,128)}) %reduce-scatter.6.cloned.1.call-update) | async-done | bytes 786448 | tf_op jit(solution)/shard_map/reduce_scatter | solution.py:144
  558.9 1.2 convert.10
  (55 shorter events, 9.1 us)
Async XLA Ops:
  7.2 11.0 %copy-start.12 = (bf16[1,128,768]{2,1,0:T(8,128)(2,1)S(1)}, bf16[1,128,768]{2,1,0:T(8,128)(2,1)}, u32[]{:S(2)}) copy-start(bf16[1,128,768]{2,1,0:T(8,128)(2,1)} %param.5) | copy-start | bytes 589828
  7.2 11.1 %copy-start.13 = (bf16[1,128,768]{2,1,0:T(8,128)(2,1)S(1)}, bf16[1,128,768]{2,1,0:T(8,128)(2,1)}, u32[]{:S(2)}) copy-start(bf16[1,128,768]{2,1,0:T(8,128)(2,1)} %param.6) | copy-start | bytes 589828
  7.2 509.0 %reduce-scatter.8.cloned.1.call-start = ((), (), s32[]{:S(2)}) async-start(), calls=%async_computation.3 | async-start | bytes 245760
  18.1 26.7 %copy-start.9 = (bf16[1,512,768]{1,2,0:T(8,128)(2,1)}, bf16[1,512,768]{1,2,0:T(8,128)(2,1)S(1)}, u32[]{:S(2)}) copy-start(bf16[1,512,768]{1,2,0:T(8,128)(2,1)S(1)} %copy.32) | copy-start | bytes 2359300
  18.3 11.6 %copy-start.11 = (bf16[1,128,768]{1,2,0:T(8,128)(2,1)}, bf16[1,128,768]{1,2,0:T(8,128)(2,1)S(1)}, u32[]{:S(2)}) copy-start(bf16[1,128,768]{1,2,0:T(8,128)(2,1)S(1)} %copy.30) | copy-start | bytes 589828
  27.6 2.3 copy-start.6
  29.1 7.4 %copy-start.3 = (bf16[1,128,768]{2,1,0:T(8,128)(2,1)S(1)}, bf16[1,128,768]{2,1,0:T(8,128)(2,1)}, u32[]{:S(2)}) copy-start(bf16[1,128,768]{2,1,0:T(8,128)(2,1)} %param.9) | copy-start | bytes 589828
  30.0 15.3 %copy-start.4 = (f32[4,128,192]{1,2,0:T(8,128)}, f32[4,128,192]{1,2,0:T(8,128)S(1)}, u32[]{:S(2)}) copy-start(f32[4,128,192]{1,2,0:T(8,128)S(1)} %get-tuple-element.29) | copy-start | bytes 1179652
  30.9 34.9 %collective-permute-start.1 = (bf16[1,32,768]{1,2,0:T(8,128)(2,1)}, bf16[1,32,768]{1,2,0:T(8,128)(2,1)}, u32[]{:S(2)}, u32[]{:S(2)}) collective-permute-start(bf16[1,32,768]{1,2,0:T(8,128)(2,1)} %get-tuple-element.25), channel_id=1, source_target_pairs={{1,0},{2,1},{3,2},{5,4},{6,5},{7,6},{9,8},{10,9},{11,10},{13,12},{... | collective-permute-start | bytes 147464 | tf_op jit(solution)/shard_map/ppermute | solution.py:26
  33.0 41.8 %collective-permute-start = (bf16[1,32,768]{1,2,0:T(8,128)(2,1)}, bf16[1,32,768]{1,2,0:T(8,128)(2,1)}, u32[]{:S(2)}, u32[]{:S(2)}) collective-permute-start(bf16[1,32,768]{1,2,0:T(8,128)(2,1)} %get-tuple-element.24), channel_id=1, source_target_pairs={{0,1},{1,2},{2,3},{4,5},{5,6},{6,7},{8,9},{9,10},{10,11},{12,13},{... | collective-permute-start | bytes 147464 | tf_op jit(solution)/shard_map/ppermute | solution.py:23
  37.2 9.6 %collective-permute-start.3 = (bf16[1,32,768]{2,1,0:T(8,128)(2,1)}, bf16[1,32,768]{2,1,0:T(8,128)(2,1)}, u32[]{:S(2)}, u32[]{:S(2)}) collective-permute-start(bf16[1,32,768]{2,1,0:T(8,128)(2,1)} %get-tuple-element.23), channel_id=1, source_target_pairs={{0,1},{1,2},{2,3},{4,5},{5,6},{6,7},{8,9},{9,10},{10,11},{12,13},{... | collective-permute-start | bytes 147464 | tf_op jit(solution)/shard_map/ppermute | solution.py:23
  39.8 5.6 copy-start.14
  39.9 8.8 %collective-permute-start.2 = (bf16[1,32,768]{2,1,0:T(8,128)(2,1)}, bf16[1,32,768]{2,1,0:T(8,128)(2,1)}, u32[]{:S(2)}, u32[]{:S(2)}) collective-permute-start(bf16[1,32,768]{2,1,0:T(8,128)(2,1)} %get-tuple-element.22), channel_id=1, source_target_pairs={{1,0},{2,1},{3,2},{5,4},{6,5},{7,6},{9,8},{10,9},{11,10},{13,12},{... | collective-permute-start | bytes 147464 | tf_op jit(solution)/shard_map/ppermute | solution.py:26
  45.5 3.2 copy-start.10
  50.7 6.2 %copy-start.7 = (bf16[1,512,768]{1,2,0:T(8,128)(2,1)S(1)}, bf16[1,512,768]{1,2,0:T(8,128)(2,1)}, u32[]{:S(2)}) copy-start(bf16[1,512,768]{1,2,0:T(8,128)(2,1)} %copy-done.6) | copy-start | bytes 2359300
  74.8 1.8 copy-start
  79.7 377.9 %copy-start.2 = (f32[512,768]{1,0:T(8,128)S(1)}, f32[512,768]{1,0:T(8,128)}, u32[]{:S(2)}) copy-start(f32[512,768]{1,0:T(8,128)} %copy.35) | copy-start | bytes 4718596
  452.9 4.8 copy-start.1
  457.4 101.5 %reduce-scatter.6.cloned.1.call-start = ((), (), s32[]{:S(2)}) async-start(), calls=%async_computation.2 | async-start | bytes 3932160 | tf_op jit(solution)/shard_map/reduce_scatter | solution.py:144
  459.8 1.0 copy-start.5
  459.8 2.7 copy-start.8
Sparse Core Ops, SparseCore 0:
  457.5 58.6 reduce-scatter.7
  518.8 40.1 reduce-scatter.5
where the time goes:
time: 569 us; the launch traced here: 568 us
  blocking collectives  393 us (69%)
  waiting for transfers between devices  84.9 us (15%)
  matrix products  35.9 us (6%)
  local copies, waits for them, and re-layouts  19.8 us (3%)
  between operations  15 us (3%)
  starting transfers between devices  10.9 us (2%)
  other arithmetic  8.49 us (1%)
    unnamed x1, blocking collectives  373 us
    unnamed x3, waiting for transfers between devices  43.9 us
    reduce_scatter x1, waiting for transfers between devices, body(): lax.psum_scatter(key_side(grad_scores, soft_rounded, queries[0], grad_att...  41 us
  transfers between devices with their start and end apart: 6, of which 2 were waited for; matrix products, arithmetic and copies ran while one was open for 8% of the time, Pallas kernels for 0%

commit v1 on v0

v1 whole, which is shorter than its diff:
```python
import math

import jax
import jax.numpy as jnp
from jax import lax
from jax.experimental import pallas as pl
from jax.experimental.pallas import tpu as pltpu
from jax.sharding import Mesh, PartitionSpec as P

HEADS = 4
HEAD_DIM = 192
TAPS = 3
STEP = 32
ROWS = 128
SPLITS = {64: (4, 2, 8), 4: (1, 2, 2)}

tanh_scale = 0.7978845608028654
cubic_term = 0.044715
norm_epsilon = 1e-06

F32 = jnp.float32
BF16 = jnp.bfloat16
WINDOW = (0, 128, 384, 512)
FIRST = (0, 64, 0, 64)
NT = (((1,), (1,)), ((), ()))
TN = (((0,), (0,)), ((), ()))


def dot(a, b, dims=(((1,), (0,)), ((), ()))):
    return lax.dot_general(a, b, dims, preferred_element_type=F32)


def masked_window(value, head):
    lane = lax.broadcasted_iota(jnp.int32, value.shape, 1)
    first = FIRST[head]
    keep = (lane >= first) & (lane < first + HEAD_DIM)
    return jnp.where(keep, value, jnp.zeros_like(value))


def window(ref, head):
    return ref[:, WINDOW[head] : WINDOW[head] + 256]


def place(parts):
    a, b, c, d = parts
    return jnp.concatenate(
        [
            a[:, :128],
            a[:, 128:] + b[:, :128],
            b[:, 128:],
            c[:, :128],
            c[:, 128:] + d[:, :128],
            d[:, 128:],
        ],
        axis=1,
    )


def gelu_value(value):
    inner = tanh_scale * (value + cubic_term * value * value * value)
    return 0.5 * value * (1.0 + jnp.tanh(inner))


def gelu_slope(value):
    square = value * value
    tangent = jnp.tanh(tanh_scale * (value + cubic_term * square * value))
    return 0.5 * (1.0 + tangent) + 0.5 * value * (1.0 - tangent * tangent) * tanh_scale * (
        1.0 + 3.0 * cubic_term * square
    )


def block_start(me, relative):
    return pl.multiple_of(jnp.bitwise_xor(me, relative) * ROWS, ROWS)


def forward_kernel(ids, *refs):
    q, k, v = refs[0:4], refs[4:8], refs[8:12]
    soft_ref, attended_ref, acted_ref = refs[12:15]
    q_all, km, vm, s_ref, p_ref, o_ref = refs[15:]
    me = ids[0]
    inverse = 1.0 / math.sqrt(HEAD_DIM)
    for r in range(4):
        at = slice(r * ROWS, (r + 1) * ROWS)
        q_all[at, :] = q[r][...]
        for h in range(HEADS):
            km[h, at, :] = masked_window(window(k[r], h), h)
            vm[h, at, :] = masked_window(window(v[r], h), h)
    for h in range(HEADS):
        s_ref[...] = dot(window(q_all, h), km[h], NT)
        for c in range(8):
            at = slice(c * 64, (c + 1) * 64)
            s = s_ref[at, :] * inverse
            e = jnp.exp(s - jnp.max(s, axis=1, keepdims=True))
            p = e / jnp.sum(e, axis=1, keepdims=True)
            soft_ref[h, at, :] = p
            p_ref[at, :] = p.astype(BF16)
        o_ref[h] = dot(p_ref[...], vm[h])
    acted_ref[0:STEP, :] = jnp.zeros((STEP, 768), BF16)
    acted_ref[STEP + 512 :, :] = jnp.zeros((STEP, 768), BF16)
    for r in range(4):
        at = slice(r * ROWS, (r + 1) * ROWS)
        attended = place([o_ref[h, at, :] for h in range(HEADS)]).astype(BF16)
        attended_ref[at, :] = attended
        full = attended.astype(F32)
        factor = lax.rsqrt(jnp.mean(full * full, axis=1, keepdims=True) + norm_epsilon)
        start = pl.multiple_of(block_start(me, r) + STEP, STEP)
        acted_ref[pl.ds(start, ROWS), :] = gelu_value(full * factor).astype(BF16)


def weight_kernel(ids, acted_ref, g0, g1, g2, g3, *refs):
    outs, (slab, shifted, total) = refs[:-3], refs[-3:]
    me, mx = ids[0], ids[1]
    parts = len(outs)
    slab[0:STEP, :] = jnp.zeros((STEP, HEAD_DIM), BF16)
    slab[STEP + 512 :, :] = jnp.zeros((STEP, HEAD_DIM), BF16)
    for r, g in enumerate((g0, g1, g2, g3)):
        mine = g[:, 0:192].astype(F32)
        for s in range(1, 4):
            mine = jnp.where(me == s, g[:, 192 * s : 192 * s + 192].astype(F32), mine)
        start = pl.multiple_of(block_start(me, r) + STEP, STEP)
        slab[pl.ds(start, ROWS), :] = mine.astype(BF16)
    for t in range(TAPS):
        first = (2 - t) * STEP
        shifted[:, 192 * t : 192 * t + 192] = slab[first : first + 512, :]
    result = dot(acted_ref[STEP : STEP + 512, :], shifted[...], TN)
    rows = 768 // parts
    half = rows // 2
    for j in range(parts):
        total[j] = result[j * rows : (j + 1) * rows]
    for n, out in enumerate(outs):
        piece = total[lax.rem(mx + n, parts)]
        out[...] = jnp.concatenate([piece[:half], piece[half:]], axis=1).astype(BF16)


def backward_kernel(ids, *refs):
    q, k, v, g = refs[0:4], refs[4:8], refs[8:12], refs[12:16]
    soft_ref, attended_ref, acted_ref, w_ref = refs[16:20]
    conv_ref, dq_ref, dk_ref, dv_ref = refs[20:24]
    km, vm, qm, g_pad, ga_ref, do_ref, dp_ref, ds_ref = refs[24:]
    me = ids[0]
    inverse = 1.0 / math.sqrt(HEAD_DIM)
    own = pl.multiple_of(me * ROWS, ROWS)
    conv = jnp.zeros((ROWS, 768), F32)
    for t in range(TAPS):
        rows = acted_ref[pl.ds(pl.multiple_of(own + t * STEP, STEP), ROWS), :]
        conv = conv + dot(rows, w_ref[t])
    conv_ref[...] = conv.astype(BF16)
    g_pad[0:STEP, :] = jnp.zeros((STEP, 768), BF16)
    g_pad[STEP + 512 :, :] = jnp.zeros((STEP, 768), BF16)
    for r in range(4):
        at = slice(r * ROWS, (r + 1) * ROWS)
        start = pl.multiple_of(block_start(me, r) + STEP, STEP)
        g_pad[pl.ds(start, ROWS), :] = g[r][...]
        for h in range(HEADS):
            km[h, at, :] = masked_window(window(k[r], h), h)
            vm[h, at, :] = masked_window(window(v[r], h), h)
            qm[h, at, :] = masked_window(window(q[r], h), h)
    ga_ref[...] = dot(g_pad[2 * STEP : 2 * STEP + 512, :], w_ref[0], NT)
    ga_ref[...] += dot(g_pad[STEP : STEP + 512, :], w_ref[1], NT)
    ga_ref[...] += dot(g_pad[0:512, :], w_ref[2], NT)
    for r in range(4):
        at = slice(r * ROWS, (r + 1) * ROWS)
        full = attended_ref[at, :].astype(F32)
        factor = lax.rsqrt(jnp.mean(full * full, axis=1, keepdims=True) + norm_epsilon)
        normed = full * factor
        grad = ga_ref[pl.ds(block_start(me, r), ROWS), :] * gelu_slope(normed)
        inner = jnp.mean(grad * normed, axis=1, keepdims=True)
        do_ref[at, :] = (factor * (grad - normed * inner)).astype(BF16)
    dq, dk, dv = [], [], []
    for h in range(HEADS):
        grad_out = window(do_ref, h)
        dp_ref[...] = dot(grad_out, vm[h], NT)
        for c in range(8):
            at = slice(c * 64, (c + 1) * 64)
            p = soft_ref[h, at, :]
            dp = dp_ref[at, :]
            inner = jnp.sum(dp * p, axis=1, keepdims=True)
            wide = 512 if c < 2 else ROWS
            ds_ref[at, 0:wide] = (p[:, :wide] * (dp[:, :wide] - inner) * inverse).astype(BF16)
        dq.append(dot(ds_ref[0:ROWS, :], km[h]))
        dk.append(dot(ds_ref[:, 0:ROWS], qm[h], TN))
        dv.append(dot(soft_ref[h, :, 0:ROWS].astype(BF16), masked_window(grad_out, h), TN))
    dq_ref[...] = place(dq).astype(BF16)
    dk_ref[...] = place(dk).astype(BF16)
    dv_ref[...] = place(dv).astype(BF16)


def sum_kernel(ids, *refs):
    parts, outs, total = refs[: ids_parts(refs)], refs[ids_parts(refs) : -1], refs[-1]
    mz = ids[2]
    value = parts[0][...].astype(F32)
    for part in parts[1:]:
        value = value + part[...].astype(F32)
    count = len(outs)
    rows = value.shape[0] // count
    for j in range(count):
        total[j, 0:rows, :] = value[j * rows : (j + 1) * rows]
    for n, out in enumerate(outs):
        out[...] = total[lax.rem(mz + n, count), 0:rows, :].astype(BF16)


def ids_parts(refs):
    shape = refs[0].shape
    count = 0
    while refs[count].shape == shape and count < len(refs) - 1:
        count += 1
    return count


def half_kernel(ids, *refs):
    parts, (keep_ref, send_ref) = refs[:-2], refs[-2:]
    my = ids[3]
    value = parts[0][...].astype(F32)
    for part in parts[1:]:
        value = value + part[...].astype(F32)
    low, high = value[:, :576], value[:, 576:]
    keep_ref[...] = jnp.where(my == 0, low, high)
    send_ref[...] = jnp.where(my == 0, high, low).astype(BF16)


def last_kernel(scale, keep_ref, got_ref, out_ref):
    value = (keep_ref[...] + got_ref[...].astype(F32)) * scale
    for t in range(TAPS):
        out_ref[:, t, :] = value[:, 192 * t : 192 * t + 192]


def call(kernel, outs, scratch, args, flops, limit=24):
    size = sum(math.prod(a.shape) * a.dtype.itemsize for a in (*args, *outs))
    return pl.pallas_call(
        kernel,
        out_shape=outs,
        in_specs=[
            pl.BlockSpec(memory_space=pltpu.SMEM if a.dtype == jnp.int32 else pltpu.VMEM)
            for a in args
        ],
        out_specs=[pl.BlockSpec(memory_space=pltpu.VMEM) for _ in outs],
        scratch_shapes=scratch,
        compiler_params=pltpu.CompilerParams(vmem_limit_bytes=limit << 20),
        cost_estimate=pl.CostEstimate(
            flops=flops, bytes_accessed=size, transcendentals=0
        ),
    )(*args)


def shaped(shape, dtype=BF16):
    return jax.ShapeDtypeStruct(shape, dtype)


def shift(value, axis, by):
    count = lax.axis_size(axis)
    return lax.ppermute(value, axis, [(i, (i + by) % count) for i in range(count)])


def blocks(value):
    across = shift(value, "yl", 1)
    return value, shift(value, "core", 1), across, shift(across, "core", 1)


def body(queries, key_rows, value_rows, conv_weight, output_gradient):
    x_size, z_size = lax.axis_size("x"), lax.axis_size("z")
    sizes = [lax.axis_size(a) for a in ("x", "yh", "z", "yl", "core")]
    grad_scale = 1.0 / math.sqrt(math.prod(sizes) * ROWS)
    me = lax.axis_index("yl") * 2 + lax.axis_index("core")
    ids = jnp.stack(
        [me, lax.axis_index("x"), lax.axis_index("z"), lax.axis_index("yh")]
    ).astype(jnp.int32)
    weight = jnp.transpose(conv_weight, (1, 0, 2))
    k = blocks(key_rows[0])
    q = blocks(queries[0])
    v = blocks(value_rows[0])
    g = blocks(output_gradient[0])
    soft, attended, acted = call(
        forward_kernel,
        [shaped((HEADS, 512, 512), F32), shaped((512, 768)), shaped((576, 768))],
        [
            pltpu.VMEM((512, 768), BF16),
            pltpu.VMEM((HEADS, 512, 256), BF16),
            pltpu.VMEM((HEADS, 512, 256), BF16),
            pltpu.VMEM((512, 512), F32),
            pltpu.VMEM((512, 512), BF16),
            pltpu.VMEM((HEADS, 512, 256), F32),
        ],
        [ids, *q, *k, *v],
        2_000_000_000,
    )
    rows = 768 // x_size
    pieces = call(
        weight_kernel,
        [shaped((rows // 2, 1152)) for _ in range(x_size)],
        [
            pltpu.VMEM((576, HEAD_DIM), BF16),
            pltpu.VMEM((512, 576), BF16),
            pltpu.VMEM((x_size, rows, 576), F32),
        ],
        [ids, acted, *g],
        500_000_000,
    )
    got = [pieces[0]] + [shift(pieces[n], "x", n) for n in range(1, x_size)]
    conv_out, grad_queries, grad_keys, grad_values = call(
        backward_kernel,
        [shaped((ROWS, 768)) for _ in range(4)],
        [
            pltpu.VMEM((HEADS, 512, 256), BF16),
            pltpu.VMEM((HEADS, 512, 256), BF16),
            pltpu.VMEM((HEADS, 512, 256), BF16),
            pltpu.VMEM((576, 768), BF16),
            pltpu.VMEM((512, 768), F32),
            pltpu.VMEM((512, 768), BF16),
            pltpu.VMEM((512, 512), F32),
            pltpu.VMEM((512, 512), BF16),
        ],
        [ids, *q, *k, *v, *g, soft, attended, acted, weight],
        4_000_000_000,
        36,
    )
    few = rows // 2 // z_size
    pieces = call(
        sum_kernel,
        [shaped((few, 1152)) for _ in range(z_size)],
        [pltpu.VMEM((z_size, -(-few // 8) * 8, 1152), F32)],
        [ids, *got],
        1_000_000,
    )
    got = [pieces[0]] + [shift(pieces[n], "z", n) for n in range(1, z_size)]
    keep, send = call(
        half_kernel, [shaped((few, 576), F32), shaped((few, 576))], [], [ids, *got], 1_000_000
    )
    other = shift(send, "yh", 1)
    (grad_weight,) = call(
        lambda *refs: last_kernel(grad_scale, *refs),
        [shaped((few, TAPS, HEAD_DIM), F32)],
        [],
        [keep, other],
        1_000_000,
    )
    return conv_out[None], grad_queries[None], grad_keys[None], grad_values[None], grad_weight


def solution(mesh):
    x, yh, z = SPLITS[mesh.shape["dp"]]
    fine = Mesh(mesh.devices.reshape(x, yh, z, 2, 2), ("x", "yh", "z", "yl", "core"))
    dp, seq = ("x", "yh", "z"), ("yl", "core")
    return jax.shard_map(
        body,
        mesh=fine,
        in_specs=(P(dp, seq, None), P(dp, seq, None), P(dp, seq, None), P(), P(dp, seq, None)),
        out_specs=(
            P(dp, seq, None),
            P(dp, seq, None),
            P(dp, seq, None),
            P(dp, seq, None),
            P(dp, None, seq),
        ),
        check_vma=False,
    )
```

time: 569 us -> 78.9 us (0.14)
  blocking collectives: 393 us -> 0 us
  waiting for transfers between devices: 84.9 us -> 13.3 us
  matrix products: 35.9 us -> 0 us
  starting transfers between devices: 10.9 us -> 44.8 us
  local copies, waits for them, and re-layouts: 19.8 us -> 3 us
  Pallas kernels: 0 us -> 15.9 us
  between operations: 15 us -> 0.74 us
  other arithmetic: 8.49 us -> 0.08 us
    unnamed x1 -> x0, blocking collectives: 373 us -> none
    unnamed x3 -> x0, waiting for transfers between devices: 43.9 us -> none
    reduce_scatter x1 -> x0, waiting for transfers between devices: 41 us -> none  [body(): lax.psum_scatter(key_side(grad_scores, soft_rounded, queries[0], grad_att...]
    dot_general x14 -> x0, matrix products: 34.4 us -> none  [the longest x3 6.48 us: body(): jnp.einsum('pc,dc->pd', reverse_rows, conv_weight[:, kernel_tap_index, :]...]
    ppermute x4 -> x23, starting transfers between devices: 10.6 us -> 44.8 us  [shift(): lax.ppermute(value, axis, [(i, (i + by) % count) for i in range(count)])]
    all_gather x2 -> x0, blocking collectives: 19.6 us -> none  [the longest x1 10.6 us: body(): lax.all_gather(value_rows, 'seq', axis=1, tiled=True)]
    pallas_call x0 -> x6, Pallas kernels: none -> 15.9 us  [call(): pl.pallas_call(kernel, out_shape=outs, in_specs=[pl.BlockSpec(memory_spac...]
    ppermute x4 -> x23, waiting for transfers between devices: 0.01 us -> 13.3 us  [shift(): lax.ppermute(value, axis, [(i, (i + by) % count) for i in range(count)])]
  transfers between devices with their start and end apart: 6 -> 23, of which waited for: 2 -> 5; matrix products, arithmetic and copies ran while one was open for 8% -> 0% of each run, Pallas kernels for 0% -> 15%
where the time goes in v1:
time: 78.9 us; the launch traced here: 77.8 us
  starting transfers between devices  44.8 us (57%)
  Pallas kernels  15.9 us (20%)
  waiting for transfers between devices  13.3 us (17%)
  local copies, waits for them, and re-layouts  3 us (4%)
    ppermute x23, starting transfers between devices, shift(): lax.ppermute(value, axis, [(i, (i + by) % count) for i in range(count)])  44.8 us
    pallas_call x6, Pallas kernels, call(): pl.pallas_call(kernel, out_shape=outs, in_specs=[pl.BlockSpec(memory_spac...  15.9 us
    ppermute x23, waiting for transfers between devices, shift(): lax.ppermute(value, axis, [(i, (i + by) % count) for i in range(count)])  13.3 us
    unnamed x16, local copies, waits for them, and re-layouts  3 us
  transfers between devices with their start and end apart: 23, of which 5 were waited for; matrix products, arithmetic and copies ran while one was open for 0% of the time, Pallas kernels for 15%

profile of v1, /device:TPU:1, one launch (start us, length us, event | category | flops | bytes accessed | tf_op | source)
XLA Modules:
  0.0 77.8 jit_solution(12682472312677854504)
XLA Ops:
  0.6 2.2 %collective-permute-start.1 = (bf16[128,768]{1,0:T(8,128)(2,1)}, bf16[128,768]{1,0:T(8,128)(2,1)S(1)}, u32[]{:S(2)}, u32[]{:S(2)}) collective-permute-start(bf16[128,768]{1,0:T(8,128)(2,1)} %bitcast.14), channel_id=1, source_target_pairs={{0,2},{2,0},{1,3},{3,1},{4,6},{6,4},{5,7},{7,5},{8,10},{10,8},{9,1... | collective-permute-start | bytes 589832 | tf_op jit(solution)/shard_map/ppermute | solution.py:251
  2.8 1.2 %collective-permute-start = (bf16[128,768]{1,0:T(8,128)(2,1)}, bf16[128,768]{1,0:T(8,128)(2,1)S(1)}, u32[]{:S(2)}, u32[]{:S(2)}) collective-permute-start(bf16[128,768]{1,0:T(8,128)(2,1)} %bitcast.15), channel_id=1, source_target_pairs={{0,1},{1,0},{2,3},{3,2},{4,5},{5,4},{6,7},{7,6},{8,9},{9,8},{10,11... | collective-permute-start | bytes 589832 | tf_op jit(solution)/shard_map/ppermute | solution.py:251
  4.0 1.6 %collective-permute-start.4 = (bf16[128,768]{1,0:T(8,128)(2,1)}, bf16[128,768]{1,0:T(8,128)(2,1)S(1)}, u32[]{:S(2)}, u32[]{:S(2)}) collective-permute-start(bf16[128,768]{1,0:T(8,128)(2,1)} %bitcast.18), channel_id=1, source_target_pairs={{0,2},{2,0},{1,3},{3,1},{4,6},{6,4},{5,7},{7,5},{8,10},{10,8},{9,1... | collective-permute-start | bytes 589832 | tf_op jit(solution)/shard_map/ppermute | solution.py:251
  6.0 0.6 collective-permute-done.1.refs_2_
  6.6 5.3 %collective-permute-start.6 = (bf16[128,768]{1,0:T(8,128)(2,1)}, bf16[128,768]{1,0:T(8,128)(2,1)S(1)}, u32[]{:S(2)}, u32[]{:S(2)}) collective-permute-start(bf16[128,768]{1,0:T(8,128)(2,1)} %bitcast.23), channel_id=1, source_target_pairs={{0,1},{1,0},{2,3},{3,2},{4,5},{5,4},{6,7},{7,6},{8,9},{9,8},{10,11... | collective-permute-start | bytes 589832 | tf_op jit(solution)/shard_map/ppermute | solution.py:251
  11.9 4.2 %collective-permute-start.2 = (bf16[128,768]{1,0:T(8,128)(2,1)S(1)}, bf16[128,768]{1,0:T(8,128)(2,1)S(1)}, u32[]{:S(2)}, u32[]{:S(2)}) collective-permute-start(bf16[128,768]{1,0:T(8,128)(2,1)S(1)} %collective-permute-done.1.refs_2_), channel_id=1, source_target_pairs={{0,1},{1,0},{2,3},{3,2},{4,5},{5,4},{6,7},{7,6},{8,9},{9,8},{10,11... | collective-permute-start | bytes 589832 | tf_op jit(solution)/shard_map/ppermute | solution.py:251
  16.1 4.0 %collective-permute-start.8 = (bf16[128,768]{1,0:T(8,128)(2,1)S(1)}, bf16[128,768]{1,0:T(8,128)(2,1)S(1)}, u32[]{:S(2)}, u32[]{:S(2)}) collective-permute-start(bf16[128,768]{1,0:T(8,128)(2,1)S(1)} %collective-permute-done.7.refs_10_), channel_id=1, source_target_pairs={{0,1},{1,0},{2,3},{3,2},{4,5},{5,4},{6,7},{7,6},{8,9},{9,8},{10,11... | collective-permute-start | bytes 589832 | tf_op jit(solution)/shard_map/ppermute | solution.py:251
  20.2 2.1 %collective-permute-start.11 = (bf16[128,768]{1,0:T(8,128)(2,1)S(1)}, bf16[128,768]{1,0:T(8,128)(2,1)S(1)}, u32[]{:S(2)}, u32[]{:S(2)}) collective-permute-start(bf16[128,768]{1,0:T(8,128)(2,1)S(1)} %collective-permute-done.10.refs_14_.g2), channel_id=1, source_target_pairs={{0,1},{1,0},{2,3},{3,2},{4,5},{5,4},{6,7},{7,6},{8,9},{9,8},{10,11... | collective-permute-start | bytes 589832 | tf_op jit(solution)/shard_map/ppermute | solution.py:251
  22.4 1.1 %copy-done.1 = bf16[1,128,768]{2,1,0:T(8,128)(2,1)S(1)} copy-done((bf16[1,128,768]{2,1,0:T(8,128)(2,1)S(1)}, bf16[1,128,768]{2,1,0:T(8,128)(2,1)}, u32[]{:S(2)}) %copy-start.1) | copy-done | bytes 196632
  23.4 1.0 %copy-done.3 = bf16[1,128,768]{2,1,0:T(8,128)(2,1)S(1)} copy-done((bf16[1,128,768]{2,1,0:T(8,128)(2,1)S(1)}, bf16[1,128,768]{2,1,0:T(8,128)(2,1)}, u32[]{:S(2)}) %copy-start.3) | copy-done | bytes 196632
  24.4 0.9 %copy-done.5 = bf16[1,128,768]{2,1,0:T(8,128)(2,1)S(1)} copy-done((bf16[1,128,768]{2,1,0:T(8,128)(2,1)S(1)}, bf16[1,128,768]{2,1,0:T(8,128)(2,1)}, u32[]{:S(2)}) %copy-start.5) | copy-done | bytes 196632
  25.4 3.5 %shard_map.92 = (f32[4,512,512]{2,1,0:T(8,128)S(1)}, bf16[512,768]{1,0:T(8,128)(2,1)S(1)}, bf16[576,768]{1,0:T(8,128)(2,1)S(1)}) custom-call(s32[4]{0:T(128)S(1)} %pad_add_fusion.ids, bf16[128,768]{1,0:T(8,128)(2,1)S(1)} %bitcast.16, bf16[128,768]{1,0:T(8,128)(2,1)S(1)} %collective-permute-done.refs_1_, bf16[128,768]{1,0:T(8,128)(2,1)S(1)} %collective-permute-done.1.refs_2_, ...), custom_call_target="tpu_custom_call" | custom-call | flops 2000000000 | bytes 8224784 | tf_op jit(solution)/shard_map/pallas_call | solution.py:229
  28.9 2.1 %shard_map.94 = (bf16[96,1152]{1,0:T(8,128)(2,1)S(1)}, bf16[96,1152]{1,0:T(8,128)(2,1)S(1)}, bf16[96,1152]{1,0:T(8,128)(2,1)S(1)}, bf16[96,1152]{1,0:T(8,128)(2,1)S(1)}) custom-call(s32[4]{0:T(128)S(1)} %pad_add_fusion.ids, bf16[576,768]{1,0:T(8,128)(2,1)S(1)} %get-tuple-element.28.refs_18_.acted_ref, bf16[128,768]{1,0:T(8,128)(2,1)S(1)} %bitcast.28, ...), custom_call_target="tpu_custom_call" | custom-call | flops 500000000 | bytes 2555920 | tf_op jit(solution)/shard_map/pallas_call | solution.py:229
  31.0 0.7 collective-permute-start.12
  31.8 2.4 %collective-permute-start.13 = (bf16[96,1152]{1,0:T(8,128)(2,1)S(1)}, bf16[96,1152]{1,0:T(8,128)(2,1)S(1)}, u32[]{:S(2)}, u32[]{:S(2)}) collective-permute-start(bf16[96,1152]{1,0:T(8,128)(2,1)S(1)} %get-tuple-element.35), channel_id=1, source_target_pairs={{0,128},{64,192},{128,0},{192,64},{1,129},{65,193},{129,1},{193,65... | collective-permute-start | bytes 663560 | tf_op jit(solution)/shard_map/ppermute | solution.py:251
  34.2 1.2 %collective-permute-start.14 = (bf16[96,1152]{1,0:T(8,128)(2,1)S(1)}, bf16[96,1152]{1,0:T(8,128)(2,1)S(1)}, u32[]{:S(2)}, u32[]{:S(2)}) collective-permute-start(bf16[96,1152]{1,0:T(8,128)(2,1)S(1)} %get-tuple-element.36), channel_id=1, source_target_pairs={{0,192},{64,0},{128,64},{192,128},{1,193},{65,1},{129,65},{193,129... | collective-permute-start | bytes 663560 | tf_op jit(solution)/shard_map/ppermute | solution.py:251
  35.4 3.9 %collective-permute-done.12.refs_1_ = bf16[96,1152]{1,0:T(8,128)(2,1)S(1)} collective-permute-done((bf16[96,1152]{1,0:T(8,128)(2,1)S(1)}, bf16[96,1152]{1,0:T(8,128)(2,1)S(1)}, u32[]{:S(2)}, u32[]{:S(2)}) %collective-permute-start.12) | collective-permute-done | bytes 221216 | tf_op jit(solution)/shard_map/ppermute | solution.py:251
  39.3 5.2 %collective-permute-done.13.refs_2_ = bf16[96,1152]{1,0:T(8,128)(2,1)S(1)} collective-permute-done((bf16[96,1152]{1,0:T(8,128)(2,1)S(1)}, bf16[96,1152]{1,0:T(8,128)(2,1)S(1)}, u32[]{:S(2)}, u32[]{:S(2)}) %collective-permute-start.13) | collective-permute-done | bytes 221216 | tf_op jit(solution)/shard_map/ppermute | solution.py:251
  44.5 0.8 shard_map.95
  45.2 1.7 %collective-permute-start.15 = (bf16[12,1152]{1,0:T(8,128)(2,1)S(1)}, bf16[12,1152]{1,0:T(8,128)(2,1)S(1)}, u32[]{:S(2)}, u32[]{:S(2)}) collective-permute-start(bf16[12,1152]{1,0:T(8,128)(2,1)S(1)} %get-tuple-element.38), channel_id=1, source_target_pairs={{0,4},{4,8},{8,12},{12,16},{16,20},{20,24},{24,28},{28,0},{1,5},{5... | collective-permute-start | bytes 82952 | tf_op jit(solution)/shard_map/ppermute | solution.py:251
  47.0 3.0 %collective-permute-start.16 = (bf16[12,1152]{1,0:T(8,128)(2,1)S(1)}, bf16[12,1152]{1,0:T(8,128)(2,1)S(1)}, u32[]{:S(2)}, u32[]{:S(2)}) collective-permute-start(bf16[12,1152]{1,0:T(8,128)(2,1)S(1)} %get-tuple-element.39), channel_id=1, source_target_pairs={{0,8},{4,12},{8,16},{12,20},{16,24},{20,28},{24,0},{28,4},{1,9},{5... | collective-permute-start | bytes 82952 | tf_op jit(solution)/shard_map/ppermute | solution.py:251
  49.9 3.8 %collective-permute-start.17 = (bf16[12,1152]{1,0:T(8,128)(2,1)S(1)}, bf16[12,1152]{1,0:T(8,128)(2,1)S(1)}, u32[]{:S(2)}, u32[]{:S(2)}) collective-permute-start(bf16[12,1152]{1,0:T(8,128)(2,1)S(1)} %get-tuple-element.40), channel_id=1, source_target_pairs={{0,12},{4,16},{8,20},{12,24},{16,28},{20,0},{24,4},{28,8},{1,13},{... | collective-permute-start | bytes 82952 | tf_op jit(solution)/shard_map/ppermute | solution.py:251
  53.7 0.5 collective-permute-start.18
  54.2 4.5 %collective-permute-start.19 = (bf16[12,1152]{1,0:T(8,128)(2,1)S(1)}, bf16[12,1152]{1,0:T(8,128)(2,1)S(1)}, u32[]{:S(2)}, u32[]{:S(2)}) collective-permute-start(bf16[12,1152]{1,0:T(8,128)(2,1)S(1)} %get-tuple-element.42), channel_id=1, source_target_pairs={{0,20},{4,24},{8,28},{12,0},{16,4},{20,8},{24,12},{28,16},{1,21},{... | collective-permute-start | bytes 82952 | tf_op jit(solution)/shard_map/ppermute | solution.py:251
  58.6 2.4 %collective-permute-start.20 = (bf16[12,1152]{1,0:T(8,128)(2,1)S(1)}, bf16[12,1152]{1,0:T(8,128)(2,1)S(1)}, u32[]{:S(2)}, u32[]{:S(2)}) collective-permute-start(bf16[12,1152]{1,0:T(8,128)(2,1)S(1)} %get-tuple-element.43), channel_id=1, source_target_pairs={{0,24},{4,28},{8,0},{12,4},{16,8},{20,12},{24,16},{28,20},{1,25},{... | collective-permute-start | bytes 82952 | tf_op jit(solution)/shard_map/ppermute | solution.py:251
  61.0 0.7 collective-permute-start.21
  61.8 2.7 %collective-permute-done.20.refs_6_ = bf16[12,1152]{1,0:T(8,128)(2,1)S(1)} collective-permute-done((bf16[12,1152]{1,0:T(8,128)(2,1)S(1)}, bf16[12,1152]{1,0:T(8,128)(2,1)S(1)}, u32[]{:S(2)}, u32[]{:S(2)}) %collective-permute-start.20) | collective-permute-done | bytes 27680 | tf_op jit(solution)/shard_map/ppermute | solution.py:251
  64.5 0.8 %collective-permute-done.21.refs_7_ = bf16[12,1152]{1,0:T(8,128)(2,1)S(1)} collective-permute-done((bf16[12,1152]{1,0:T(8,128)(2,1)S(1)}, bf16[12,1152]{1,0:T(8,128)(2,1)S(1)}, u32[]{:S(2)}, u32[]{:S(2)}) %collective-permute-start.21) | collective-permute-done | bytes 27680 | tf_op jit(solution)/shard_map/ppermute | solution.py:251
  65.3 0.7 shard_map.96
  66.0 3.0 %collective-permute-start.22 = (bf16[12,576]{1,0:T(8,128)(2,1)S(1)}, bf16[12,576]{1,0:T(8,128)(2,1)S(1)}, u32[]{:S(2)}, u32[]{:S(2)}) collective-permute-start(bf16[12,576]{1,0:T(8,128)(2,1)S(1)} %get-tuple-element.46), channel_id=1, source_target_pairs={{0,32},{32,0},{1,33},{33,1},{2,34},{34,2},{3,35},{35,3},{4,36},{36... | collective-permute-start | bytes 41480 | tf_op jit(solution)/shard_map/ppermute | solution.py:251
  69.0 8.1 %shard_map.93 = (bf16[128,768]{1,0:T(8,128)(2,1)}, bf16[128,768]{1,0:T(8,128)(2,1)}, bf16[128,768]{1,0:T(8,128)(2,1)}, bf16[128,768]{1,0:T(8,128)(2,1)}) custom-call(s32[4]{0:T(128)S(1)} %pad_add_fusion.ids, bf16[128,768]{1,0:T(8,128)(2,1)S(1)} %bitcast.17, bf16[128,768]{1,0:T(8,128)(2,1)S(1)} %collective-permute-done.refs_1_, ...), custom_call_target="tpu_custom_call" | custom-call | flops 4000000000 | bytes 13336592 | tf_op jit(solution)/shard_map/pallas_call | solution.py:229
  77.1 0.7 shard_map.97
  (37 shorter events, 0.4 us)
Async XLA Ops:
  0.6 6.0 %collective-permute-start.1 = (bf16[128,768]{1,0:T(8,128)(2,1)}, bf16[128,768]{1,0:T(8,128)(2,1)S(1)}, u32[]{:S(2)}, u32[]{:S(2)}) collective-permute-start(bf16[128,768]{1,0:T(8,128)(2,1)} %bitcast.14), channel_id=1, source_target_pairs={{0,2},{2,0},{1,3},{3,1},{4,6},{6,4},{5,7},{7,5},{8,10},{10,8},{9,1... | collective-permute-start | bytes 589832 | tf_op jit(solution)/shard_map/ppermute | solution.py:251
  2.8 9.1 %collective-permute-start = (bf16[128,768]{1,0:T(8,128)(2,1)}, bf16[128,768]{1,0:T(8,128)(2,1)S(1)}, u32[]{:S(2)}, u32[]{:S(2)}) collective-permute-start(bf16[128,768]{1,0:T(8,128)(2,1)} %bitcast.15), channel_id=1, source_target_pairs={{0,1},{1,0},{2,3},{3,2},{4,5},{5,4},{6,7},{7,6},{8,9},{9,8},{10,11... | collective-permute-start | bytes 589832 | tf_op jit(solution)/shard_map/ppermute | solution.py:251
  4.0 7.9 %collective-permute-start.4 = (bf16[128,768]{1,0:T(8,128)(2,1)}, bf16[128,768]{1,0:T(8,128)(2,1)S(1)}, u32[]{:S(2)}, u32[]{:S(2)}) collective-permute-start(bf16[128,768]{1,0:T(8,128)(2,1)} %bitcast.18), channel_id=1, source_target_pairs={{0,2},{2,0},{1,3},{3,1},{4,6},{6,4},{5,7},{7,5},{8,10},{10,8},{9,1... | collective-permute-start | bytes 589832 | tf_op jit(solution)/shard_map/ppermute | solution.py:251
  5.7 10.5 %collective-permute-start.3 = (bf16[128,768]{1,0:T(8,128)(2,1)}, bf16[128,768]{1,0:T(8,128)(2,1)S(1)}, u32[]{:S(2)}, u32[]{:S(2)}) collective-permute-start(bf16[128,768]{1,0:T(8,128)(2,1)} %bitcast.19), channel_id=1, source_target_pairs={{0,1},{1,0},{2,3},{3,2},{4,5},{5,4},{6,7},{7,6},{8,9},{9,8},{10,11... | collective-permute-start | bytes 589832 | tf_op jit(solution)/shard_map/ppermute | solution.py:251
  5.9 10.2 %collective-permute-start.7 = (bf16[128,768]{1,0:T(8,128)(2,1)}, bf16[128,768]{1,0:T(8,128)(2,1)S(1)}, u32[]{:S(2)}, u32[]{:S(2)}) collective-permute-start(bf16[128,768]{1,0:T(8,128)(2,1)} %bitcast.22), channel_id=1, source_target_pairs={{0,2},{2,0},{1,3},{3,1},{4,6},{6,4},{5,7},{7,5},{8,10},{10,8},{9,1... | collective-permute-start | bytes 589832 | tf_op jit(solution)/shard_map/ppermute | solution.py:251
  6.6 13.6 %collective-permute-start.6 = (bf16[128,768]{1,0:T(8,128)(2,1)}, bf16[128,768]{1,0:T(8,128)(2,1)S(1)}, u32[]{:S(2)}, u32[]{:S(2)}) collective-permute-start(bf16[128,768]{1,0:T(8,128)(2,1)} %bitcast.23), channel_id=1, source_target_pairs={{0,1},{1,0},{2,3},{3,2},{4,5},{5,4},{6,7},{7,6},{8,9},{9,8},{10,11... | collective-permute-start | bytes 589832 | tf_op jit(solution)/shard_map/ppermute | solution.py:251
  11.9 8.3 %collective-permute-start.10 = (bf16[128,768]{1,0:T(8,128)(2,1)}, bf16[128,768]{1,0:T(8,128)(2,1)S(1)}, u32[]{:S(2)}, u32[]{:S(2)}) collective-permute-start(bf16[128,768]{1,0:T(8,128)(2,1)} %bitcast.26), channel_id=1, source_target_pairs={{0,2},{2,0},{1,3},{3,1},{4,6},{6,4},{5,7},{7,5},{8,10},{10,8},{9,1... | collective-permute-start | bytes 589832 | tf_op jit(solution)/shard_map/ppermute | solution.py:251
  11.9 10.4 %collective-permute-start.2 = (bf16[128,768]{1,0:T(8,128)(2,1)S(1)}, bf16[128,768]{1,0:T(8,128)(2,1)S(1)}, u32[]{:S(2)}, u32[]{:S(2)}) collective-permute-start(bf16[128,768]{1,0:T(8,128)(2,1)S(1)} %collective-permute-done.1.refs_2_), channel_id=1, source_target_pairs={{0,1},{1,0},{2,3},{3,2},{4,5},{5,4},{6,7},{7,6},{8,9},{9,8},{10,11... | collective-permute-start | bytes 589832 | tf_op jit(solution)/shard_map/ppermute | solution.py:251
  16.1 6.2 %collective-permute-start.5 = (bf16[128,768]{1,0:T(8,128)(2,1)S(1)}, bf16[128,768]{1,0:T(8,128)(2,1)S(1)}, u32[]{:S(2)}, u32[]{:S(2)}) collective-permute-start(bf16[128,768]{1,0:T(8,128)(2,1)S(1)} %collective-permute-done.4.refs_6_), channel_id=1, source_target_pairs={{0,1},{1,0},{2,3},{3,2},{4,5},{5,4},{6,7},{7,6},{8,9},{9,8},{10,11... | collective-permute-start | bytes 589832 | tf_op jit(solution)/shard_map/ppermute | solution.py:251
  16.1 6.2 %collective-permute-start.8 = (bf16[128,768]{1,0:T(8,128)(2,1)S(1)}, bf16[128,768]{1,0:T(8,128)(2,1)S(1)}, u32[]{:S(2)}, u32[]{:S(2)}) collective-permute-start(bf16[128,768]{1,0:T(8,128)(2,1)S(1)} %collective-permute-done.7.refs_10_), channel_id=1, source_target_pairs={{0,1},{1,0},{2,3},{3,2},{4,5},{5,4},{6,7},{7,6},{8,9},{9,8},{10,11... | collective-permute-start | bytes 589832 | tf_op jit(solution)/shard_map/ppermute | solution.py:251
  20.2 8.7 %collective-permute-start.9 = (bf16[128,768]{1,0:T(8,128)(2,1)}, bf16[128,768]{1,0:T(8,128)(2,1)S(1)}, u32[]{:S(2)}, u32[]{:S(2)}) collective-permute-start(bf16[128,768]{1,0:T(8,128)(2,1)} %bitcast.27), channel_id=1, source_target_pairs={{0,1},{1,0},{2,3},{3,2},{4,5},{5,4},{6,7},{7,6},{8,9},{9,8},{10,11... | collective-permute-start | bytes 589832 | tf_op jit(solution)/shard_map/ppermute | solution.py:251
  20.2 8.7 %collective-permute-start.11 = (bf16[128,768]{1,0:T(8,128)(2,1)S(1)}, bf16[128,768]{1,0:T(8,128)(2,1)S(1)}, u32[]{:S(2)}, u32[]{:S(2)}) collective-permute-start(bf16[128,768]{1,0:T(8,128)(2,1)S(1)} %collective-permute-done.10.refs_14_.g2), channel_id=1, source_target_pairs={{0,1},{1,0},{2,3},{3,2},{4,5},{5,4},{6,7},{7,6},{8,9},{9,8},{10,11... | collective-permute-start | bytes 589832 | tf_op jit(solution)/shard_map/ppermute | solution.py:251
  22.3 46.6 %copy-start = (bf16[768,3,768]{2,0,1:T(8,128)(2,1)S(1)}, bf16[768,3,768]{2,0,1:T(8,128)(2,1)}, u32[]{:S(2)}) copy-start(bf16[768,3,768]{2,0,1:T(8,128)(2,1)} %param.8) | copy-start | bytes 10616836
  22.4 1.1 %copy-start.1 = (bf16[1,128,768]{2,1,0:T(8,128)(2,1)S(1)}, bf16[1,128,768]{2,1,0:T(8,128)(2,1)}, u32[]{:S(2)}) copy-start(bf16[1,128,768]{2,1,0:T(8,128)(2,1)} %param.5) | copy-start | bytes 589828
  23.4 1.0 %copy-start.3 = (bf16[1,128,768]{2,1,0:T(8,128)(2,1)S(1)}, bf16[1,128,768]{2,1,0:T(8,128)(2,1)}, u32[]{:S(2)}) copy-start(bf16[1,128,768]{2,1,0:T(8,128)(2,1)} %param.6) | copy-start | bytes 589828
  24.4 0.9 %copy-start.5 = (bf16[1,128,768]{2,1,0:T(8,128)(2,1)S(1)}, bf16[1,128,768]{2,1,0:T(8,128)(2,1)}, u32[]{:S(2)}) copy-start(bf16[1,128,768]{2,1,0:T(8,128)(2,1)} %param.7) | copy-start | bytes 589828
  25.4 3.6 %copy-start.7 = (bf16[1,128,768]{2,1,0:T(8,128)(2,1)S(1)}, bf16[1,128,768]{2,1,0:T(8,128)(2,1)}, u32[]{:S(2)}) copy-start(bf16[1,128,768]{2,1,0:T(8,128)(2,1)} %param.9) | copy-start | bytes 589828
  25.4 43.6 %copy-start.2 = (bf16[1,128,768]{2,1,0:T(8,128)(2,1)S(1)}, bf16[1,128,768]{2,1,0:T(8,128)(2,1)}, u32[]{:S(2)}) copy-start(bf16[1,128,768]{2,1,0:T(8,128)(2,1)} %param.5) | copy-start | bytes 589828
  25.4 43.6 %copy-start.4 = (bf16[1,128,768]{2,1,0:T(8,128)(2,1)S(1)}, bf16[1,128,768]{2,1,0:T(8,128)(2,1)}, u32[]{:S(2)}) copy-start(bf16[1,128,768]{2,1,0:T(8,128)(2,1)} %param.6) | copy-start | bytes 589828
  25.4 43.6 %copy-start.6 = (bf16[1,128,768]{2,1,0:T(8,128)(2,1)S(1)}, bf16[1,128,768]{2,1,0:T(8,128)(2,1)}, u32[]{:S(2)}) copy-start(bf16[1,128,768]{2,1,0:T(8,128)(2,1)} %param.7) | copy-start | bytes 589828
  31.0 8.3 %collective-permute-start.12 = (bf16[96,1152]{1,0:T(8,128)(2,1)S(1)}, bf16[96,1152]{1,0:T(8,128)(2,1)S(1)}, u32[]{:S(2)}, u32[]{:S(2)}) collective-permute-start(bf16[96,1152]{1,0:T(8,128)(2,1)S(1)} %get-tuple-element.34), channel_id=1, source_target_pairs={{0,64},{64,128},{128,192},{192,0},{1,65},{65,129},{129,193},{193,1... | collective-permute-start | bytes 663560 | tf_op jit(solution)/shard_map/ppermute | solution.py:251
  31.8 12.7 %collective-permute-start.13 = (bf16[96,1152]{1,0:T(8,128)(2,1)S(1)}, bf16[96,1152]{1,0:T(8,128)(2,1)S(1)}, u32[]{:S(2)}, u32[]{:S(2)}) collective-permute-start(bf16[96,1152]{1,0:T(8,128)(2,1)S(1)} %get-tuple-element.35), channel_id=1, source_target_pairs={{0,128},{64,192},{128,0},{192,64},{1,129},{65,193},{129,1},{193,65... | collective-permute-start | bytes 663560 | tf_op jit(solution)/shard_map/ppermute | solution.py:251
  34.2 10.3 %collective-permute-start.14 = (bf16[96,1152]{1,0:T(8,128)(2,1)S(1)}, bf16[96,1152]{1,0:T(8,128)(2,1)S(1)}, u32[]{:S(2)}, u32[]{:S(2)}) collective-permute-start(bf16[96,1152]{1,0:T(8,128)(2,1)S(1)} %get-tuple-element.36), channel_id=1, source_target_pairs={{0,192},{64,0},{128,64},{192,128},{1,193},{65,1},{129,65},{193,129... | collective-permute-start | bytes 663560 | tf_op jit(solution)/shard_map/ppermute | solution.py:251
  45.2 13.4 %collective-permute-start.15 = (bf16[12,1152]{1,0:T(8,128)(2,1)S(1)}, bf16[12,1152]{1,0:T(8,128)(2,1)S(1)}, u32[]{:S(2)}, u32[]{:S(2)}) collective-permute-start(bf16[12,1152]{1,0:T(8,128)(2,1)S(1)} %get-tuple-element.38), channel_id=1, source_target_pairs={{0,4},{4,8},{8,12},{12,16},{16,20},{20,24},{24,28},{28,0},{1,5},{5... | collective-permute-start | bytes 82952 | tf_op jit(solution)/shard_map/ppermute | solution.py:251
  47.0 14.1 %collective-permute-start.16 = (bf16[12,1152]{1,0:T(8,128)(2,1)S(1)}, bf16[12,1152]{1,0:T(8,128)(2,1)S(1)}, u32[]{:S(2)}, u32[]{:S(2)}) collective-permute-start(bf16[12,1152]{1,0:T(8,128)(2,1)S(1)} %get-tuple-element.39), channel_id=1, source_target_pairs={{0,8},{4,12},{8,16},{12,20},{16,24},{20,28},{24,0},{28,4},{1,9},{5... | collective-permute-start | bytes 82952 | tf_op jit(solution)/shard_map/ppermute | solution.py:251
  49.9 11.8 %collective-permute-start.17 = (bf16[12,1152]{1,0:T(8,128)(2,1)S(1)}, bf16[12,1152]{1,0:T(8,128)(2,1)S(1)}, u32[]{:S(2)}, u32[]{:S(2)}) collective-permute-start(bf16[12,1152]{1,0:T(8,128)(2,1)S(1)} %get-tuple-element.40), channel_id=1, source_target_pairs={{0,12},{4,16},{8,20},{12,24},{16,28},{20,0},{24,4},{28,8},{1,13},{... | collective-permute-start | bytes 82952 | tf_op jit(solution)/shard_map/ppermute | solution.py:251
  53.7 8.1 %collective-permute-start.18 = (bf16[12,1152]{1,0:T(8,128)(2,1)S(1)}, bf16[12,1152]{1,0:T(8,128)(2,1)S(1)}, u32[]{:S(2)}, u32[]{:S(2)}) collective-permute-start(bf16[12,1152]{1,0:T(8,128)(2,1)S(1)} %get-tuple-element.41), channel_id=1, source_target_pairs={{0,16},{4,20},{8,24},{12,28},{16,0},{20,4},{24,8},{28,12},{1,17},{... | collective-permute-start | bytes 82952 | tf_op jit(solution)/shard_map/ppermute | solution.py:251
  54.2 7.6 %collective-permute-start.19 = (bf16[12,1152]{1,0:T(8,128)(2,1)S(1)}, bf16[12,1152]{1,0:T(8,128)(2,1)S(1)}, u32[]{:S(2)}, u32[]{:S(2)}) collective-permute-start(bf16[12,1152]{1,0:T(8,128)(2,1)S(1)} %get-tuple-element.42), channel_id=1, source_target_pairs={{0,20},{4,24},{8,28},{12,0},{16,4},{20,8},{24,12},{28,16},{1,21},{... | collective-permute-start | bytes 82952 | tf_op jit(solution)/shard_map/ppermute | solution.py:251
  58.6 5.8 %collective-permute-start.20 = (bf16[12,1152]{1,0:T(8,128)(2,1)S(1)}, bf16[12,1152]{1,0:T(8,128)(2,1)S(1)}, u32[]{:S(2)}, u32[]{:S(2)}) collective-permute-start(bf16[12,1152]{1,0:T(8,128)(2,1)S(1)} %get-tuple-element.43), channel_id=1, source_target_pairs={{0,24},{4,28},{8,0},{12,4},{16,8},{20,12},{24,16},{28,20},{1,25},{... | collective-permute-start | bytes 82952 | tf_op jit(solution)/shard_map/ppermute | solution.py:251
  61.0 4.2 %collective-permute-start.21 = (bf16[12,1152]{1,0:T(8,128)(2,1)S(1)}, bf16[12,1152]{1,0:T(8,128)(2,1)S(1)}, u32[]{:S(2)}, u32[]{:S(2)}) collective-permute-start(bf16[12,1152]{1,0:T(8,128)(2,1)S(1)} %get-tuple-element.44), channel_id=1, source_target_pairs={{0,28},{4,0},{8,4},{12,8},{16,12},{20,16},{24,20},{28,24},{1,29},{... | collective-permute-start | bytes 82952 | tf_op jit(solution)/shard_map/ppermute | solution.py:251
  66.0 11.1 %collective-permute-start.22 = (bf16[12,576]{1,0:T(8,128)(2,1)S(1)}, bf16[12,576]{1,0:T(8,128)(2,1)S(1)}, u32[]{:S(2)}, u32[]{:S(2)}) collective-permute-start(bf16[12,576]{1,0:T(8,128)(2,1)S(1)} %get-tuple-element.46), channel_id=1, source_target_pairs={{0,32},{32,0},{1,33},{33,1},{2,34},{34,2},{3,35},{35,3},{4,36},{36... | collective-permute-start | bytes 41480 | tf_op jit(solution)/shard_map/ppermute | solution.py:251

commit v2 on v1

--- a/solution.py
+++ b/solution.py
@@ -6,6 +6,7 @@
 from jax.experimental import pallas as pl
 from jax.experimental.pallas import tpu as pltpu
 from jax.sharding import Mesh, PartitionSpec as P
+
 
 HEADS = 4
 HEAD_DIM = 192
@@ -76,15 +77,27 @@
 def forward_kernel(ids, *refs):
     q, k, v = refs[0:4], refs[4:8], refs[8:12]
     soft_ref, attended_ref, acted_ref = refs[12:15]
-    q_all, km, vm, s_ref, p_ref, o_ref = refs[15:]
+    q_all, km, vm, s_ref, p_ref, o_ref, own, sems = refs[15:]
     me = ids[0]
     inverse = 1.0 / math.sqrt(HEAD_DIM)
-    for r in range(4):
+    copies = [
+        pltpu.make_async_copy(source, own.at[n], sems.at[n])
+        for n, source in enumerate((q[0], k[0], v[0]))
+    ]
+    for copy in copies:
+        copy.start()
+    for r in (1, 2, 3, 0):
         at = slice(r * ROWS, (r + 1) * ROWS)
-        q_all[at, :] = q[r][...]
+        if r == 0:
+            for copy in copies:
+                copy.wait()
+            q_block, k_block, v_block = own.at[0], own.at[1], own.at[2]
+        else:
+            q_block, k_block, v_block = q[r], k[r], v[r]
+        q_all[at, :] = q_block[...]
         for h in range(HEADS):
-            km[h, at, :] = masked_window(window(k[r], h), h)
-            vm[h, at, :] = masked_window(window(v[r], h), h)
+            km[h, at, :] = masked_window(window(k_block, h), h)
+            vm[h, at, :] = masked_window(window(v_block, h), h)
     for h in range(HEADS):
         s_ref[...] = dot(window(q_all, h), km[h], NT)
         for c in range(8):
@@ -107,16 +120,18 @@
         acted_ref[pl.ds(start, ROWS), :] = gelu_value(full * factor).astype(BF16)
 
 
-def weight_kernel(ids, acted_ref, g0, g1, g2, g3, *refs):
+def weight_kernel(ids, acted_ref, g_own, g_core, g_across, g_diag, *refs):
     outs, (slab, shifted, total) = refs[:-3], refs[-3:]
     me, mx = ids[0], ids[1]
     parts = len(outs)
     slab[0:STEP, :] = jnp.zeros((STEP, HEAD_DIM), BF16)
     slab[STEP + 512 :, :] = jnp.zeros((STEP, HEAD_DIM), BF16)
-    for r, g in enumerate((g0, g1, g2, g3)):
+    for r, g in enumerate((g_own, g_core, g_across, g_diag)):
         mine = g[:, 0:192].astype(F32)
-        for s in range(1, 4):
-            mine = jnp.where(me == s, g[:, 192 * s : 192 * s + 192].astype(F32), mine)
+        count = g.shape[1] // HEAD_DIM
+        for s in range(1, count):
+            here = lax.rem(me, count) == s
+            mine = jnp.where(here, g[:, 192 * s : 192 * s + 192].astype(F32), mine)
         start = pl.multiple_of(block_start(me, r) + STEP, STEP)
         slab[pl.ds(start, ROWS), :] = mine.astype(BF16)
     for t in range(TAPS):
@@ -133,10 +148,11 @@
 
 
 def backward_kernel(ids, *refs):
-    q, k, v, g = refs[0:4], refs[4:8], refs[8:12], refs[12:16]
-    soft_ref, attended_ref, acted_ref, w_ref = refs[16:20]
-    conv_ref, dq_ref, dk_ref, dv_ref = refs[20:24]
-    km, vm, qm, g_pad, ga_ref, do_ref, dp_ref, ds_ref = refs[24:]
+    q, k, v = refs[0:4], refs[4:8], refs[8:12]
+    g_whole, g_need, g_rest = refs[12:14], refs[14:16], refs[16:18]
+    soft_ref, attended_ref, acted_ref, w_ref = refs[18:22]
+    conv_ref, dq_ref, dk_ref, dv_ref = refs[22:26]
+    km, vm, qm, g_pad, ga_ref, do_ref, dp_ref, ds_ref = refs[26:]
     me = ids[0]
     inverse = 1.0 / math.sqrt(HEAD_DIM)
     own = pl.multiple_of(me * ROWS, ROWS)
@@ -150,7 +166,14 @@
     for r in range(4):
         at = slice(r * ROWS, (r + 1) * ROWS)
         start = pl.multiple_of(block_start(me, r) + STEP, STEP)
-        g_pad[pl.ds(start, ROWS), :] = g[r][...]
+        if r < 2:
+            g_pad[pl.ds(start, ROWS), :] = g_whole[r][...]
+        else:
+            side = lax.div(me, 2)
+            need = pl.ds(pl.multiple_of(side * 384, 128), 384)
+            rest = pl.ds(pl.multiple_of((1 - side) * 384, 128), 384)
+            g_pad[pl.ds(start, ROWS), need] = g_need[r - 2][...]
+            g_pad[pl.ds(start, ROWS), rest] = g_rest[r - 2][...]
         for h in range(HEADS):
             km[h, at, :] = masked_window(window(k[r], h), h)
             vm[h, at, :] = masked_window(window(v[r], h), h)
@@ -196,7 +219,7 @@
     for j in range(count):
         total[j, 0:rows, :] = value[j * rows : (j + 1) * rows]
     for n, out in enumerate(outs):
-        out[...] = total[lax.rem(mz + n, count), 0:rows, :].astype(BF16)
+        out[...] = total[lax.rem(mz + n, count), 0:rows, :]
 
 
 def ids_parts(refs):
@@ -224,14 +247,20 @@
         out_ref[:, t, :] = value[:, 192 * t : 192 * t + 192]
 
 
-def call(kernel, outs, scratch, args, flops, limit=24):
+def call(kernel, outs, scratch, args, flops, limit=24, in_hbm=()):
     size = sum(math.prod(a.shape) * a.dtype.itemsize for a in (*args, *outs))
-    return pl.pallas_call(
+    run = pl.pallas_call(
         kernel,
         out_shape=outs,
         in_specs=[
-            pl.BlockSpec(memory_space=pltpu.SMEM if a.dtype == jnp.int32 else pltpu.VMEM)
-            for a in args
+            pl.BlockSpec(
+                memory_space=pltpu.SMEM
+                if a.dtype == jnp.int32
+                else pltpu.HBM
+                if n in in_hbm
+                else pltpu.VMEM
+            )
+            for n, a in enumerate(args)
         ],
         out_specs=[pl.BlockSpec(memory_space=pltpu.VMEM) for _ in outs],
         scratch_shapes=scratch,
@@ -239,7 +268,12 @@
         cost_estimate=pl.CostEstimate(
             flops=flops, bytes_accessed=size, transcendentals=0
         ),
-    )(*args)
+    )
+    args = [
+        pltpu.with_memory_space_constraint(a, pltpu.HBM) if n in in_hbm else a
+        for n, a in enumerate(args)
+    ]
+    return run(*args)
 
 
 def shaped(shape, dtype=BF16):
@@ -251,9 +285,19 @@
     return lax.ppermute(value, axis, [(i, (i + by) % count) for i in range(count)])
 
 
-def blocks(value):
-    across = shift(value, "yl", 1)
-    return value, shift(value, "core", 1), across, shift(across, "core", 1)
+def ring(terms, axis):
+    count = len(terms)
+    right, left = count // 2, count - 1 - count // 2
+    ahead = behind = None
+    for step in range(right):
+        n = right - step
+        ahead = terms[n] if step == 0 else terms[n] + ahead.astype(F32)
+        ahead = shift(ahead.astype(BF16), axis, 1)
+        if step < left:
+            n = count - left + step
+            behind = terms[n] if step == 0 else terms[n] + behind.astype(F32)
+            behind = shift(behind.astype(BF16), axis, -1)
+    return [terms[0], ahead] + ([behind] if left else [])
 
 
 def body(queries, key_rows, value_rows, conv_weight, output_gradient):
@@ -265,10 +309,25 @@
         [me, lax.axis_index("x"), lax.axis_index("z"), lax.axis_index("yh")]
     ).astype(jnp.int32)
     weight = jnp.transpose(conv_weight, (1, 0, 2))
-    k = blocks(key_rows[0])
-    q = blocks(queries[0])
-    v = blocks(value_rows[0])
-    g = blocks(output_gradient[0])
+    k, q, v, g = key_rows[0], queries[0], value_rows[0], output_gradient[0]
+    half = 384
+    side = lax.axis_index("yl")
+    sent = {
+        "k": k,
+        "q": q,
+        "v": v,
+        "need": lax.dynamic_slice(g, (0, (1 - side) * half), (ROWS, half)),
+        "rest": lax.dynamic_slice(g, (0, side * half), (ROWS, half)),
+    }
+    across = {n: shift(a, "yl", 1) for n, a in sent.items()}
+    near = {n: shift(a, "core", 1) for n, a in (("k", k), ("q", q), ("v", v), ("g", g))}
+    diag = {n: shift(a, "core", 1) for n, a in across.items()}
+    q = (q, near["q"], across["q"], diag["q"])
+    k = (k, near["k"], across["k"], diag["k"])
+    v = (v, near["v"], across["v"], diag["v"])
+    whole = (g, near["g"])
+    need = (across["need"], diag["need"])
+    rest = (across["rest"], diag["rest"])
     soft, attended, acted = call(
         forward_kernel,
         [shaped((HEADS, 512, 512), F32), shaped((512, 768)), shaped((576, 768))],
@@ -279,9 +338,12 @@
             pltpu.VMEM((512, 512), F32),
             pltpu.VMEM((512, 512), BF16),
             pltpu.VMEM((HEADS, 512, 256), F32),
+            pltpu.VMEM((3, ROWS, 768), BF16),
+            pltpu.SemaphoreType.DMA((3,)),
         ],
         [ids, *q, *k, *v],
         2_000_000_000,
+        in_hbm=(1, 5, 9),
     )
     rows = 768 // x_size
     pieces = call(
@@ -292,7 +354,7 @@
             pltpu.VMEM((512, 576), BF16),
             pltpu.VMEM((x_size, rows, 576), F32),
         ],
-        [ids, acted, *g],
+        [ids, acted, *whole, *need],
         500_000_000,
     )
     got = [pieces[0]] + [shift(pieces[n], "x", n) for n in range(1, x_size)]
@@ -309,19 +371,19 @@
             pltpu.VMEM((512, 512), F32),
             pltpu.VMEM((512, 512), BF16),
         ],
-        [ids, *q, *k, *v, *g, soft, attended, acted, weight],
+        [ids, *q, *k, *v, *whole, *need, *rest, soft, attended, acted, weight],
         4_000_000_000,
         36,
     )
     few = rows // 2 // z_size
     pieces = call(
         sum_kernel,
-        [shaped((few, 1152)) for _ in range(z_size)],
+        [shaped((few, 1152), F32) for _ in range(z_size)],
         [pltpu.VMEM((z_size, -(-few // 8) * 8, 1152), F32)],
         [ids, *got],
         1_000_000,
     )
-    got = [pieces[0]] + [shift(pieces[n], "z", n) for n in range(1, z_size)]
+    got = ring(pieces, "z")
     keep, send = call(
         half_kernel, [shaped((few, 576), F32), shaped((few, 576))], [], [ids, *got], 1_000_000
     )

time: 78.9 us -> 79.2 us (level)
  the two profiles are of different devices: /device:TPU:1 before, /device:TPU:2 now
where the time goes in v2:
time: 79.2 us; the launch traced here: 79.1 us
  waiting for transfers between devices  32.1 us (41%)
  starting transfers between devices  28 us (35%)
  Pallas kernels  17 us (21%)
  local copies, waits for them, and re-layouts  1.03 us (1%)
  between operations  0.84 us (1%)
    ppermute x25, waiting for transfers between devices, shift(): lax.ppermute(value, axis, [(i, (i + by) % count) for i in range(count)])  32.1 us
    ppermute x25, starting transfers between devices, shift(): lax.ppermute(value, axis, [(i, (i + by) % count) for i in range(count)])  28 us
    pallas_call x6, Pallas kernels, call(): return run(*args)  17 us
  transfers between devices with their start and end apart: 25, of which 12 were waited for; matrix products, arithmetic and copies ran while one was open for 0% of the time, Pallas kernels for 18%

profile of v2, /device:TPU:2, one launch (start us, length us, event | category | flops | bytes accessed | tf_op | source)
XLA Modules:
  0.0 79.1 jit_solution(1362173037428955487)
XLA Ops:
  0.6 1.0 %dynamic-slice_bitcast_fusion = (bf16[128,384]{1,0:T(8,128)(2,1)S(1)}, bf16[128,384]{1,0:T(8,128)(2,1)S(1)}) fusion(bf16[1,128,768]{2,1,0:T(8,128)(2,1)} %param.9, s32[]{:T(128)S(6)} %select_n.7, s32[]{:T(128)S(6)} %select_n.6), kind=kLoop, calls=%fused_computation | loop fusion | bytes 393224 | tf_op jit(solution)/shard_map/dynamic_slice | solution.py:320
  1.7 1.7 %collective-permute-start.10 = (bf16[128,384]{1,0:T(8,128)(2,1)S(1)}, bf16[128,384]{1,0:T(8,128)(2,1)S(1)}, u32[]{:S(2)}, u32[]{:S(2)}) collective-permute-start(bf16[128,384]{1,0:T(8,128)(2,1)S(1)} %get-tuple-element.48), channel_id=1, source_target_pairs={{0,2},{2,0},{1,3},{3,1},{4,6},{6,4},{5,7},{7,5},{8,10},{10,8},{9,1... | collective-permute-start | bytes 294920 | tf_op jit(solution)/shard_map/ppermute | solution.py:285
  3.8 1.6 %collective-permute-start.4 = (bf16[128,768]{1,0:T(8,128)(2,1)}, bf16[128,768]{1,0:T(8,128)(2,1)S(1)}, u32[]{:S(2)}, u32[]{:S(2)}) collective-permute-start(bf16[128,768]{1,0:T(8,128)(2,1)} %bitcast.25), channel_id=1, source_target_pairs={{0,2},{2,0},{1,3},{3,1},{4,6},{6,4},{5,7},{7,5},{8,10},{10,8},{9,1... | collective-permute-start | bytes 589832 | tf_op jit(solution)/shard_map/ppermute | solution.py:285
  5.8 1.2 %collective-permute-done.10.refs_14_.g_across = bf16[128,384]{1,0:T(8,128)(2,1)S(1)} collective-permute-done((bf16[128,384]{1,0:T(8,128)(2,1)S(1)}, bf16[128,384]{1,0:T(8,128)(2,1)S(1)}, u32[]{:S(2)}, u32[]{:S(2)}) %collective-permute-start.10) | collective-permute-done | bytes 98336 | tf_op jit(solution)/shard_map/ppermute | solution.py:285
  7.0 4.3 %collective-permute-done.1.refs_2_ = bf16[128,768]{1,0:T(8,128)(2,1)S(1)} collective-permute-done((bf16[128,768]{1,0:T(8,128)(2,1)}, bf16[128,768]{1,0:T(8,128)(2,1)S(1)}, u32[]{:S(2)}, u32[]{:S(2)}) %collective-permute-start.1) | collective-permute-done | bytes 196640 | tf_op jit(solution)/shard_map/ppermute | solution.py:285
  11.3 0.5 collective-permute-start.2
  11.8 3.7 %collective-permute-done.4.refs_6_ = bf16[128,768]{1,0:T(8,128)(2,1)S(1)} collective-permute-done((bf16[128,768]{1,0:T(8,128)(2,1)}, bf16[128,768]{1,0:T(8,128)(2,1)S(1)}, u32[]{:S(2)}, u32[]{:S(2)}) %collective-permute-start.4) | collective-permute-done | bytes 196640 | tf_op jit(solution)/shard_map/ppermute | solution.py:285
  15.5 3.5 %collective-permute-done.7.refs_10_ = bf16[128,768]{1,0:T(8,128)(2,1)S(1)} collective-permute-done((bf16[128,768]{1,0:T(8,128)(2,1)}, bf16[128,768]{1,0:T(8,128)(2,1)S(1)}, u32[]{:S(2)}, u32[]{:S(2)}) %collective-permute-start.7) | collective-permute-done | bytes 196640 | tf_op jit(solution)/shard_map/ppermute | solution.py:285
  19.0 0.5 collective-permute-start.9
  19.7 0.7 collective-permute-done.8.refs_11_
  20.4 4.6 %shard_map.92 = (f32[4,512,512]{2,1,0:T(8,128)S(1)}, bf16[512,768]{1,0:T(8,128)(2,1)S(1)}, bf16[576,768]{1,0:T(8,128)(2,1)S(1)}) custom-call(s32[4]{0:T(128)S(1)} %pad_add_fusion.ids, bf16[128,768]{1,0:T(8,128)(2,1)} %bitcast.23, bf16[128,768]{1,0:T(8,128)(2,1)S(1)} %collective-permute-done.refs_1_, bf16[128,768]{1,0:T(8,128)(2,1)S(1)} %collective-permute-done.1.refs_2_, ...), custom_call_target="tpu_custom_call" | custom-call | flops 2000000000 | bytes 8224784 | tf_op jit(solution)/shard_map/pallas_call | solution.py:276
  25.1 2.1 %shard_map.94 = (bf16[96,1152]{1,0:T(8,128)(2,1)S(1)}, bf16[96,1152]{1,0:T(8,128)(2,1)S(1)}, bf16[96,1152]{1,0:T(8,128)(2,1)S(1)}, bf16[96,1152]{1,0:T(8,128)(2,1)S(1)}) custom-call(s32[4]{0:T(128)S(1)} %pad_add_fusion.ids, bf16[576,768]{1,0:T(8,128)(2,1)S(1)} %get-tuple-element.28.refs_20_.acted_ref, bf16[128,768]{1,0:T(8,128)(2,1)S(1)} %bitcast.18, ...), custom_call_target="tpu_custom_call" | custom-call | flops 500000000 | bytes 2359312 | tf_op jit(solution)/shard_map/pallas_call | solution.py:276
  27.2 1.6 %collective-permute-start.14 = (bf16[96,1152]{1,0:T(8,128)(2,1)S(1)}, bf16[96,1152]{1,0:T(8,128)(2,1)S(1)}, u32[]{:S(2)}, u32[]{:S(2)}) collective-permute-start(bf16[96,1152]{1,0:T(8,128)(2,1)S(1)} %get-tuple-element.34), channel_id=1, source_target_pairs={{0,64},{64,128},{128,192},{192,0},{1,65},{65,129},{129,193},{193,1... | collective-permute-start | bytes 663560 | tf_op jit(solution)/shard_map/ppermute | solution.py:285
  28.8 1.5 %collective-permute-start.15 = (bf16[96,1152]{1,0:T(8,128)(2,1)S(1)}, bf16[96,1152]{1,0:T(8,128)(2,1)S(1)}, u32[]{:S(2)}, u32[]{:S(2)}) collective-permute-start(bf16[96,1152]{1,0:T(8,128)(2,1)S(1)} %get-tuple-element.35), channel_id=1, source_target_pairs={{0,128},{64,192},{128,0},{192,64},{1,129},{65,193},{129,1},{193,65... | collective-permute-start | bytes 663560 | tf_op jit(solution)/shard_map/ppermute | solution.py:285
  30.3 1.8 %collective-permute-start.16 = (bf16[96,1152]{1,0:T(8,128)(2,1)S(1)}, bf16[96,1152]{1,0:T(8,128)(2,1)S(1)}, u32[]{:S(2)}, u32[]{:S(2)}) collective-permute-start(bf16[96,1152]{1,0:T(8,128)(2,1)S(1)} %get-tuple-element.36), channel_id=1, source_target_pairs={{0,192},{64,0},{128,64},{192,128},{1,193},{65,1},{129,65},{193,129... | collective-permute-start | bytes 663560 | tf_op jit(solution)/shard_map/ppermute | solution.py:285
  32.0 1.5 %collective-permute-start.12 = (bf16[128,384]{1,0:T(8,128)(2,1)S(1)}, bf16[128,384]{1,0:T(8,128)(2,1)S(1)}, u32[]{:S(2)}, u32[]{:S(2)}) collective-permute-start(bf16[128,384]{1,0:T(8,128)(2,1)S(1)} %get-tuple-element.47), channel_id=1, source_target_pairs={{0,2},{2,0},{1,3},{3,1},{4,6},{6,4},{5,7},{7,5},{8,10},{10,8},{9,1... | collective-permute-start | bytes 294920 | tf_op jit(solution)/shard_map/ppermute | solution.py:285
  33.5 2.0 %collective-permute-done.14.refs_1_ = bf16[96,1152]{1,0:T(8,128)(2,1)S(1)} collective-permute-done((bf16[96,1152]{1,0:T(8,128)(2,1)S(1)}, bf16[96,1152]{1,0:T(8,128)(2,1)S(1)}, u32[]{:S(2)}, u32[]{:S(2)}) %collective-permute-start.14) | collective-permute-done | bytes 221216 | tf_op jit(solution)/shard_map/ppermute | solution.py:285
  35.6 3.0 %collective-permute-done.15.refs_2_ = bf16[96,1152]{1,0:T(8,128)(2,1)S(1)} collective-permute-done((bf16[96,1152]{1,0:T(8,128)(2,1)S(1)}, bf16[96,1152]{1,0:T(8,128)(2,1)S(1)}, u32[]{:S(2)}, u32[]{:S(2)}) %collective-permute-start.15) | collective-permute-done | bytes 221216 | tf_op jit(solution)/shard_map/ppermute | solution.py:285
  38.6 3.3 %collective-permute-done.16.refs_3_ = bf16[96,1152]{1,0:T(8,128)(2,1)S(1)} collective-permute-done((bf16[96,1152]{1,0:T(8,128)(2,1)S(1)}, bf16[96,1152]{1,0:T(8,128)(2,1)S(1)}, u32[]{:S(2)}, u32[]{:S(2)}) %collective-permute-start.16) | collective-permute-done | bytes 221216 | tf_op jit(solution)/shard_map/ppermute | solution.py:285
  41.9 0.8 shard_map.95
  42.7 1.7 %collective-permute-start.17 = (bf16[12,1152]{1,0:T(8,128)(2,1)S(1)}, bf16[12,1152]{1,0:T(8,128)(2,1)S(1)}, u32[]{:S(2)}, u32[]{:S(2)}) collective-permute-start(bf16[12,1152]{1,0:T(8,128)(2,1)S(1)} %convert_element_type.36), channel_id=1, source_target_pairs={{0,4},{4,8},{8,12},{12,16},{16,20},{20,24},{24,28},{28,0},{1,5},{5... | collective-permute-start | bytes 82952 | tf_op jit(solution)/shard_map/ppermute | solution.py:285
  44.4 4.1 %collective-permute-start.21 = (bf16[12,1152]{1,0:T(8,128)(2,1)S(1)}, bf16[12,1152]{1,0:T(8,128)(2,1)S(1)}, u32[]{:S(2)}, u32[]{:S(2)}) collective-permute-start(bf16[12,1152]{1,0:T(8,128)(2,1)S(1)} %convert_element_type.43), channel_id=1, source_target_pairs={{0,28},{4,0},{8,4},{12,8},{16,12},{20,16},{24,20},{28,24},{1,29},{... | collective-permute-start | bytes 82952 | tf_op jit(solution)/shard_map/ppermute | solution.py:285
  48.6 1.7 %collective-permute-done.17 = bf16[12,1152]{1,0:T(8,128)(2,1)S(1)} collective-permute-done((bf16[12,1152]{1,0:T(8,128)(2,1)S(1)}, bf16[12,1152]{1,0:T(8,128)(2,1)S(1)}, u32[]{:S(2)}, u32[]{:S(2)}) %collective-permute-start.17) | collective-permute-done | bytes 27680 | tf_op jit(solution)/shard_map/ppermute | solution.py:285
  50.4 3.4 %collective-permute-start.22 = (bf16[12,1152]{1,0:T(8,128)(2,1)S(1)}, bf16[12,1152]{1,0:T(8,128)(2,1)S(1)}, u32[]{:S(2)}, u32[]{:S(2)}) collective-permute-start(bf16[12,1152]{1,0:T(8,128)(2,1)S(1)} %add_convert_fusion.1), channel_id=1, source_target_pairs={{0,28},{4,0},{8,4},{12,8},{16,12},{20,16},{24,20},{28,24},{1,29},{... | collective-permute-start | bytes 82952 | tf_op jit(solution)/shard_map/ppermute | solution.py:285
  53.8 1.7 %collective-permute-done.18 = bf16[12,1152]{1,0:T(8,128)(2,1)S(1)} collective-permute-done((bf16[12,1152]{1,0:T(8,128)(2,1)S(1)}, bf16[12,1152]{1,0:T(8,128)(2,1)S(1)}, u32[]{:S(2)}, u32[]{:S(2)}) %collective-permute-start.18) | collective-permute-done | bytes 27680 | tf_op jit(solution)/shard_map/ppermute | solution.py:285
  55.7 3.4 %collective-permute-start.23 = (bf16[12,1152]{1,0:T(8,128)(2,1)S(1)}, bf16[12,1152]{1,0:T(8,128)(2,1)S(1)}, u32[]{:S(2)}, u32[]{:S(2)}) collective-permute-start(bf16[12,1152]{1,0:T(8,128)(2,1)S(1)} %add_convert_fusion), channel_id=1, source_target_pairs={{0,28},{4,0},{8,4},{12,8},{16,12},{20,16},{24,20},{28,24},{1,29},{... | collective-permute-start | bytes 82952 | tf_op jit(solution)/shard_map/ppermute | solution.py:285
  59.1 1.7 %collective-permute-done.19 = bf16[12,1152]{1,0:T(8,128)(2,1)S(1)} collective-permute-done((bf16[12,1152]{1,0:T(8,128)(2,1)S(1)}, bf16[12,1152]{1,0:T(8,128)(2,1)S(1)}, u32[]{:S(2)}, u32[]{:S(2)}) %collective-permute-start.19) | collective-permute-done | bytes 27680 | tf_op jit(solution)/shard_map/ppermute | solution.py:285
  60.9 5.1 %collective-permute-done.20.refs_1_ = bf16[12,1152]{1,0:T(8,128)(2,1)S(1)} collective-permute-done((bf16[12,1152]{1,0:T(8,128)(2,1)S(1)}, bf16[12,1152]{1,0:T(8,128)(2,1)S(1)}, u32[]{:S(2)}, u32[]{:S(2)}) %collective-permute-start.20) | collective-permute-done | bytes 27680 | tf_op jit(solution)/shard_map/ppermute | solution.py:285
  66.1 0.7 shard_map.96
  66.8 3.5 %collective-permute-start.24 = (bf16[12,576]{1,0:T(8,128)(2,1)S(1)}, bf16[12,576]{1,0:T(8,128)(2,1)S(1)}, u32[]{:S(2)}, u32[]{:S(2)}) collective-permute-start(bf16[12,576]{1,0:T(8,128)(2,1)S(1)} %get-tuple-element.46), channel_id=1, source_target_pairs={{0,32},{32,0},{1,33},{33,1},{2,34},{34,2},{3,35},{35,3},{4,36},{36... | collective-permute-start | bytes 41480 | tf_op jit(solution)/shard_map/ppermute | solution.py:285
  70.3 8.1 %shard_map.93 = (bf16[128,768]{1,0:T(8,128)(2,1)}, bf16[128,768]{1,0:T(8,128)(2,1)}, bf16[128,768]{1,0:T(8,128)(2,1)}, bf16[128,768]{1,0:T(8,128)(2,1)}) custom-call(s32[4]{0:T(128)S(1)} %pad_add_fusion.ids, bf16[128,768]{1,0:T(8,128)(2,1)S(1)} %bitcast.24, bf16[128,768]{1,0:T(8,128)(2,1)S(1)} %collective-permute-done.refs_1_, ...), custom_call_target="tpu_custom_call" | custom-call | flops 4000000000 | bytes 13336592 | tf_op jit(solution)/shard_map/pallas_call | solution.py:276
  78.4 0.7 shard_map.97
  (43 shorter events, 1.5 us)
Async XLA Ops:
  0.6 24.5 %copy-start = (bf16[1,128,768]{2,1,0:T(8,128)(2,1)S(1)}, bf16[1,128,768]{2,1,0:T(8,128)(2,1)}, u32[]{:S(2)}) copy-start(bf16[1,128,768]{2,1,0:T(8,128)(2,1)} %param.9) | copy-start | bytes 589828
  1.7 5.4 %collective-permute-start.10 = (bf16[128,384]{1,0:T(8,128)(2,1)S(1)}, bf16[128,384]{1,0:T(8,128)(2,1)S(1)}, u32[]{:S(2)}, u32[]{:S(2)}) collective-permute-start(bf16[128,384]{1,0:T(8,128)(2,1)S(1)} %get-tuple-element.48), channel_id=1, source_target_pairs={{0,2},{2,0},{1,3},{3,1},{4,6},{6,4},{5,7},{7,5},{8,10},{10,8},{9,1... | collective-permute-start | bytes 294920 | tf_op jit(solution)/shard_map/ppermute | solution.py:285
  3.3 8.0 %collective-permute-start.1 = (bf16[128,768]{1,0:T(8,128)(2,1)}, bf16[128,768]{1,0:T(8,128)(2,1)S(1)}, u32[]{:S(2)}, u32[]{:S(2)}) collective-permute-start(bf16[128,768]{1,0:T(8,128)(2,1)} %bitcast.21), channel_id=1, source_target_pairs={{0,2},{2,0},{1,3},{3,1},{4,6},{6,4},{5,7},{7,5},{8,10},{10,8},{9,1... | collective-permute-start | bytes 589832 | tf_op jit(solution)/shard_map/ppermute | solution.py:285
  3.8 7.5 %collective-permute-start = (bf16[128,768]{1,0:T(8,128)(2,1)}, bf16[128,768]{1,0:T(8,128)(2,1)S(1)}, u32[]{:S(2)}, u32[]{:S(2)}) collective-permute-start(bf16[128,768]{1,0:T(8,128)(2,1)} %bitcast.22), channel_id=1, source_target_pairs={{0,1},{1,0},{2,3},{3,2},{4,5},{5,4},{6,7},{7,6},{8,9},{9,8},{10,11... | collective-permute-start | bytes 589832 | tf_op jit(solution)/shard_map/ppermute | solution.py:285
  3.8 11.7 %collective-permute-start.4 = (bf16[128,768]{1,0:T(8,128)(2,1)}, bf16[128,768]{1,0:T(8,128)(2,1)S(1)}, u32[]{:S(2)}, u32[]{:S(2)}) collective-permute-start(bf16[128,768]{1,0:T(8,128)(2,1)} %bitcast.25), channel_id=1, source_target_pairs={{0,2},{2,0},{1,3},{3,1},{4,6},{6,4},{5,7},{7,5},{8,10},{10,8},{9,1... | collective-permute-start | bytes 589832 | tf_op jit(solution)/shard_map/ppermute | solution.py:285
  5.4 13.6 %collective-permute-start.7 = (bf16[128,768]{1,0:T(8,128)(2,1)}, bf16[128,768]{1,0:T(8,128)(2,1)S(1)}, u32[]{:S(2)}, u32[]{:S(2)}) collective-permute-start(bf16[128,768]{1,0:T(8,128)(2,1)} %bitcast.29), channel_id=1, source_target_pairs={{0,2},{2,0},{1,3},{3,1},{4,6},{6,4},{5,7},{7,5},{8,10},{10,8},{9,1... | collective-permute-start | bytes 589832 | tf_op jit(solution)/shard_map/ppermute | solution.py:285
  7.0 12.0 %collective-permute-start.3 = (bf16[128,768]{1,0:T(8,128)(2,1)}, bf16[128,768]{1,0:T(8,128)(2,1)S(1)}, u32[]{:S(2)}, u32[]{:S(2)}) collective-permute-start(bf16[128,768]{1,0:T(8,128)(2,1)} %bitcast.26), channel_id=1, source_target_pairs={{0,1},{1,0},{2,3},{3,2},{4,5},{5,4},{6,7},{7,6},{8,9},{9,8},{10,11... | collective-permute-start | bytes 589832 | tf_op jit(solution)/shard_map/ppermute | solution.py:285
  11.3 8.3 %collective-permute-start.6 = (bf16[128,768]{1,0:T(8,128)(2,1)}, bf16[128,768]{1,0:T(8,128)(2,1)S(1)}, u32[]{:S(2)}, u32[]{:S(2)}) collective-permute-start(bf16[128,768]{1,0:T(8,128)(2,1)} %bitcast.30), channel_id=1, source_target_pairs={{0,1},{1,0},{2,3},{3,2},{4,5},{5,4},{6,7},{7,6},{8,9},{9,8},{10,11... | collective-permute-start | bytes 589832 | tf_op jit(solution)/shard_map/ppermute | solution.py:285
  11.3 8.4 %collective-permute-start.2 = (bf16[128,768]{1,0:T(8,128)(2,1)S(1)}, bf16[128,768]{1,0:T(8,128)(2,1)S(1)}, u32[]{:S(2)}, u32[]{:S(2)}) collective-permute-start(bf16[128,768]{1,0:T(8,128)(2,1)S(1)} %collective-permute-done.1.refs_2_), channel_id=1, source_target_pairs={{0,1},{1,0},{2,3},{3,2},{4,5},{5,4},{6,7},{7,6},{8,9},{9,8},{10,11... | collective-permute-start | bytes 589832 | tf_op jit(solution)/shard_map/ppermute | solution.py:285
  15.5 4.2 %collective-permute-start.5 = (bf16[128,768]{1,0:T(8,128)(2,1)S(1)}, bf16[128,768]{1,0:T(8,128)(2,1)S(1)}, u32[]{:S(2)}, u32[]{:S(2)}) collective-permute-start(bf16[128,768]{1,0:T(8,128)(2,1)S(1)} %collective-permute-done.4.refs_6_), channel_id=1, source_target_pairs={{0,1},{1,0},{2,3},{3,2},{4,5},{5,4},{6,7},{7,6},{8,9},{9,8},{10,11... | collective-permute-start | bytes 589832 | tf_op jit(solution)/shard_map/ppermute | solution.py:285
  19.0 1.4 %collective-permute-start.8 = (bf16[128,768]{1,0:T(8,128)(2,1)S(1)}, bf16[128,768]{1,0:T(8,128)(2,1)S(1)}, u32[]{:S(2)}, u32[]{:S(2)}) collective-permute-start(bf16[128,768]{1,0:T(8,128)(2,1)S(1)} %collective-permute-done.7.refs_10_), channel_id=1, source_target_pairs={{0,1},{1,0},{2,3},{3,2},{4,5},{5,4},{6,7},{7,6},{8,9},{9,8},{10,11... | collective-permute-start | bytes 589832 | tf_op jit(solution)/shard_map/ppermute | solution.py:285
  19.0 6.1 %collective-permute-start.9 = (bf16[128,768]{1,0:T(8,128)(2,1)}, bf16[128,768]{1,0:T(8,128)(2,1)S(1)}, u32[]{:S(2)}, u32[]{:S(2)}) collective-permute-start(bf16[128,768]{1,0:T(8,128)(2,1)} %bitcast.17), channel_id=1, source_target_pairs={{0,1},{1,0},{2,3},{3,2},{4,5},{5,4},{6,7},{7,6},{8,9},{9,8},{10,11... | collective-permute-start | bytes 589832 | tf_op jit(solution)/shard_map/ppermute | solution.py:285
  19.6 50.7 %copy-start.1 = (bf16[768,3,768]{2,0,1:T(8,128)(2,1)S(1)}, bf16[768,3,768]{2,0,1:T(8,128)(2,1)}, u32[]{:S(2)}) copy-start(bf16[768,3,768]{2,0,1:T(8,128)(2,1)} %param.8) | copy-start | bytes 10616836
  19.6 50.7 %copy-start.2 = (bf16[1,128,768]{2,1,0:T(8,128)(2,1)S(1)}, bf16[1,128,768]{2,1,0:T(8,128)(2,1)}, u32[]{:S(2)}) copy-start(bf16[1,128,768]{2,1,0:T(8,128)(2,1)} %param.5) | copy-start | bytes 589828
  19.6 50.7 %copy-start.3 = (bf16[1,128,768]{2,1,0:T(8,128)(2,1)S(1)}, bf16[1,128,768]{2,1,0:T(8,128)(2,1)}, u32[]{:S(2)}) copy-start(bf16[1,128,768]{2,1,0:T(8,128)(2,1)} %param.6) | copy-start | bytes 589828
  19.6 50.7 %copy-start.4 = (bf16[1,128,768]{2,1,0:T(8,128)(2,1)S(1)}, bf16[1,128,768]{2,1,0:T(8,128)(2,1)}, u32[]{:S(2)}) copy-start(bf16[1,128,768]{2,1,0:T(8,128)(2,1)} %param.7) | copy-start | bytes 589828
  19.6 5.5 %collective-permute-start.11 = (bf16[128,384]{1,0:T(8,128)(2,1)S(1)}, bf16[128,384]{1,0:T(8,128)(2,1)S(1)}, u32[]{:S(2)}, u32[]{:S(2)}) collective-permute-start(bf16[128,384]{1,0:T(8,128)(2,1)S(1)} %collective-permute-done.10.refs_14_.g_across), channel_id=1, source_target_pairs={{0,1},{1,0},{2,3},{3,2},{4,5},{5,4},{6,7},{7,6},{8,9},{9,8},{10,11... | collective-permute-start | bytes 294920 | tf_op jit(solution)/shard_map/ppermute | solution.py:285
  27.2 8.4 %collective-permute-start.14 = (bf16[96,1152]{1,0:T(8,128)(2,1)S(1)}, bf16[96,1152]{1,0:T(8,128)(2,1)S(1)}, u32[]{:S(2)}, u32[]{:S(2)}) collective-permute-start(bf16[96,1152]{1,0:T(8,128)(2,1)S(1)} %get-tuple-element.34), channel_id=1, source_target_pairs={{0,64},{64,128},{128,192},{192,0},{1,65},{65,129},{129,193},{193,1... | collective-permute-start | bytes 663560 | tf_op jit(solution)/shard_map/ppermute | solution.py:285
  28.8 9.8 %collective-permute-start.15 = (bf16[96,1152]{1,0:T(8,128)(2,1)S(1)}, bf16[96,1152]{1,0:T(8,128)(2,1)S(1)}, u32[]{:S(2)}, u32[]{:S(2)}) collective-permute-start(bf16[96,1152]{1,0:T(8,128)(2,1)S(1)} %get-tuple-element.35), channel_id=1, source_target_pairs={{0,128},{64,192},{128,0},{192,64},{1,129},{65,193},{129,1},{193,65... | collective-permute-start | bytes 663560 | tf_op jit(solution)/shard_map/ppermute | solution.py:285
  30.3 11.7 %collective-permute-start.16 = (bf16[96,1152]{1,0:T(8,128)(2,1)S(1)}, bf16[96,1152]{1,0:T(8,128)(2,1)S(1)}, u32[]{:S(2)}, u32[]{:S(2)}) collective-permute-start(bf16[96,1152]{1,0:T(8,128)(2,1)S(1)} %get-tuple-element.36), channel_id=1, source_target_pairs={{0,192},{64,0},{128,64},{192,128},{1,193},{65,1},{129,65},{193,129... | collective-permute-start | bytes 663560 | tf_op jit(solution)/shard_map/ppermute | solution.py:285
  32.0 12.4 %collective-permute-start.12 = (bf16[128,384]{1,0:T(8,128)(2,1)S(1)}, bf16[128,384]{1,0:T(8,128)(2,1)S(1)}, u32[]{:S(2)}, u32[]{:S(2)}) collective-permute-start(bf16[128,384]{1,0:T(8,128)(2,1)S(1)} %get-tuple-element.47), channel_id=1, source_target_pairs={{0,2},{2,0},{1,3},{3,1},{4,6},{6,4},{5,7},{7,5},{8,10},{10,8},{9,1... | collective-permute-start | bytes 294920 | tf_op jit(solution)/shard_map/ppermute | solution.py:285
  42.7 7.6 %collective-permute-start.17 = (bf16[12,1152]{1,0:T(8,128)(2,1)S(1)}, bf16[12,1152]{1,0:T(8,128)(2,1)S(1)}, u32[]{:S(2)}, u32[]{:S(2)}) collective-permute-start(bf16[12,1152]{1,0:T(8,128)(2,1)S(1)} %convert_element_type.36), channel_id=1, source_target_pairs={{0,4},{4,8},{8,12},{12,16},{16,20},{20,24},{24,28},{28,0},{1,5},{5... | collective-permute-start | bytes 82952 | tf_op jit(solution)/shard_map/ppermute | solution.py:285
  44.4 25.9 %collective-permute-start.13 = (bf16[128,384]{1,0:T(8,128)(2,1)S(1)}, bf16[128,384]{1,0:T(8,128)(2,1)S(1)}, u32[]{:S(2)}, u32[]{:S(2)}) collective-permute-start(bf16[128,384]{1,0:T(8,128)(2,1)S(1)} %collective-permute-done.12.refs_16_), channel_id=1, source_target_pairs={{0,1},{1,0},{2,3},{3,2},{4,5},{5,4},{6,7},{7,6},{8,9},{9,8},{10,11... | collective-permute-start | bytes 294920 | tf_op jit(solution)/shard_map/ppermute | solution.py:285
  44.4 6.0 %collective-permute-start.21 = (bf16[12,1152]{1,0:T(8,128)(2,1)S(1)}, bf16[12,1152]{1,0:T(8,128)(2,1)S(1)}, u32[]{:S(2)}, u32[]{:S(2)}) collective-permute-start(bf16[12,1152]{1,0:T(8,128)(2,1)S(1)} %convert_element_type.43), channel_id=1, source_target_pairs={{0,28},{4,0},{8,4},{12,8},{16,12},{20,16},{24,20},{28,24},{1,29},{... | collective-permute-start | bytes 82952 | tf_op jit(solution)/shard_map/ppermute | solution.py:285
  50.3 5.2 %collective-permute-start.18 = (bf16[12,1152]{1,0:T(8,128)(2,1)S(1)}, bf16[12,1152]{1,0:T(8,128)(2,1)S(1)}, u32[]{:S(2)}, u32[]{:S(2)}) collective-permute-start(bf16[12,1152]{1,0:T(8,128)(2,1)S(1)} %add_convert_fusion.4), channel_id=1, source_target_pairs={{0,4},{4,8},{8,12},{12,16},{16,20},{20,24},{24,28},{28,0},{1,5},{5... | collective-permute-start | bytes 82952 | tf_op jit(solution)/shard_map/ppermute | solution.py:285
  50.4 5.2 %collective-permute-start.22 = (bf16[12,1152]{1,0:T(8,128)(2,1)S(1)}, bf16[12,1152]{1,0:T(8,128)(2,1)S(1)}, u32[]{:S(2)}, u32[]{:S(2)}) collective-permute-start(bf16[12,1152]{1,0:T(8,128)(2,1)S(1)} %add_convert_fusion.1), channel_id=1, source_target_pairs={{0,28},{4,0},{8,4},{12,8},{16,12},{20,16},{24,20},{28,24},{1,29},{... | collective-permute-start | bytes 82952 | tf_op jit(solution)/shard_map/ppermute | solution.py:285
  55.6 5.2 %collective-permute-start.19 = (bf16[12,1152]{1,0:T(8,128)(2,1)S(1)}, bf16[12,1152]{1,0:T(8,128)(2,1)S(1)}, u32[]{:S(2)}, u32[]{:S(2)}) collective-permute-start(bf16[12,1152]{1,0:T(8,128)(2,1)S(1)} %add_convert_fusion.3), channel_id=1, source_target_pairs={{0,4},{4,8},{8,12},{12,16},{16,20},{20,24},{24,28},{28,0},{1,5},{5... | collective-permute-start | bytes 82952 | tf_op jit(solution)/shard_map/ppermute | solution.py:285
  55.7 5.2 %collective-permute-start.23 = (bf16[12,1152]{1,0:T(8,128)(2,1)S(1)}, bf16[12,1152]{1,0:T(8,128)(2,1)S(1)}, u32[]{:S(2)}, u32[]{:S(2)}) collective-permute-start(bf16[12,1152]{1,0:T(8,128)(2,1)S(1)} %add_convert_fusion), channel_id=1, source_target_pairs={{0,28},{4,0},{8,4},{12,8},{16,12},{20,16},{24,20},{28,24},{1,29},{... | collective-permute-start | bytes 82952 | tf_op jit(solution)/shard_map/ppermute | solution.py:285
  60.8 5.2 %collective-permute-start.20 = (bf16[12,1152]{1,0:T(8,128)(2,1)S(1)}, bf16[12,1152]{1,0:T(8,128)(2,1)S(1)}, u32[]{:S(2)}, u32[]{:S(2)}) collective-permute-start(bf16[12,1152]{1,0:T(8,128)(2,1)S(1)} %add_convert_fusion.2), channel_id=1, source_target_pairs={{0,4},{4,8},{8,12},{12,16},{16,20},{20,24},{24,28},{28,0},{1,5},{5... | collective-permute-start | bytes 82952 | tf_op jit(solution)/shard_map/ppermute | solution.py:285
  66.8 11.6 %collective-permute-start.24 = (bf16[12,576]{1,0:T(8,128)(2,1)S(1)}, bf16[12,576]{1,0:T(8,128)(2,1)S(1)}, u32[]{:S(2)}, u32[]{:S(2)}) collective-permute-start(bf16[12,576]{1,0:T(8,128)(2,1)S(1)} %get-tuple-element.46), channel_id=1, source_target_pairs={{0,32},{32,0},{1,33},{33,1},{2,34},{34,2},{3,35},{35,3},{4,36},{36... | collective-permute-start | bytes 41480 | tf_op jit(solution)/shard_map/ppermute | solution.py:285

commit v3 on v2

--- a/solution.py
+++ b/solution.py
@@ -13,7 +13,7 @@
 TAPS = 3
 STEP = 32
 ROWS = 128
-SPLITS = {64: (4, 2, 8), 4: (1, 2, 2)}
+SPLITS = {64: (4, 2, 8), 16: (1, 2, 8)}
 
 tanh_scale = 0.7978845608028654
 cubic_term = 0.044715
@@ -74,15 +74,16 @@
     return pl.multiple_of(jnp.bitwise_xor(me, relative) * ROWS, ROWS)
 
 
-def forward_kernel(ids, *refs):
-    q, k, v = refs[0:4], refs[4:8], refs[8:12]
-    soft_ref, attended_ref, acted_ref = refs[12:15]
-    q_all, km, vm, s_ref, p_ref, o_ref, own, sems = refs[15:]
-    me = ids[0]
+def score_kernel(ids, *refs):
+    q, k, own_v = refs[0:4], refs[4:8], refs[8]
+    soft_ref, rounded_ref, v_ref = refs[9:12]
+    q_all, km, s_ref, own, sems = refs[12:]
     inverse = 1.0 / math.sqrt(HEAD_DIM)
     copies = [
-        pltpu.make_async_copy(source, own.at[n], sems.at[n])
-        for n, source in enumerate((q[0], k[0], v[0]))
+        pltpu.make_async_copy(source, target, sems.at[n])
+        for n, (source, target) in enumerate(
+            ((q[0], own.at[0]), (k[0], own.at[1]), (own_v, v_ref))
+        )
     ]
     for copy in copies:
         copy.start()
@@ -91,13 +92,9 @@
         if r == 0:
             for copy in copies:
                 copy.wait()
-            q_block, k_block, v_block = own.at[0], own.at[1], own.at[2]
-        else:
-            q_block, k_block, v_block = q[r], k[r], v[r]
-        q_all[at, :] = q_block[...]
+        q_all[at, :] = own[0] if r == 0 else q[r][...]
         for h in range(HEADS):
-            km[h, at, :] = masked_window(window(k_block, h), h)
-            vm[h, at, :] = masked_window(window(v_block, h), h)
+            km[h, at, :] = masked_window(window(own.at[1] if r == 0 else k[r], h), h)
     for h in range(HEADS):
         s_ref[...] = dot(window(q_all, h), km[h], NT)
         for c in range(8):
@@ -106,8 +103,20 @@
             e = jnp.exp(s - jnp.max(s, axis=1, keepdims=True))
             p = e / jnp.sum(e, axis=1, keepdims=True)
             soft_ref[h, at, :] = p
-            p_ref[at, :] = p.astype(BF16)
-        o_ref[h] = dot(p_ref[...], vm[h])
+            rounded_ref[h, at, :] = p.astype(BF16)
+
+
+def attend_kernel(ids, *refs):
+    rounded_ref, v = refs[0], refs[1:5]
+    attended_ref, acted_ref = refs[5:7]
+    vm, o_ref = refs[7:]
+    me = ids[0]
+    for r in range(4):
+        at = slice(r * ROWS, (r + 1) * ROWS)
+        for h in range(HEADS):
+            vm[h, at, :] = masked_window(window(v[r], h), h)
+    for h in range(HEADS):
+        o_ref[h] = dot(rounded_ref[h], vm[h])
     acted_ref[0:STEP, :] = jnp.zeros((STEP, 768), BF16)
     acted_ref[STEP + 512 :, :] = jnp.zeros((STEP, 768), BF16)
     for r in range(4):
@@ -143,7 +152,7 @@
     for j in range(parts):
         total[j] = result[j * rows : (j + 1) * rows]
     for n, out in enumerate(outs):
-        piece = total[lax.rem(mx + n, parts)]
+        piece = total[jnp.bitwise_xor(mx, n)]
         out[...] = jnp.concatenate([piece[:half], piece[half:]], axis=1).astype(BF16)
 
 
@@ -208,46 +217,45 @@
     dv_ref[...] = place(dv).astype(BF16)
 
 
-def sum_kernel(ids, *refs):
-    parts, outs, total = refs[: ids_parts(refs)], refs[ids_parts(refs) : -1], refs[-1]
-    mz = ids[2]
+def total_of(parts):
     value = parts[0][...].astype(F32)
     for part in parts[1:]:
         value = value + part[...].astype(F32)
-    count = len(outs)
-    rows = value.shape[0] // count
-    for j in range(count):
-        total[j, 0:rows, :] = value[j * rows : (j + 1) * rows]
+    return value
+
+
+def near_kernel(ids, *refs):
+    parts, outs, total = refs[:-5], refs[-5:-1], refs[-1]
+    low = lax.rem(ids[2], 4)
+    value = total_of(parts)
+    few = value.shape[0] // 8
+    for j in range(4):
+        for high in range(2):
+            at = (4 * high + j) * few
+            total[j, high * few : (high + 1) * few, :] = value[at : at + few]
     for n, out in enumerate(outs):
-        out[...] = total[lax.rem(mz + n, count), 0:rows, :]
-
-
-def ids_parts(refs):
-    shape = refs[0].shape
-    count = 0
-    while refs[count].shape == shape and count < len(refs) - 1:
-        count += 1
-    return count
-
-
-def half_kernel(ids, *refs):
-    parts, (keep_ref, send_ref) = refs[:-2], refs[-2:]
-    my = ids[3]
-    value = parts[0][...].astype(F32)
-    for part in parts[1:]:
-        value = value + part[...].astype(F32)
-    low, high = value[:, :576], value[:, 576:]
-    keep_ref[...] = jnp.where(my == 0, low, high)
-    send_ref[...] = jnp.where(my == 0, high, low).astype(BF16)
-
-
-def last_kernel(scale, keep_ref, got_ref, out_ref):
-    value = (keep_ref[...] + got_ref[...].astype(F32)) * scale
+        out[...] = total[jnp.bitwise_xor(low, n)].astype(out.dtype)
+
+
+def far_kernel(ids, *refs):
+    parts, outs = refs[:-4], refs[-4:]
+    high, my = lax.div(ids[2], 4), ids[3]
+    value = total_of(parts)
+    few, wide = value.shape[0] // 2, value.shape[1] // 2
+    rows = (value[:few], value[few:])
+    for n, out in enumerate(outs):
+        piece = jnp.where(high == n // 2, rows[0], rows[1])
+        piece = jnp.where(my == n % 2, piece[:, :wide], piece[:, wide:])
+        out[...] = piece.astype(out.dtype)
+
+
+def last_kernel(scale, *refs):
+    value = total_of(refs[:-1]) * scale
     for t in range(TAPS):
-        out_ref[:, t, :] = value[:, 192 * t : 192 * t + 192]
-
-
-def call(kernel, outs, scratch, args, flops, limit=24, in_hbm=()):
+        refs[-1][:, t, :] = value[:, 192 * t : 192 * t + 192]
+
+
+def call(kernel, outs, scratch, args, flops, limit=16, in_hbm=()):
     size = sum(math.prod(a.shape) * a.dtype.itemsize for a in (*args, *outs))
     run = pl.pallas_call(
         kernel,
@@ -280,28 +288,13 @@
     return jax.ShapeDtypeStruct(shape, dtype)
 
 
-def shift(value, axis, by):
+def swap(value, axis, mask):
     count = lax.axis_size(axis)
-    return lax.ppermute(value, axis, [(i, (i + by) % count) for i in range(count)])
-
-
-def ring(terms, axis):
-    count = len(terms)
-    right, left = count // 2, count - 1 - count // 2
-    ahead = behind = None
-    for step in range(right):
-        n = right - step
-        ahead = terms[n] if step == 0 else terms[n] + ahead.astype(F32)
-        ahead = shift(ahead.astype(BF16), axis, 1)
-        if step < left:
-            n = count - left + step
-            behind = terms[n] if step == 0 else terms[n] + behind.astype(F32)
-            behind = shift(behind.astype(BF16), axis, -1)
-    return [terms[0], ahead] + ([behind] if left else [])
+    return lax.ppermute(value, axis, [(i, i ^ mask) for i in range(count)])
 
 
 def body(queries, key_rows, value_rows, conv_weight, output_gradient):
-    x_size, z_size = lax.axis_size("x"), lax.axis_size("z")
+    x_size = lax.axis_size("x")
     sizes = [lax.axis_size(a) for a in ("x", "yh", "z", "yl", "core")]
     grad_scale = 1.0 / math.sqrt(math.prod(sizes) * ROWS)
     me = lax.axis_index("yl") * 2 + lax.axis_index("core")
@@ -319,31 +312,40 @@
         "need": lax.dynamic_slice(g, (0, (1 - side) * half), (ROWS, half)),
         "rest": lax.dynamic_slice(g, (0, side * half), (ROWS, half)),
     }
-    across = {n: shift(a, "yl", 1) for n, a in sent.items()}
-    near = {n: shift(a, "core", 1) for n, a in (("k", k), ("q", q), ("v", v), ("g", g))}
-    diag = {n: shift(a, "core", 1) for n, a in across.items()}
+    across = {n: swap(a, "yl", 1) for n, a in sent.items()}
+    near = {n: swap(a, "core", 1) for n, a in (("k", k), ("q", q), ("v", v), ("g", g))}
+    diag = {n: swap(a, "core", 1) for n, a in across.items()}
     q = (q, near["q"], across["q"], diag["q"])
     k = (k, near["k"], across["k"], diag["k"])
     v = (v, near["v"], across["v"], diag["v"])
     whole = (g, near["g"])
     need = (across["need"], diag["need"])
     rest = (across["rest"], diag["rest"])
-    soft, attended, acted = call(
-        forward_kernel,
-        [shaped((HEADS, 512, 512), F32), shaped((512, 768)), shaped((576, 768))],
+    soft, rounded, own_v = call(
+        score_kernel,
+        [
+            shaped((HEADS, 512, 512), F32),
+            shaped((HEADS, 512, 512)),
+            shaped((ROWS, 768)),
+        ],
         [
             pltpu.VMEM((512, 768), BF16),
             pltpu.VMEM((HEADS, 512, 256), BF16),
-            pltpu.VMEM((HEADS, 512, 256), BF16),
             pltpu.VMEM((512, 512), F32),
-            pltpu.VMEM((512, 512), BF16),
-            pltpu.VMEM((HEADS, 512, 256), F32),
-            pltpu.VMEM((3, ROWS, 768), BF16),
+            pltpu.VMEM((2, ROWS, 768), BF16),
             pltpu.SemaphoreType.DMA((3,)),
         ],
-        [ids, *q, *k, *v],
-        2_000_000_000,
+        [ids, *q, *k, v[0]],
+        1_000_000_000,
         in_hbm=(1, 5, 9),
+    )
+    v = (own_v, *v[1:])
+    attended, acted = call(
+        attend_kernel,
+        [shaped((512, 768)), shaped((576, 768))],
+        [pltpu.VMEM((HEADS, 512, 256), BF16), pltpu.VMEM((HEADS, 512, 256), F32)],
+        [ids, rounded, *v],
+        1_000_000_000,
     )
     rows = 768 // x_size
     pieces = call(
@@ -357,7 +359,7 @@
         [ids, acted, *whole, *need],
         500_000_000,
     )
-    got = [pieces[0]] + [shift(pieces[n], "x", n) for n in range(1, x_size)]
+    got = [pieces[0]] + [swap(pieces[n], "x", n) for n in range(1, x_size)]
     conv_out, grad_queries, grad_keys, grad_values = call(
         backward_kernel,
         [shaped((ROWS, 768)) for _ in range(4)],
@@ -373,26 +375,31 @@
         ],
         [ids, *q, *k, *v, *whole, *need, *rest, soft, attended, acted, weight],
         4_000_000_000,
-        36,
-    )
-    few = rows // 2 // z_size
+        24,
+    )
+    few = rows // 16
     pieces = call(
-        sum_kernel,
-        [shaped((few, 1152), F32) for _ in range(z_size)],
-        [pltpu.VMEM((z_size, -(-few // 8) * 8, 1152), F32)],
+        near_kernel,
+        [shaped((2 * few, 1152), F32)] + [shaped((2 * few, 1152)) for _ in range(3)],
+        [pltpu.VMEM((4, 2 * few, 1152), F32)],
         [ids, *got],
         1_000_000,
     )
-    got = ring(pieces, "z")
-    keep, send = call(
-        half_kernel, [shaped((few, 576), F32), shaped((few, 576))], [], [ids, *got], 1_000_000
-    )
-    other = shift(send, "yh", 1)
+    got = [pieces[0]] + [swap(pieces[n], "z", n) for n in range(1, 4)]
+    pieces = call(
+        far_kernel,
+        [shaped((few, 576), F32)] + [shaped((few, 576)) for _ in range(3)],
+        [],
+        [ids, *got],
+        1_000_000,
+    )
+    got = [pieces[0]] + [swap(pieces[1], "yh", 1), swap(pieces[2], "z", 4)]
+    got.append(swap(pieces[3], ("yh", "z"), 12))
     (grad_weight,) = call(
         lambda *refs: last_kernel(grad_scale, *refs),
         [shaped((few, TAPS, HEAD_DIM), F32)],
         [],
-        [keep, other],
+        got,
         1_000_000,
     )
     return conv_out[None], grad_queries[None], grad_keys[None], grad_values[None], grad_weight

time: 79.2 us -> 74.5 us (0.941)
  the two profiles are of different devices: /device:TPU:2 before, /device:TPU:16 now
where the time goes in v3:
time: 74.5 us; the launch traced here: 74.3 us
  waiting for transfers between devices  28.5 us (38%)
  starting transfers between devices  26.7 us (36%)
  Pallas kernels  17.3 us (23%)
  local copies, waits for them, and re-layouts  0.99 us (1%)
  between operations  0.77 us (1%)
    ppermute x23, waiting for transfers between devices, swap(): return lax.ppermute(value, axis, [(i, i ^ mask) for i in range(count)])  28.5 us
    ppermute x23, starting transfers between devices, swap(): return lax.ppermute(value, axis, [(i, i ^ mask) for i in range(count)])  26.7 us
    pallas_call x7, Pallas kernels, call(): return run(*args)  17.3 us
  transfers between devices with their start and end apart: 23, of which 9 were waited for; matrix products, arithmetic and copies ran while one was open for 0% of the time, Pallas kernels for 20%

profile of v3, /device:TPU:16, one launch (start us, length us, event | category | flops | bytes accessed | tf_op | source)
XLA Modules:
  0.0 74.3 jit_solution(4928628570189255577)
XLA Ops:
  0.6 1.0 %dynamic-slice_bitcast_fusion = (bf16[128,384]{1,0:T(8,128)(2,1)S(1)}, bf16[128,384]{1,0:T(8,128)(2,1)S(1)}) fusion(bf16[1,128,768]{2,1,0:T(8,128)(2,1)} %param.9, s32[]{:T(128)S(6)} %select_n.7, s32[]{:T(128)S(6)} %select_n.6), kind=kLoop, calls=%fused_computation | loop fusion | bytes 393224 | tf_op jit(solution)/shard_map/dynamic_slice | solution.py:313
  1.6 1.4 %collective-permute-start.10 = (bf16[128,384]{1,0:T(8,128)(2,1)S(1)}, bf16[128,384]{1,0:T(8,128)(2,1)S(1)}, u32[]{:S(2)}, u32[]{:S(2)}) collective-permute-start(bf16[128,384]{1,0:T(8,128)(2,1)S(1)} %get-tuple-element.48), channel_id=1, source_target_pairs={{0,2},{2,0},{1,3},{3,1},{4,6},{6,4},{5,7},{7,5},{8,10},{10,8},{9,1... | collective-permute-start | bytes 294920 | tf_op jit(solution)/shard_map/ppermute | solution.py:293
  3.0 0.7 collective-permute-start.1
  3.7 1.3 %collective-permute-start.4 = (bf16[128,768]{1,0:T(8,128)(2,1)}, bf16[128,768]{1,0:T(8,128)(2,1)S(1)}, u32[]{:S(2)}, u32[]{:S(2)}) collective-permute-start(bf16[128,768]{1,0:T(8,128)(2,1)} %bitcast.25), channel_id=1, source_target_pairs={{0,2},{2,0},{1,3},{3,1},{4,6},{6,4},{5,7},{7,5},{8,10},{10,8},{9,1... | collective-permute-start | bytes 589832 | tf_op jit(solution)/shard_map/ppermute | solution.py:293
  5.0 0.5 collective-permute-start.3
  5.5 1.8 %collective-permute-done.10.refs_14_.g_across = bf16[128,384]{1,0:T(8,128)(2,1)S(1)} collective-permute-done((bf16[128,384]{1,0:T(8,128)(2,1)S(1)}, bf16[128,384]{1,0:T(8,128)(2,1)S(1)}, u32[]{:S(2)}, u32[]{:S(2)}) %collective-permute-start.10) | collective-permute-done | bytes 98336 | tf_op jit(solution)/shard_map/ppermute | solution.py:293
  7.3 1.4 %collective-permute-start.7 = (bf16[128,768]{1,0:T(8,128)(2,1)}, bf16[128,768]{1,0:T(8,128)(2,1)S(1)}, u32[]{:S(2)}, u32[]{:S(2)}) collective-permute-start(bf16[128,768]{1,0:T(8,128)(2,1)} %bitcast.29), channel_id=1, source_target_pairs={{0,2},{2,0},{1,3},{3,1},{4,6},{6,4},{5,7},{7,5},{8,10},{10,8},{9,1... | collective-permute-start | bytes 589832 | tf_op jit(solution)/shard_map/ppermute | solution.py:293
  8.6 2.9 %collective-permute-done.1.refs_2_ = bf16[128,768]{1,0:T(8,128)(2,1)S(1)} collective-permute-done((bf16[128,768]{1,0:T(8,128)(2,1)}, bf16[128,768]{1,0:T(8,128)(2,1)S(1)}, u32[]{:S(2)}, u32[]{:S(2)}) %collective-permute-start.1) | collective-permute-done | bytes 196640 | tf_op jit(solution)/shard_map/ppermute | solution.py:293
  11.5 4.2 %collective-permute-done.4.refs_6_ = bf16[128,768]{1,0:T(8,128)(2,1)S(1)} collective-permute-done((bf16[128,768]{1,0:T(8,128)(2,1)}, bf16[128,768]{1,0:T(8,128)(2,1)S(1)}, u32[]{:S(2)}, u32[]{:S(2)}) %collective-permute-start.4) | collective-permute-done | bytes 196640 | tf_op jit(solution)/shard_map/ppermute | solution.py:293
  15.7 0.5 collective-permute-start.6
  16.3 2.6 %collective-permute-done.7.refs_3_.refs_10_ = bf16[128,768]{1,0:T(8,128)(2,1)S(1)} collective-permute-done((bf16[128,768]{1,0:T(8,128)(2,1)}, bf16[128,768]{1,0:T(8,128)(2,1)S(1)}, u32[]{:S(2)}, u32[]{:S(2)}) %collective-permute-start.7) | collective-permute-done | bytes 196640 | tf_op jit(solution)/shard_map/ppermute | solution.py:293
  19.0 0.6 collective-permute-start.11
  19.6 3.3 %shard_map.92 = (f32[4,512,512]{2,1,0:T(8,128)S(1)}, bf16[4,512,512]{2,1,0:T(8,128)(2,1)S(1)}, bf16[128,768]{1,0:T(8,128)(2,1)S(1)}) custom-call(s32[4]{0:T(128)S(1)} %pad_add_fusion.ids, bf16[128,768]{1,0:T(8,128)(2,1)} %bitcast.23, bf16[128,768]{1,0:T(8,128)(2,1)S(1)} %collective-permute-done.refs_1_, bf16[128,768]{1,0:T(8,128)(2,1)S(1)} %collective-permute-done.1.refs_2_, ...), custom_call_target="tpu_custom_call" | custom-call | flops 1000000000 | bytes 8257552 | tf_op jit(solution)/shard_map/pallas_call | solution.py:284
  23.0 1.9 %shard_map.93 = (bf16[512,768]{1,0:T(8,128)(2,1)S(1)}, bf16[576,768]{1,0:T(8,128)(2,1)S(1)}) custom-call(s32[4]{0:T(128)S(1)} %pad_add_fusion.ids, bf16[4,512,512]{2,1,0:T(8,128)(2,1)S(1)} %get-tuple-element.28.refs_0_, bf16[128,768]{1,0:T(8,128)(2,1)S(1)} %get-tuple-element.26.refs_1_.refs_8_, bf16[128,768]{1,0:T(8,128)(2,1)S(1)} %collective-permute-done.6.refs_2_.refs_9_, ...), custom_call_target="tpu_custom_call" | custom-call | flops 1000000000 | bytes 4554768 | tf_op jit(solution)/shard_map/pallas_call | solution.py:284
  24.9 2.0 %shard_map.95 = (bf16[96,1152]{1,0:T(8,128)(2,1)S(1)}, bf16[96,1152]{1,0:T(8,128)(2,1)S(1)}, bf16[96,1152]{1,0:T(8,128)(2,1)S(1)}, bf16[96,1152]{1,0:T(8,128)(2,1)S(1)}) custom-call(s32[4]{0:T(128)S(1)} %pad_add_fusion.ids, bf16[576,768]{1,0:T(8,128)(2,1)S(1)} %get-tuple-element.30.refs_20_.acted_ref, bf16[128,768]{1,0:T(8,128)(2,1)S(1)} %bitcast.18, ...), custom_call_target="tpu_custom_call" | custom-call | flops 500000000 | bytes 2359312 | tf_op jit(solution)/shard_map/pallas_call | solution.py:284
  26.9 1.6 %collective-permute-start.14 = (bf16[96,1152]{1,0:T(8,128)(2,1)S(1)}, bf16[96,1152]{1,0:T(8,128)(2,1)S(1)}, u32[]{:S(2)}, u32[]{:S(2)}) collective-permute-start(bf16[96,1152]{1,0:T(8,128)(2,1)S(1)} %get-tuple-element.36), channel_id=1, source_target_pairs={{0,64},{64,0},{128,192},{192,128},{1,65},{65,1},{129,193},{193,129... | collective-permute-start | bytes 663560 | tf_op jit(solution)/shard_map/ppermute | solution.py:293
  28.5 2.7 %collective-permute-start.15 = (bf16[96,1152]{1,0:T(8,128)(2,1)S(1)}, bf16[96,1152]{1,0:T(8,128)(2,1)S(1)}, u32[]{:S(2)}, u32[]{:S(2)}) collective-permute-start(bf16[96,1152]{1,0:T(8,128)(2,1)S(1)} %get-tuple-element.37), channel_id=1, source_target_pairs={{0,128},{64,192},{128,0},{192,64},{1,129},{65,193},{129,1},{193,65... | collective-permute-start | bytes 663560 | tf_op jit(solution)/shard_map/ppermute | solution.py:293
  31.2 0.5 collective-permute-start.16
  31.7 1.2 %collective-permute-start.12 = (bf16[128,384]{1,0:T(8,128)(2,1)S(1)}, bf16[128,384]{1,0:T(8,128)(2,1)S(1)}, u32[]{:S(2)}, u32[]{:S(2)}) collective-permute-start(bf16[128,384]{1,0:T(8,128)(2,1)S(1)} %get-tuple-element.47), channel_id=1, source_target_pairs={{0,2},{2,0},{1,3},{3,1},{4,6},{6,4},{5,7},{7,5},{8,10},{10,8},{9,1... | collective-permute-start | bytes 294920 | tf_op jit(solution)/shard_map/ppermute | solution.py:293
  32.9 3.4 %collective-permute-done.12.refs_16_ = bf16[128,384]{1,0:T(8,128)(2,1)S(1)} collective-permute-done((bf16[128,384]{1,0:T(8,128)(2,1)S(1)}, bf16[128,384]{1,0:T(8,128)(2,1)S(1)}, u32[]{:S(2)}, u32[]{:S(2)}) %collective-permute-start.12) | collective-permute-done | bytes 98336 | tf_op jit(solution)/shard_map/ppermute | solution.py:293
  36.3 5.1 %collective-permute-done.15.refs_2_ = bf16[96,1152]{1,0:T(8,128)(2,1)S(1)} collective-permute-done((bf16[96,1152]{1,0:T(8,128)(2,1)S(1)}, bf16[96,1152]{1,0:T(8,128)(2,1)S(1)}, u32[]{:S(2)}, u32[]{:S(2)}) %collective-permute-start.15) | collective-permute-done | bytes 221216 | tf_op jit(solution)/shard_map/ppermute | solution.py:293
  41.4 2.6 %collective-permute-done.16.refs_3_ = bf16[96,1152]{1,0:T(8,128)(2,1)S(1)} collective-permute-done((bf16[96,1152]{1,0:T(8,128)(2,1)S(1)}, bf16[96,1152]{1,0:T(8,128)(2,1)S(1)}, u32[]{:S(2)}, u32[]{:S(2)}) %collective-permute-start.16) | collective-permute-done | bytes 221216 | tf_op jit(solution)/shard_map/ppermute | solution.py:293
  44.0 0.7 %shard_map.96 = (f32[24,1152]{1,0:T(8,128)S(1)}, bf16[24,1152]{1,0:T(8,128)(2,1)S(1)}, bf16[24,1152]{1,0:T(8,128)(2,1)S(1)}, bf16[24,1152]{1,0:T(8,128)(2,1)S(1)}) custom-call(s32[4]{0:T(128)S(1)} %pad_add_fusion.ids, bf16[96,1152]{1,0:T(8,128)(2,1)S(1)} %get-tuple-element.35.refs_0_, bf16[96,1152]{1,0:T(8,128)(2,1)S(1)} %collective-permute-done.14.refs_1_, ...), custom_call_target="tpu_custom_call" | custom-call | flops 1000000 | bytes 1161232 | tf_op jit(solution)/shard_map/pallas_call | solution.py:284
  44.7 2.0 %collective-permute-start.17 = (bf16[24,1152]{1,0:T(8,128)(2,1)S(1)}, bf16[24,1152]{1,0:T(8,128)(2,1)S(1)}, u32[]{:S(2)}, u32[]{:S(2)}) collective-permute-start(bf16[24,1152]{1,0:T(8,128)(2,1)S(1)} %get-tuple-element.40), channel_id=1, source_target_pairs={{0,4},{4,0},{8,12},{12,8},{16,20},{20,16},{24,28},{28,24},{1,5},{5... | collective-permute-start | bytes 165896 | tf_op jit(solution)/shard_map/ppermute | solution.py:293
  46.7 3.3 %collective-permute-start.18 = (bf16[24,1152]{1,0:T(8,128)(2,1)S(1)}, bf16[24,1152]{1,0:T(8,128)(2,1)S(1)}, u32[]{:S(2)}, u32[]{:S(2)}) collective-permute-start(bf16[24,1152]{1,0:T(8,128)(2,1)S(1)} %get-tuple-element.41), channel_id=1, source_target_pairs={{0,8},{4,12},{8,0},{12,4},{16,24},{20,28},{24,16},{28,20},{1,9},{5... | collective-permute-start | bytes 165896 | tf_op jit(solution)/shard_map/ppermute | solution.py:293
  50.0 3.3 %collective-permute-done.18.refs_2_ = bf16[24,1152]{1,0:T(8,128)(2,1)S(1)} collective-permute-done((bf16[24,1152]{1,0:T(8,128)(2,1)S(1)}, bf16[24,1152]{1,0:T(8,128)(2,1)S(1)}, u32[]{:S(2)}, u32[]{:S(2)}) %collective-permute-start.18) | collective-permute-done | bytes 55328 | tf_op jit(solution)/shard_map/ppermute | solution.py:293
  53.3 2.6 %collective-permute-done.19.refs_3_ = bf16[24,1152]{1,0:T(8,128)(2,1)S(1)} collective-permute-done((bf16[24,1152]{1,0:T(8,128)(2,1)S(1)}, bf16[24,1152]{1,0:T(8,128)(2,1)S(1)}, u32[]{:S(2)}, u32[]{:S(2)}) %collective-permute-start.19) | collective-permute-done | bytes 55328 | tf_op jit(solution)/shard_map/ppermute | solution.py:293
  55.9 0.6 shard_map.97
  57.0 4.5 %collective-permute-start.21 = (bf16[12,576]{1,0:T(8,128)(2,1)S(1)}, bf16[12,576]{1,0:T(8,128)(2,1)S(1)}, u32[]{:S(2)}, u32[]{:S(2)}) collective-permute-start(bf16[12,576]{1,0:T(8,128)(2,1)S(1)} %get-tuple-element.45), channel_id=1, source_target_pairs={{0,16},{4,20},{8,24},{12,28},{16,0},{20,4},{24,8},{28,12},{1,17},{... | collective-permute-start | bytes 41480 | tf_op jit(solution)/shard_map/ppermute | solution.py:293
  61.5 4.1 %collective-permute-start.22 = (bf16[12,576]{1,0:T(8,128)(2,1)S(1)}, bf16[12,576]{1,0:T(8,128)(2,1)S(1)}, u32[]{:S(2)}, u32[]{:S(2)}) collective-permute-start(bf16[12,576]{1,0:T(8,128)(2,1)S(1)} %get-tuple-element.46), channel_id=1, source_target_pairs={{0,48},{4,52},{8,56},{12,60},{16,32},{20,36},{24,40},{28,44},{32,1... | collective-permute-start | bytes 41480 | tf_op jit(solution)/shard_map/ppermute | solution.py:293
  65.6 8.0 %shard_map.94 = (bf16[128,768]{1,0:T(8,128)(2,1)}, bf16[128,768]{1,0:T(8,128)(2,1)}, bf16[128,768]{1,0:T(8,128)(2,1)}, bf16[128,768]{1,0:T(8,128)(2,1)}) custom-call(s32[4]{0:T(128)S(1)} %pad_add_fusion.ids, bf16[128,768]{1,0:T(8,128)(2,1)S(1)} %bitcast.24, bf16[128,768]{1,0:T(8,128)(2,1)S(1)} %collective-permute-done.refs_1_, ...), custom_call_target="tpu_custom_call" | custom-call | flops 4000000000 | bytes 13336592 | tf_op jit(solution)/shard_map/pallas_call | solution.py:284
  73.6 0.7 shard_map.98
  (31 shorter events, 0.7 us)
Async XLA Ops:
  1.6 5.7 %collective-permute-start.10 = (bf16[128,384]{1,0:T(8,128)(2,1)S(1)}, bf16[128,384]{1,0:T(8,128)(2,1)S(1)}, u32[]{:S(2)}, u32[]{:S(2)}) collective-permute-start(bf16[128,384]{1,0:T(8,128)(2,1)S(1)} %get-tuple-element.48), channel_id=1, source_target_pairs={{0,2},{2,0},{1,3},{3,1},{4,6},{6,4},{5,7},{7,5},{8,10},{10,8},{9,1... | collective-permute-start | bytes 294920 | tf_op jit(solution)/shard_map/ppermute | solution.py:293
  3.0 8.5 %collective-permute-start.1 = (bf16[128,768]{1,0:T(8,128)(2,1)}, bf16[128,768]{1,0:T(8,128)(2,1)S(1)}, u32[]{:S(2)}, u32[]{:S(2)}) collective-permute-start(bf16[128,768]{1,0:T(8,128)(2,1)} %bitcast.21), channel_id=1, source_target_pairs={{0,2},{2,0},{1,3},{3,1},{4,6},{6,4},{5,7},{7,5},{8,10},{10,8},{9,1... | collective-permute-start | bytes 589832 | tf_op jit(solution)/shard_map/ppermute | solution.py:293
  3.7 12.0 %collective-permute-start.4 = (bf16[128,768]{1,0:T(8,128)(2,1)}, bf16[128,768]{1,0:T(8,128)(2,1)S(1)}, u32[]{:S(2)}, u32[]{:S(2)}) collective-permute-start(bf16[128,768]{1,0:T(8,128)(2,1)} %bitcast.25), channel_id=1, source_target_pairs={{0,2},{2,0},{1,3},{3,1},{4,6},{6,4},{5,7},{7,5},{8,10},{10,8},{9,1... | collective-permute-start | bytes 589832 | tf_op jit(solution)/shard_map/ppermute | solution.py:293
  5.0 10.7 %collective-permute-start = (bf16[128,768]{1,0:T(8,128)(2,1)}, bf16[128,768]{1,0:T(8,128)(2,1)S(1)}, u32[]{:S(2)}, u32[]{:S(2)}) collective-permute-start(bf16[128,768]{1,0:T(8,128)(2,1)} %bitcast.22), channel_id=1, source_target_pairs={{0,1},{1,0},{2,3},{3,2},{4,5},{5,4},{6,7},{7,6},{8,9},{9,8},{10,11... | collective-permute-start | bytes 589832 | tf_op jit(solution)/shard_map/ppermute | solution.py:293
  5.0 11.2 %collective-permute-start.3 = (bf16[128,768]{1,0:T(8,128)(2,1)}, bf16[128,768]{1,0:T(8,128)(2,1)S(1)}, u32[]{:S(2)}, u32[]{:S(2)}) collective-permute-start(bf16[128,768]{1,0:T(8,128)(2,1)} %bitcast.26), channel_id=1, source_target_pairs={{0,1},{1,0},{2,3},{3,2},{4,5},{5,4},{6,7},{7,6},{8,9},{9,8},{10,11... | collective-permute-start | bytes 589832 | tf_op jit(solution)/shard_map/ppermute | solution.py:293
  7.3 11.7 %collective-permute-start.7 = (bf16[128,768]{1,0:T(8,128)(2,1)}, bf16[128,768]{1,0:T(8,128)(2,1)S(1)}, u32[]{:S(2)}, u32[]{:S(2)}) collective-permute-start(bf16[128,768]{1,0:T(8,128)(2,1)} %bitcast.29), channel_id=1, source_target_pairs={{0,2},{2,0},{1,3},{3,1},{4,6},{6,4},{5,7},{7,5},{8,10},{10,8},{9,1... | collective-permute-start | bytes 589832 | tf_op jit(solution)/shard_map/ppermute | solution.py:293
  11.5 7.5 %collective-permute-start.2 = (bf16[128,768]{1,0:T(8,128)(2,1)S(1)}, bf16[128,768]{1,0:T(8,128)(2,1)S(1)}, u32[]{:S(2)}, u32[]{:S(2)}) collective-permute-start(bf16[128,768]{1,0:T(8,128)(2,1)S(1)} %collective-permute-done.1.refs_2_), channel_id=1, source_target_pairs={{0,1},{1,0},{2,3},{3,2},{4,5},{5,4},{6,7},{7,6},{8,9},{9,8},{10,11... | collective-permute-start | bytes 589832 | tf_op jit(solution)/shard_map/ppermute | solution.py:293
  15.7 3.9 %collective-permute-start.5 = (bf16[128,768]{1,0:T(8,128)(2,1)S(1)}, bf16[128,768]{1,0:T(8,128)(2,1)S(1)}, u32[]{:S(2)}, u32[]{:S(2)}) collective-permute-start(bf16[128,768]{1,0:T(8,128)(2,1)S(1)} %collective-permute-done.4.refs_6_), channel_id=1, source_target_pairs={{0,1},{1,0},{2,3},{3,2},{4,5},{5,4},{6,7},{7,6},{8,9},{9,8},{10,11... | collective-permute-start | bytes 589832 | tf_op jit(solution)/shard_map/ppermute | solution.py:293
  15.7 7.3 %collective-permute-start.6 = (bf16[128,768]{1,0:T(8,128)(2,1)}, bf16[128,768]{1,0:T(8,128)(2,1)S(1)}, u32[]{:S(2)}, u32[]{:S(2)}) collective-permute-start(bf16[128,768]{1,0:T(8,128)(2,1)} %bitcast.30), channel_id=1, source_target_pairs={{0,1},{1,0},{2,3},{3,2},{4,5},{5,4},{6,7},{7,6},{8,9},{9,8},{10,11... | collective-permute-start | bytes 589832 | tf_op jit(solution)/shard_map/ppermute | solution.py:293
  16.2 8.7 %collective-permute-start.9 = (bf16[128,768]{1,0:T(8,128)(2,1)}, bf16[128,768]{1,0:T(8,128)(2,1)S(1)}, u32[]{:S(2)}, u32[]{:S(2)}) collective-permute-start(bf16[128,768]{1,0:T(8,128)(2,1)} %bitcast.17), channel_id=1, source_target_pairs={{0,1},{1,0},{2,3},{3,2},{4,5},{5,4},{6,7},{7,6},{8,9},{9,8},{10,11... | collective-permute-start | bytes 589832 | tf_op jit(solution)/shard_map/ppermute | solution.py:293
  19.0 4.0 %collective-permute-start.8 = (bf16[128,768]{1,0:T(8,128)(2,1)S(1)}, bf16[128,768]{1,0:T(8,128)(2,1)S(1)}, u32[]{:S(2)}, u32[]{:S(2)}) collective-permute-start(bf16[128,768]{1,0:T(8,128)(2,1)S(1)} %collective-permute-done.7.refs_3_.refs_10_), channel_id=1, source_target_pairs={{0,1},{1,0},{2,3},{3,2},{4,5},{5,4},{6,7},{7,6},{8,9},{9,8},{10,11... | collective-permute-start | bytes 589832 | tf_op jit(solution)/shard_map/ppermute | solution.py:293
  19.0 5.9 %copy-start = (bf16[1,128,768]{2,1,0:T(8,128)(2,1)S(1)}, bf16[1,128,768]{2,1,0:T(8,128)(2,1)}, u32[]{:S(2)}) copy-start(bf16[1,128,768]{2,1,0:T(8,128)(2,1)} %param.9) | copy-start | bytes 589828
  19.0 5.8 %collective-permute-start.11 = (bf16[128,384]{1,0:T(8,128)(2,1)S(1)}, bf16[128,384]{1,0:T(8,128)(2,1)S(1)}, u32[]{:S(2)}, u32[]{:S(2)}) collective-permute-start(bf16[128,384]{1,0:T(8,128)(2,1)S(1)} %collective-permute-done.10.refs_14_.g_across), channel_id=1, source_target_pairs={{0,1},{1,0},{2,3},{3,2},{4,5},{5,4},{6,7},{7,6},{8,9},{9,8},{10,11... | collective-permute-start | bytes 294920 | tf_op jit(solution)/shard_map/ppermute | solution.py:293
  22.9 42.6 %copy-start.1 = (bf16[768,3,768]{2,0,1:T(8,128)(2,1)S(1)}, bf16[768,3,768]{2,0,1:T(8,128)(2,1)}, u32[]{:S(2)}) copy-start(bf16[768,3,768]{2,0,1:T(8,128)(2,1)} %param.8) | copy-start | bytes 10616836
  22.9 42.6 %copy-start.2 = (bf16[1,128,768]{2,1,0:T(8,128)(2,1)S(1)}, bf16[1,128,768]{2,1,0:T(8,128)(2,1)}, u32[]{:S(2)}) copy-start(bf16[1,128,768]{2,1,0:T(8,128)(2,1)} %param.5) | copy-start | bytes 589828
  23.0 42.6 %copy-start.3 = (bf16[1,128,768]{2,1,0:T(8,128)(2,1)S(1)}, bf16[1,128,768]{2,1,0:T(8,128)(2,1)}, u32[]{:S(2)}) copy-start(bf16[1,128,768]{2,1,0:T(8,128)(2,1)} %param.6) | copy-start | bytes 589828
  26.9 9.4 %collective-permute-start.14 = (bf16[96,1152]{1,0:T(8,128)(2,1)S(1)}, bf16[96,1152]{1,0:T(8,128)(2,1)S(1)}, u32[]{:S(2)}, u32[]{:S(2)}) collective-permute-start(bf16[96,1152]{1,0:T(8,128)(2,1)S(1)} %get-tuple-element.36), channel_id=1, source_target_pairs={{0,64},{64,0},{128,192},{192,128},{1,65},{65,1},{129,193},{193,129... | collective-permute-start | bytes 663560 | tf_op jit(solution)/shard_map/ppermute | solution.py:293
  28.5 12.9 %collective-permute-start.15 = (bf16[96,1152]{1,0:T(8,128)(2,1)S(1)}, bf16[96,1152]{1,0:T(8,128)(2,1)S(1)}, u32[]{:S(2)}, u32[]{:S(2)}) collective-permute-start(bf16[96,1152]{1,0:T(8,128)(2,1)S(1)} %get-tuple-element.37), channel_id=1, source_target_pairs={{0,128},{64,192},{128,0},{192,64},{1,129},{65,193},{129,1},{193,65... | collective-permute-start | bytes 663560 | tf_op jit(solution)/shard_map/ppermute | solution.py:293
  31.2 12.8 %collective-permute-start.16 = (bf16[96,1152]{1,0:T(8,128)(2,1)S(1)}, bf16[96,1152]{1,0:T(8,128)(2,1)S(1)}, u32[]{:S(2)}, u32[]{:S(2)}) collective-permute-start(bf16[96,1152]{1,0:T(8,128)(2,1)S(1)} %get-tuple-element.38), channel_id=1, source_target_pairs={{0,192},{64,128},{128,64},{192,0},{1,193},{65,129},{129,65},{193,1... | collective-permute-start | bytes 663560 | tf_op jit(solution)/shard_map/ppermute | solution.py:293
  31.7 4.6 %collective-permute-start.12 = (bf16[128,384]{1,0:T(8,128)(2,1)S(1)}, bf16[128,384]{1,0:T(8,128)(2,1)S(1)}, u32[]{:S(2)}, u32[]{:S(2)}) collective-permute-start(bf16[128,384]{1,0:T(8,128)(2,1)S(1)} %get-tuple-element.47), channel_id=1, source_target_pairs={{0,2},{2,0},{1,3},{3,1},{4,6},{6,4},{5,7},{7,5},{8,10},{10,8},{9,1... | collective-permute-start | bytes 294920 | tf_op jit(solution)/shard_map/ppermute | solution.py:293
  36.3 29.3 %collective-permute-start.13 = (bf16[128,384]{1,0:T(8,128)(2,1)S(1)}, bf16[128,384]{1,0:T(8,128)(2,1)S(1)}, u32[]{:S(2)}, u32[]{:S(2)}) collective-permute-start(bf16[128,384]{1,0:T(8,128)(2,1)S(1)} %collective-permute-done.12.refs_16_), channel_id=1, source_target_pairs={{0,1},{1,0},{2,3},{3,2},{4,5},{5,4},{6,7},{7,6},{8,9},{9,8},{10,11... | collective-permute-start | bytes 294920 | tf_op jit(solution)/shard_map/ppermute | solution.py:293
  44.7 5.3 %collective-permute-start.17 = (bf16[24,1152]{1,0:T(8,128)(2,1)S(1)}, bf16[24,1152]{1,0:T(8,128)(2,1)S(1)}, u32[]{:S(2)}, u32[]{:S(2)}) collective-permute-start(bf16[24,1152]{1,0:T(8,128)(2,1)S(1)} %get-tuple-element.40), channel_id=1, source_target_pairs={{0,4},{4,0},{8,12},{12,8},{16,20},{20,16},{24,28},{28,24},{1,5},{5... | collective-permute-start | bytes 165896 | tf_op jit(solution)/shard_map/ppermute | solution.py:293
  46.7 6.6 %collective-permute-start.18 = (bf16[24,1152]{1,0:T(8,128)(2,1)S(1)}, bf16[24,1152]{1,0:T(8,128)(2,1)S(1)}, u32[]{:S(2)}, u32[]{:S(2)}) collective-permute-start(bf16[24,1152]{1,0:T(8,128)(2,1)S(1)} %get-tuple-element.41), channel_id=1, source_target_pairs={{0,8},{4,12},{8,0},{12,4},{16,24},{20,28},{24,16},{28,20},{1,9},{5... | collective-permute-start | bytes 165896 | tf_op jit(solution)/shard_map/ppermute | solution.py:293
  50.0 6.0 %collective-permute-start.19 = (bf16[24,1152]{1,0:T(8,128)(2,1)S(1)}, bf16[24,1152]{1,0:T(8,128)(2,1)S(1)}, u32[]{:S(2)}, u32[]{:S(2)}) collective-permute-start(bf16[24,1152]{1,0:T(8,128)(2,1)S(1)} %get-tuple-element.42), channel_id=1, source_target_pairs={{0,12},{4,8},{8,4},{12,0},{16,28},{20,24},{24,20},{28,16},{1,13},{... | collective-permute-start | bytes 165896 | tf_op jit(solution)/shard_map/ppermute | solution.py:293
  56.6 17.0 %collective-permute-start.20 = (bf16[12,576]{1,0:T(8,128)(2,1)S(1)}, bf16[12,576]{1,0:T(8,128)(2,1)S(1)}, u32[]{:S(2)}, u32[]{:S(2)}) collective-permute-start(bf16[12,576]{1,0:T(8,128)(2,1)S(1)} %get-tuple-element.44), channel_id=1, source_target_pairs={{0,32},{32,0},{1,33},{33,1},{2,34},{34,2},{3,35},{35,3},{4,36},{36... | collective-permute-start | bytes 41480 | tf_op jit(solution)/shard_map/ppermute | solution.py:293
  57.0 16.6 %collective-permute-start.21 = (bf16[12,576]{1,0:T(8,128)(2,1)S(1)}, bf16[12,576]{1,0:T(8,128)(2,1)S(1)}, u32[]{:S(2)}, u32[]{:S(2)}) collective-permute-start(bf16[12,576]{1,0:T(8,128)(2,1)S(1)} %get-tuple-element.45), channel_id=1, source_target_pairs={{0,16},{4,20},{8,24},{12,28},{16,0},{20,4},{24,8},{28,12},{1,17},{... | collective-permute-start | bytes 41480 | tf_op jit(solution)/shard_map/ppermute | solution.py:293
  61.5 12.1 %collective-permute-start.22 = (bf16[12,576]{1,0:T(8,128)(2,1)S(1)}, bf16[12,576]{1,0:T(8,128)(2,1)S(1)}, u32[]{:S(2)}, u32[]{:S(2)}) collective-permute-start(bf16[12,576]{1,0:T(8,128)(2,1)S(1)} %get-tuple-element.46), channel_id=1, source_target_pairs={{0,48},{4,52},{8,56},{12,60},{16,32},{20,36},{24,40},{28,44},{32,1... | collective-permute-start | bytes 41480 | tf_op jit(solution)/shard_map/ppermute | solution.py:293

commit v4 on v3

--- a/solution.py
+++ b/solution.py
@@ -74,27 +74,38 @@
     return pl.multiple_of(jnp.bitwise_xor(me, relative) * ROWS, ROWS)
 
 
-def score_kernel(ids, *refs):
-    q, k, own_v = refs[0:4], refs[4:8], refs[8]
-    soft_ref, rounded_ref, v_ref = refs[9:12]
-    q_all, km, s_ref, own, sems = refs[12:]
-    inverse = 1.0 / math.sqrt(HEAD_DIM)
+def prep_kernel(ids, *refs):
+    sources, owns, (need_ref, rest_ref), sems = refs[:4], refs[4:8], refs[8:10], refs[10]
     copies = [
-        pltpu.make_async_copy(source, target, sems.at[n])
-        for n, (source, target) in enumerate(
-            ((q[0], own.at[0]), (k[0], own.at[1]), (own_v, v_ref))
-        )
+        pltpu.make_async_copy(source, own, sems.at[n])
+        for n, (source, own) in enumerate(zip(sources, owns))
     ]
     for copy in copies:
         copy.start()
-    for r in (1, 2, 3, 0):
+    for copy in copies:
+        copy.wait()
+    side = lax.div(ids[0], 2)
+    need = pl.multiple_of((1 - side) * 384, 128)
+    rest = pl.multiple_of(side * 384, 128)
+    need_ref[...] = owns[3][:, pl.ds(need, 384)]
+    rest_ref[...] = owns[3][:, pl.ds(rest, 384)]
+
+
+def keys_kernel(*refs):
+    k, km = refs[:4], refs[4]
+    for r in range(4):
         at = slice(r * ROWS, (r + 1) * ROWS)
-        if r == 0:
-            for copy in copies:
-                copy.wait()
-        q_all[at, :] = own[0] if r == 0 else q[r][...]
         for h in range(HEADS):
-            km[h, at, :] = masked_window(window(own.at[1] if r == 0 else k[r], h), h)
+            km[h, at, :] = masked_window(window(k[r], h), h)
+
+
+def score_kernel(*refs):
+    q, km = refs[0:4], refs[4]
+    soft_ref, rounded_ref = refs[5:7]
+    q_all, s_ref = refs[7:]
+    inverse = 1.0 / math.sqrt(HEAD_DIM)
+    for r in range(4):
+        q_all[r * ROWS : (r + 1) * ROWS, :] = q[r][...]
     for h in range(HEADS):
         s_ref[...] = dot(window(q_all, h), km[h], NT)
         for c in range(8):
@@ -108,8 +119,8 @@
 
 def attend_kernel(ids, *refs):
     rounded_ref, v = refs[0], refs[1:5]
-    attended_ref, acted_ref = refs[5:7]
-    vm, o_ref = refs[7:]
+    attended_ref, acted_ref, vm = refs[5:8]
+    o_ref = refs[8]
     me = ids[0]
     for r in range(4):
         at = slice(r * ROWS, (r + 1) * ROWS)
@@ -157,11 +168,11 @@
 
 
 def backward_kernel(ids, *refs):
-    q, k, v = refs[0:4], refs[4:8], refs[8:12]
-    g_whole, g_need, g_rest = refs[12:14], refs[14:16], refs[16:18]
-    soft_ref, attended_ref, acted_ref, w_ref = refs[18:22]
-    conv_ref, dq_ref, dk_ref, dv_ref = refs[22:26]
-    km, vm, qm, g_pad, ga_ref, do_ref, dp_ref, ds_ref = refs[26:]
+    q, km, vm = refs[0:4], refs[4], refs[5]
+    g_whole, g_need, g_rest = refs[6:8], refs[8:10], refs[10:12]
+    soft_ref, attended_ref, acted_ref, w_ref = refs[12:16]
+    conv_ref, dq_ref, dk_ref, dv_ref = refs[16:20]
+    qm, g_pad, ga_ref, do_ref, dp_ref, ds_ref = refs[20:]
     me = ids[0]
     inverse = 1.0 / math.sqrt(HEAD_DIM)
     own = pl.multiple_of(me * ROWS, ROWS)
@@ -184,8 +195,6 @@
             g_pad[pl.ds(start, ROWS), need] = g_need[r - 2][...]
             g_pad[pl.ds(start, ROWS), rest] = g_rest[r - 2][...]
         for h in range(HEADS):
-            km[h, at, :] = masked_window(window(k[r], h), h)
-            vm[h, at, :] = masked_window(window(v[r], h), h)
             qm[h, at, :] = masked_window(window(q[r], h), h)
     ga_ref[...] = dot(g_pad[2 * STEP : 2 * STEP + 512, :], w_ref[0], NT)
     ga_ref[...] += dot(g_pad[STEP : STEP + 512, :], w_ref[1], NT)
@@ -226,25 +235,23 @@
 
 def near_kernel(ids, *refs):
     parts, outs, total = refs[:-5], refs[-5:-1], refs[-1]
-    low = lax.rem(ids[2], 4)
+    pair = lax.div(ids[2], 2)
     value = total_of(parts)
-    few = value.shape[0] // 8
+    rows = value.shape[0] // 4
     for j in range(4):
-        for high in range(2):
-            at = (4 * high + j) * few
-            total[j, high * few : (high + 1) * few, :] = value[at : at + few]
+        total[j] = value[j * rows : (j + 1) * rows]
     for n, out in enumerate(outs):
-        out[...] = total[jnp.bitwise_xor(low, n)].astype(out.dtype)
+        out[...] = total[jnp.bitwise_xor(pair, n)].astype(out.dtype)
 
 
 def far_kernel(ids, *refs):
     parts, outs = refs[:-4], refs[-4:]
-    high, my = lax.div(ids[2], 4), ids[3]
+    odd, my = lax.rem(ids[2], 2), ids[3]
     value = total_of(parts)
     few, wide = value.shape[0] // 2, value.shape[1] // 2
     rows = (value[:few], value[few:])
     for n, out in enumerate(outs):
-        piece = jnp.where(high == n // 2, rows[0], rows[1])
+        piece = jnp.where(odd == n // 2, rows[0], rows[1])
         piece = jnp.where(my == n % 2, piece[:, :wide], piece[:, wide:])
         out[...] = piece.astype(out.dtype)
 
@@ -303,47 +310,40 @@
     ).astype(jnp.int32)
     weight = jnp.transpose(conv_weight, (1, 0, 2))
     k, q, v, g = key_rows[0], queries[0], value_rows[0], output_gradient[0]
-    half = 384
-    side = lax.axis_index("yl")
-    sent = {
-        "k": k,
-        "q": q,
-        "v": v,
-        "need": lax.dynamic_slice(g, (0, (1 - side) * half), (ROWS, half)),
-        "rest": lax.dynamic_slice(g, (0, side * half), (ROWS, half)),
-    }
-    across = {n: swap(a, "yl", 1) for n, a in sent.items()}
+    first = {n: swap(a, "yl", 1) for n, a in (("k", k), ("q", q))}
+    own_q, own_k, own_v, own_g, need, rest = call(
+        prep_kernel,
+        [shaped((ROWS, 768)) for _ in range(4)] + [shaped((ROWS, 384)) for _ in range(2)],
+        [pltpu.SemaphoreType.DMA((4,))],
+        [ids, q, k, v, g],
+        1_000_000,
+        in_hbm=(1, 2, 3, 4),
+    )
+    sent = {"v": v, "need": need, "rest": rest}
+    across = first | {n: swap(a, "yl", 1) for n, a in sent.items()}
     near = {n: swap(a, "core", 1) for n, a in (("k", k), ("q", q), ("v", v), ("g", g))}
     diag = {n: swap(a, "core", 1) for n, a in across.items()}
-    q = (q, near["q"], across["q"], diag["q"])
-    k = (k, near["k"], across["k"], diag["k"])
-    v = (v, near["v"], across["v"], diag["v"])
-    whole = (g, near["g"])
+    q = (own_q, near["q"], across["q"], diag["q"])
+    k = (own_k, near["k"], across["k"], diag["k"])
+    v = (own_v, near["v"], across["v"], diag["v"])
+    whole = (own_g, near["g"])
     need = (across["need"], diag["need"])
     rest = (across["rest"], diag["rest"])
-    soft, rounded, own_v = call(
+    (km,) = call(keys_kernel, [shaped((HEADS, 512, 256))], [], k, 1_000_000)
+    soft, rounded = call(
         score_kernel,
-        [
-            shaped((HEADS, 512, 512), F32),
-            shaped((HEADS, 512, 512)),
-            shaped((ROWS, 768)),
-        ],
+        [shaped((HEADS, 512, 512), F32), shaped((HEADS, 512, 512))],
         [
             pltpu.VMEM((512, 768), BF16),
-            pltpu.VMEM((HEADS, 512, 256), BF16),
             pltpu.VMEM((512, 512), F32),
-            pltpu.VMEM((2, ROWS, 768), BF16),
-            pltpu.SemaphoreType.DMA((3,)),
         ],
-        [ids, *q, *k, v[0]],
+        [*q, km],
         1_000_000_000,
-        in_hbm=(1, 5, 9),
-    )
-    v = (own_v, *v[1:])
-    attended, acted = call(
+    )
+    attended, acted, vm = call(
         attend_kernel,
-        [shaped((512, 768)), shaped((576, 768))],
-        [pltpu.VMEM((HEADS, 512, 256), BF16), pltpu.VMEM((HEADS, 512, 256), F32)],
+        [shaped((512, 768)), shaped((576, 768)), shaped((HEADS, 512, 256))],
+        [pltpu.VMEM((HEADS, 512, 256), F32)],
         [ids, rounded, *v],
         1_000_000_000,
     )
@@ -365,15 +365,13 @@
         [shaped((ROWS, 768)) for _ in range(4)],
         [
             pltpu.VMEM((HEADS, 512, 256), BF16),
-            pltpu.VMEM((HEADS, 512, 256), BF16),
-            pltpu.VMEM((HEADS, 512, 256), BF16),
             pltpu.VMEM((576, 768), BF16),
             pltpu.VMEM((512, 768), F32),
             pltpu.VMEM((512, 768), BF16),
             pltpu.VMEM((512, 512), F32),
             pltpu.VMEM((512, 512), BF16),
         ],
-        [ids, *q, *k, *v, *whole, *need, *rest, soft, attended, acted, weight],
+        [ids, *q, km, vm, *whole, *need, *rest, soft, attended, acted, weight],
         4_000_000_000,
         24,
     )
@@ -385,7 +383,7 @@
         [ids, *got],
         1_000_000,
     )
-    got = [pieces[0]] + [swap(pieces[n], "z", n) for n in range(1, 4)]
+    got = [pieces[0]] + [swap(pieces[n], "z", 2 * n) for n in range(1, 4)]
     pieces = call(
         far_kernel,
         [shaped((few, 576), F32)] + [shaped((few, 576)) for _ in range(3)],
@@ -393,8 +391,8 @@
         [ids, *got],
         1_000_000,
     )
-    got = [pieces[0]] + [swap(pieces[1], "yh", 1), swap(pieces[2], "z", 4)]
-    got.append(swap(pieces[3], ("yh", "z"), 12))
+    got = [pieces[0]] + [swap(pieces[1], "yh", 1), swap(pieces[2], "z", 1)]
+    got.append(swap(pieces[3], ("yh", "z"), 9))
     (grad_weight,) = call(
         lambda *refs: last_kernel(grad_scale, *refs),
         [shaped((few, TAPS, HEAD_DIM), F32)],

time: 74.5 us -> 73.4 us (0.985)
  the two profiles are of different devices: /device:TPU:16 before, /device:TPU:24 now
where the time goes in v4:
time: 73.4 us; the launch traced here: 73.3 us
  waiting for transfers between devices  30.1 us (41%)
  starting transfers between devices  24.8 us (34%)
  Pallas kernels  17.5 us (24%)
    ppermute x23, waiting for transfers between devices, swap(): return lax.ppermute(value, axis, [(i, i ^ mask) for i in range(count)])  30.1 us
    ppermute x23, starting transfers between devices, swap(): return lax.ppermute(value, axis, [(i, i ^ mask) for i in range(count)])  24.8 us
    pallas_call x9, Pallas kernels, call(): return run(*args)  17.5 us
  transfers between devices with their start and end apart: 23, of which 9 were waited for; matrix products, arithmetic and copies ran while one was open for 0% of the time, Pallas kernels for 20%

profile of v4, /device:TPU:24, one launch (start us, length us, event | category | flops | bytes accessed | tf_op | source)
XLA Modules:
  0.0 73.3 jit_solution(9933289761850125888)
XLA Ops:
  0.6 0.8 %collective-permute-start.4 = (bf16[128,768]{1,0:T(8,128)(2,1)}, bf16[128,768]{1,0:T(8,128)(2,1)S(1)}, u32[]{:S(2)}, u32[]{:S(2)}) collective-permute-start(bf16[128,768]{1,0:T(8,128)(2,1)} %bitcast.14), channel_id=1, source_target_pairs={{0,2},{2,0},{1,3},{3,1},{4,6},{6,4},{5,7},{7,5},{8,10},{10,8},{9,1... | collective-permute-start | bytes 589832 | tf_op jit(solution)/shard_map/ppermute | solution.py:300
  1.5 1.3 %collective-permute-start.1 = (bf16[128,768]{1,0:T(8,128)(2,1)}, bf16[128,768]{1,0:T(8,128)(2,1)S(1)}, u32[]{:S(2)}, u32[]{:S(2)}) collective-permute-start(bf16[128,768]{1,0:T(8,128)(2,1)} %bitcast.17), channel_id=1, source_target_pairs={{0,2},{2,0},{1,3},{3,1},{4,6},{6,4},{5,7},{7,5},{8,10},{10,8},{9,1... | collective-permute-start | bytes 589832 | tf_op jit(solution)/shard_map/ppermute | solution.py:300
  2.7 0.7 %collective-permute-start.7 = (bf16[128,768]{1,0:T(8,128)(2,1)}, bf16[128,768]{1,0:T(8,128)(2,1)S(1)}, u32[]{:S(2)}, u32[]{:S(2)}) collective-permute-start(bf16[128,768]{1,0:T(8,128)(2,1)} %bitcast.20), channel_id=1, source_target_pairs={{0,2},{2,0},{1,3},{3,1},{4,6},{6,4},{5,7},{7,5},{8,10},{10,8},{9,1... | collective-permute-start | bytes 589832 | tf_op jit(solution)/shard_map/ppermute | solution.py:300
  3.6 1.8 %shard_map.92 = (bf16[128,768]{1,0:T(8,128)(2,1)S(1)}, bf16[128,768]{1,0:T(8,128)(2,1)S(1)}, bf16[128,768]{1,0:T(8,128)(2,1)S(1)}, bf16[128,768]{1,0:T(8,128)(2,...) custom-call(s32[4]{0:T(128)S(1)} %pad_add_fusion.ids, bf16[128,768]{1,0:T(8,128)(2,1)} %bitcast.18, ...), custom_call_target="tpu_custom_call" | custom-call | flops 1000000 | bytes 1769488 | tf_op jit(solution)/shard_map/pallas_call | solution.py:291
  5.4 1.4 %collective-permute-start.10 = (bf16[128,384]{1,0:T(8,128)(2,1)S(1)}, bf16[128,384]{1,0:T(8,128)(2,1)S(1)}, u32[]{:S(2)}, u32[]{:S(2)}) collective-permute-start(bf16[128,384]{1,0:T(8,128)(2,1)S(1)} %get-tuple-element.38), channel_id=1, source_target_pairs={{0,2},{2,0},{1,3},{3,1},{4,6},{6,4},{5,7},{7,5},{8,10},{10,8},{9,1... | collective-permute-start | bytes 294920 | tf_op jit(solution)/shard_map/ppermute | solution.py:300
  6.8 1.9 %collective-permute-done.4.refs_2_ = bf16[128,768]{1,0:T(8,128)(2,1)S(1)} collective-permute-done((bf16[128,768]{1,0:T(8,128)(2,1)}, bf16[128,768]{1,0:T(8,128)(2,1)S(1)}, u32[]{:S(2)}, u32[]{:S(2)}) %collective-permute-start.4) | collective-permute-done | bytes 196640 | tf_op jit(solution)/shard_map/ppermute | solution.py:300
  8.7 9.4 %collective-permute-done.10.refs_8_.g_across = bf16[128,384]{1,0:T(8,128)(2,1)S(1)} collective-permute-done((bf16[128,384]{1,0:T(8,128)(2,1)S(1)}, bf16[128,384]{1,0:T(8,128)(2,1)S(1)}, u32[]{:S(2)}, u32[]{:S(2)}) %collective-permute-start.10) | collective-permute-done | bytes 98336 | tf_op jit(solution)/shard_map/ppermute | solution.py:300
  18.1 0.5 collective-permute-start.2
  18.7 0.4 collective-permute-start.8
  19.3 0.4 collective-permute-done.refs_1_
  19.9 0.1 collective-permute-done.2.refs_3_
  20.0 1.6 %shard_map.94 = (f32[4,512,512]{2,1,0:T(8,128)S(1)}, bf16[4,512,512]{2,1,0:T(8,128)(2,1)S(1)}) custom-call(bf16[128,768]{1,0:T(8,128)(2,1)S(1)} %get-tuple-element.32.refs_0_, bf16[128,768]{1,0:T(8,128)(2,1)S(1)} %collective-permute-done.refs_1_, bf16[128,768]{1,0:T(8,128)(2,1)S(1)} %collective-permute-done.1.refs_2_, ...), custom_call_target="tpu_custom_call" | custom-call | flops 1000000000 | bytes 8126464 | tf_op jit(solution)/shard_map/pallas_call | solution.py:291
  21.7 1.9 %shard_map.95 = (bf16[512,768]{1,0:T(8,128)(2,1)S(1)}, bf16[576,768]{1,0:T(8,128)(2,1)S(1)}, bf16[4,512,256]{2,1,0:T(8,128)(2,1)S(1)}) custom-call(s32[4]{0:T(128)S(1)} %pad_add_fusion.ids, bf16[4,512,512]{2,1,0:T(8,128)(2,1)S(1)} %get-tuple-element.34.refs_0_, bf16[128,768]{1,0:T(8,128)(2,1)S(1)} %get-tuple-element.35.refs_1_, ...), custom_call_target="tpu_custom_call" | custom-call | flops 1000000000 | bytes 5603344 | tf_op jit(solution)/shard_map/pallas_call | solution.py:291
  23.6 2.0 %shard_map.97 = (bf16[96,1152]{1,0:T(8,128)(2,1)S(1)}, bf16[96,1152]{1,0:T(8,128)(2,1)S(1)}, bf16[96,1152]{1,0:T(8,128)(2,1)S(1)}, bf16[96,1152]{1,0:T(8,128)(2,1)S(1)}) custom-call(s32[4]{0:T(128)S(1)} %pad_add_fusion.ids, bf16[576,768]{1,0:T(8,128)(2,1)S(1)} %get-tuple-element.42.refs_14_.acted_ref, bf16[128,768]{1,0:T(8,128)(2,1)S(1)} %get-tuple-element.37.refs_6_.g_own, ...), custom_call_target="tpu_custom_call" | custom-call | flops 500000000 | bytes 2359312 | tf_op jit(solution)/shard_map/pallas_call | solution.py:291
  25.6 1.6 %collective-permute-start.14 = (bf16[96,1152]{1,0:T(8,128)(2,1)S(1)}, bf16[96,1152]{1,0:T(8,128)(2,1)S(1)}, u32[]{:S(2)}, u32[]{:S(2)}) collective-permute-start(bf16[96,1152]{1,0:T(8,128)(2,1)S(1)} %get-tuple-element.48), channel_id=1, source_target_pairs={{0,64},{64,0},{128,192},{192,128},{1,65},{65,1},{129,193},{193,129... | collective-permute-start | bytes 663560 | tf_op jit(solution)/shard_map/ppermute | solution.py:300
  27.2 2.7 %collective-permute-start.15 = (bf16[96,1152]{1,0:T(8,128)(2,1)S(1)}, bf16[96,1152]{1,0:T(8,128)(2,1)S(1)}, u32[]{:S(2)}, u32[]{:S(2)}) collective-permute-start(bf16[96,1152]{1,0:T(8,128)(2,1)S(1)} %get-tuple-element.49), channel_id=1, source_target_pairs={{0,128},{64,192},{128,0},{192,64},{1,129},{65,193},{129,1},{193,65... | collective-permute-start | bytes 663560 | tf_op jit(solution)/shard_map/ppermute | solution.py:300
  29.9 0.5 collective-permute-start.16
  30.4 0.7 %collective-permute-start.12 = (bf16[128,384]{1,0:T(8,128)(2,1)S(1)}, bf16[128,384]{1,0:T(8,128)(2,1)S(1)}, u32[]{:S(2)}, u32[]{:S(2)}) collective-permute-start(bf16[128,384]{1,0:T(8,128)(2,1)S(1)} %get-tuple-element.39), channel_id=1, source_target_pairs={{0,2},{2,0},{1,3},{3,1},{4,6},{6,4},{5,7},{7,5},{8,10},{10,8},{9,1... | collective-permute-start | bytes 294920 | tf_op jit(solution)/shard_map/ppermute | solution.py:300
  31.1 3.9 %collective-permute-done.12.refs_10_ = bf16[128,384]{1,0:T(8,128)(2,1)S(1)} collective-permute-done((bf16[128,384]{1,0:T(8,128)(2,1)S(1)}, bf16[128,384]{1,0:T(8,128)(2,1)S(1)}, u32[]{:S(2)}, u32[]{:S(2)}) %collective-permute-start.12) | collective-permute-done | bytes 98336 | tf_op jit(solution)/shard_map/ppermute | solution.py:300
  35.0 5.3 %collective-permute-done.15.refs_2_ = bf16[96,1152]{1,0:T(8,128)(2,1)S(1)} collective-permute-done((bf16[96,1152]{1,0:T(8,128)(2,1)S(1)}, bf16[96,1152]{1,0:T(8,128)(2,1)S(1)}, u32[]{:S(2)}, u32[]{:S(2)}) %collective-permute-start.15) | collective-permute-done | bytes 221216 | tf_op jit(solution)/shard_map/ppermute | solution.py:300
  40.3 2.6 %collective-permute-done.16.refs_3_ = bf16[96,1152]{1,0:T(8,128)(2,1)S(1)} collective-permute-done((bf16[96,1152]{1,0:T(8,128)(2,1)S(1)}, bf16[96,1152]{1,0:T(8,128)(2,1)S(1)}, u32[]{:S(2)}, u32[]{:S(2)}) %collective-permute-start.16) | collective-permute-done | bytes 221216 | tf_op jit(solution)/shard_map/ppermute | solution.py:300
  42.9 0.7 shard_map.98
  43.6 3.4 %collective-permute-start.17 = (bf16[24,1152]{1,0:T(8,128)(2,1)S(1)}, bf16[24,1152]{1,0:T(8,128)(2,1)S(1)}, u32[]{:S(2)}, u32[]{:S(2)}) collective-permute-start(bf16[24,1152]{1,0:T(8,128)(2,1)S(1)} %get-tuple-element.52), channel_id=1, source_target_pairs={{0,8},{4,12},{8,0},{12,4},{16,24},{20,28},{24,16},{28,20},{1,9},{5... | collective-permute-start | bytes 165896 | tf_op jit(solution)/shard_map/ppermute | solution.py:300
  47.0 5.4 %collective-permute-start.18 = (bf16[24,1152]{1,0:T(8,128)(2,1)S(1)}, bf16[24,1152]{1,0:T(8,128)(2,1)S(1)}, u32[]{:S(2)}, u32[]{:S(2)}) collective-permute-start(bf16[24,1152]{1,0:T(8,128)(2,1)S(1)} %get-tuple-element.53), channel_id=1, source_target_pairs={{0,16},{4,20},{8,24},{12,28},{16,0},{20,4},{24,8},{28,12},{1,17},{... | collective-permute-start | bytes 165896 | tf_op jit(solution)/shard_map/ppermute | solution.py:300
  52.4 2.8 %collective-permute-done.18.refs_2_ = bf16[24,1152]{1,0:T(8,128)(2,1)S(1)} collective-permute-done((bf16[24,1152]{1,0:T(8,128)(2,1)S(1)}, bf16[24,1152]{1,0:T(8,128)(2,1)S(1)}, u32[]{:S(2)}, u32[]{:S(2)}) %collective-permute-start.18) | collective-permute-done | bytes 55328 | tf_op jit(solution)/shard_map/ppermute | solution.py:300
  55.2 3.5 %collective-permute-done.19.refs_3_ = bf16[24,1152]{1,0:T(8,128)(2,1)S(1)} collective-permute-done((bf16[24,1152]{1,0:T(8,128)(2,1)S(1)}, bf16[24,1152]{1,0:T(8,128)(2,1)S(1)}, u32[]{:S(2)}, u32[]{:S(2)}) %collective-permute-start.19) | collective-permute-done | bytes 55328 | tf_op jit(solution)/shard_map/ppermute | solution.py:300
  58.7 0.6 shard_map.99
  59.4 1.3 %collective-permute-start.20 = (bf16[12,576]{1,0:T(8,128)(2,1)S(1)}, bf16[12,576]{1,0:T(8,128)(2,1)S(1)}, u32[]{:S(2)}, u32[]{:S(2)}) collective-permute-start(bf16[12,576]{1,0:T(8,128)(2,1)S(1)} %get-tuple-element.56), channel_id=1, source_target_pairs={{0,32},{32,0},{1,33},{33,1},{2,34},{34,2},{3,35},{35,3},{4,36},{36... | collective-permute-start | bytes 41480 | tf_op jit(solution)/shard_map/ppermute | solution.py:300
  60.7 1.5 %collective-permute-start.21 = (bf16[12,576]{1,0:T(8,128)(2,1)S(1)}, bf16[12,576]{1,0:T(8,128)(2,1)S(1)}, u32[]{:S(2)}, u32[]{:S(2)}) collective-permute-start(bf16[12,576]{1,0:T(8,128)(2,1)S(1)} %get-tuple-element.57), channel_id=1, source_target_pairs={{0,4},{4,0},{8,12},{12,8},{16,20},{20,16},{24,28},{28,24},{1,5},{5... | collective-permute-start | bytes 41480 | tf_op jit(solution)/shard_map/ppermute | solution.py:300
  62.2 2.3 %collective-permute-start.22 = (bf16[12,576]{1,0:T(8,128)(2,1)S(1)}, bf16[12,576]{1,0:T(8,128)(2,1)S(1)}, u32[]{:S(2)}, u32[]{:S(2)}) collective-permute-start(bf16[12,576]{1,0:T(8,128)(2,1)S(1)} %get-tuple-element.58), channel_id=1, source_target_pairs={{0,36},{4,32},{8,44},{12,40},{16,52},{20,48},{24,60},{28,56},{32,4... | collective-permute-start | bytes 41480 | tf_op jit(solution)/shard_map/ppermute | solution.py:300
  64.4 8.1 %shard_map.96 = (bf16[128,768]{1,0:T(8,128)(2,1)}, bf16[128,768]{1,0:T(8,128)(2,1)}, bf16[128,768]{1,0:T(8,128)(2,1)}, bf16[128,768]{1,0:T(8,128)(2,1)}) custom-call(s32[4]{0:T(128)S(1)} %pad_add_fusion.ids, bf16[128,768]{1,0:T(8,128)(2,1)S(1)} %get-tuple-element.32.refs_0_, bf16[128,768]{1,0:T(8,128)(2,1)S(1)} %collective-permute-done.refs_1_, ...), custom_call_target="tpu_custom_call" | custom-call | flops 4000000000 | bytes 13860880 | tf_op jit(solution)/shard_map/pallas_call | solution.py:291
  72.5 0.7 shard_map.100
  (26 shorter events, 0.5 us)
Async XLA Ops:
  0.6 8.1 %collective-permute-start.4 = (bf16[128,768]{1,0:T(8,128)(2,1)}, bf16[128,768]{1,0:T(8,128)(2,1)S(1)}, u32[]{:S(2)}, u32[]{:S(2)}) collective-permute-start(bf16[128,768]{1,0:T(8,128)(2,1)} %bitcast.14), channel_id=1, source_target_pairs={{0,2},{2,0},{1,3},{3,1},{4,6},{6,4},{5,7},{7,5},{8,10},{10,8},{9,1... | collective-permute-start | bytes 589832 | tf_op jit(solution)/shard_map/ppermute | solution.py:300
  1.5 17.2 %collective-permute-start.3 = (bf16[128,768]{1,0:T(8,128)(2,1)}, bf16[128,768]{1,0:T(8,128)(2,1)S(1)}, u32[]{:S(2)}, u32[]{:S(2)}) collective-permute-start(bf16[128,768]{1,0:T(8,128)(2,1)} %bitcast.15), channel_id=1, source_target_pairs={{0,1},{1,0},{2,3},{3,2},{4,5},{5,4},{6,7},{7,6},{8,9},{9,8},{10,11... | collective-permute-start | bytes 589832 | tf_op jit(solution)/shard_map/ppermute | solution.py:300
  1.5 16.6 %collective-permute-start.1 = (bf16[128,768]{1,0:T(8,128)(2,1)}, bf16[128,768]{1,0:T(8,128)(2,1)S(1)}, u32[]{:S(2)}, u32[]{:S(2)}) collective-permute-start(bf16[128,768]{1,0:T(8,128)(2,1)} %bitcast.17), channel_id=1, source_target_pairs={{0,2},{2,0},{1,3},{3,1},{4,6},{6,4},{5,7},{7,5},{8,10},{10,8},{9,1... | collective-permute-start | bytes 589832 | tf_op jit(solution)/shard_map/ppermute | solution.py:300
  2.7 16.0 %collective-permute-start.7 = (bf16[128,768]{1,0:T(8,128)(2,1)}, bf16[128,768]{1,0:T(8,128)(2,1)S(1)}, u32[]{:S(2)}, u32[]{:S(2)}) collective-permute-start(bf16[128,768]{1,0:T(8,128)(2,1)} %bitcast.20), channel_id=1, source_target_pairs={{0,2},{2,0},{1,3},{3,1},{4,6},{6,4},{5,7},{7,5},{8,10},{10,8},{9,1... | collective-permute-start | bytes 589832 | tf_op jit(solution)/shard_map/ppermute | solution.py:300
  5.4 12.7 %collective-permute-start.10 = (bf16[128,384]{1,0:T(8,128)(2,1)S(1)}, bf16[128,384]{1,0:T(8,128)(2,1)S(1)}, u32[]{:S(2)}, u32[]{:S(2)}) collective-permute-start(bf16[128,384]{1,0:T(8,128)(2,1)S(1)} %get-tuple-element.38), channel_id=1, source_target_pairs={{0,2},{2,0},{1,3},{3,1},{4,6},{6,4},{5,7},{7,5},{8,10},{10,8},{9,1... | collective-permute-start | bytes 294920 | tf_op jit(solution)/shard_map/ppermute | solution.py:300
  8.7 10.4 %collective-permute-start.5 = (bf16[128,768]{1,0:T(8,128)(2,1)S(1)}, bf16[128,768]{1,0:T(8,128)(2,1)S(1)}, u32[]{:S(2)}, u32[]{:S(2)}) collective-permute-start(bf16[128,768]{1,0:T(8,128)(2,1)S(1)} %collective-permute-done.4.refs_2_), channel_id=1, source_target_pairs={{0,1},{1,0},{2,3},{3,2},{4,5},{5,4},{6,7},{7,6},{8,9},{9,8},{10,11... | collective-permute-start | bytes 589832 | tf_op jit(solution)/shard_map/ppermute | solution.py:300
  18.1 1.7 %collective-permute-start = (bf16[128,768]{1,0:T(8,128)(2,1)}, bf16[128,768]{1,0:T(8,128)(2,1)S(1)}, u32[]{:S(2)}, u32[]{:S(2)}) collective-permute-start(bf16[128,768]{1,0:T(8,128)(2,1)} %bitcast.19), channel_id=1, source_target_pairs={{0,1},{1,0},{2,3},{3,2},{4,5},{5,4},{6,7},{7,6},{8,9},{9,8},{10,11... | collective-permute-start | bytes 589832 | tf_op jit(solution)/shard_map/ppermute | solution.py:300
  18.1 1.9 %collective-permute-start.2 = (bf16[128,768]{1,0:T(8,128)(2,1)S(1)}, bf16[128,768]{1,0:T(8,128)(2,1)S(1)}, u32[]{:S(2)}, u32[]{:S(2)}) collective-permute-start(bf16[128,768]{1,0:T(8,128)(2,1)S(1)} %collective-permute-done.1.refs_2_), channel_id=1, source_target_pairs={{0,1},{1,0},{2,3},{3,2},{4,5},{5,4},{6,7},{7,6},{8,9},{9,8},{10,11... | collective-permute-start | bytes 589832 | tf_op jit(solution)/shard_map/ppermute | solution.py:300
  18.6 3.1 %collective-permute-start.6 = (bf16[128,768]{1,0:T(8,128)(2,1)}, bf16[128,768]{1,0:T(8,128)(2,1)S(1)}, u32[]{:S(2)}, u32[]{:S(2)}) collective-permute-start(bf16[128,768]{1,0:T(8,128)(2,1)} %bitcast.22), channel_id=1, source_target_pairs={{0,1},{1,0},{2,3},{3,2},{4,5},{5,4},{6,7},{7,6},{8,9},{9,8},{10,11... | collective-permute-start | bytes 589832 | tf_op jit(solution)/shard_map/ppermute | solution.py:300
  18.7 3.0 %collective-permute-start.8 = (bf16[128,768]{1,0:T(8,128)(2,1)S(1)}, bf16[128,768]{1,0:T(8,128)(2,1)S(1)}, u32[]{:S(2)}, u32[]{:S(2)}) collective-permute-start(bf16[128,768]{1,0:T(8,128)(2,1)S(1)} %collective-permute-done.7.refs_3_), channel_id=1, source_target_pairs={{0,1},{1,0},{2,3},{3,2},{4,5},{5,4},{6,7},{7,6},{8,9},{9,8},{10,11... | collective-permute-start | bytes 589832 | tf_op jit(solution)/shard_map/ppermute | solution.py:300
  19.1 4.5 %collective-permute-start.9 = (bf16[128,768]{1,0:T(8,128)(2,1)}, bf16[128,768]{1,0:T(8,128)(2,1)S(1)}, u32[]{:S(2)}, u32[]{:S(2)}) collective-permute-start(bf16[128,768]{1,0:T(8,128)(2,1)} %bitcast.24), channel_id=1, source_target_pairs={{0,1},{1,0},{2,3},{3,2},{4,5},{5,4},{6,7},{7,6},{8,9},{9,8},{10,11... | collective-permute-start | bytes 589832 | tf_op jit(solution)/shard_map/ppermute | solution.py:300
  19.8 3.8 %collective-permute-start.11 = (bf16[128,384]{1,0:T(8,128)(2,1)S(1)}, bf16[128,384]{1,0:T(8,128)(2,1)S(1)}, u32[]{:S(2)}, u32[]{:S(2)}) collective-permute-start(bf16[128,384]{1,0:T(8,128)(2,1)S(1)} %collective-permute-done.10.refs_8_.g_across), channel_id=1, source_target_pairs={{0,1},{1,0},{2,3},{3,2},{4,5},{5,4},{6,7},{7,6},{8,9},{9,8},{10,11... | collective-permute-start | bytes 294920 | tf_op jit(solution)/shard_map/ppermute | solution.py:300
  21.7 42.8 %copy-start = (bf16[768,3,768]{2,0,1:T(8,128)(2,1)S(1)}, bf16[768,3,768]{2,0,1:T(8,128)(2,1)}, u32[]{:S(2)}) copy-start(bf16[768,3,768]{2,0,1:T(8,128)(2,1)} %param.8) | copy-start | bytes 10616836
  25.6 9.4 %collective-permute-start.14 = (bf16[96,1152]{1,0:T(8,128)(2,1)S(1)}, bf16[96,1152]{1,0:T(8,128)(2,1)S(1)}, u32[]{:S(2)}, u32[]{:S(2)}) collective-permute-start(bf16[96,1152]{1,0:T(8,128)(2,1)S(1)} %get-tuple-element.48), channel_id=1, source_target_pairs={{0,64},{64,0},{128,192},{192,128},{1,65},{65,1},{129,193},{193,129... | collective-permute-start | bytes 663560 | tf_op jit(solution)/shard_map/ppermute | solution.py:300
  27.2 13.1 %collective-permute-start.15 = (bf16[96,1152]{1,0:T(8,128)(2,1)S(1)}, bf16[96,1152]{1,0:T(8,128)(2,1)S(1)}, u32[]{:S(2)}, u32[]{:S(2)}) collective-permute-start(bf16[96,1152]{1,0:T(8,128)(2,1)S(1)} %get-tuple-element.49), channel_id=1, source_target_pairs={{0,128},{64,192},{128,0},{192,64},{1,129},{65,193},{129,1},{193,65... | collective-permute-start | bytes 663560 | tf_op jit(solution)/shard_map/ppermute | solution.py:300
  29.9 13.0 %collective-permute-start.16 = (bf16[96,1152]{1,0:T(8,128)(2,1)S(1)}, bf16[96,1152]{1,0:T(8,128)(2,1)S(1)}, u32[]{:S(2)}, u32[]{:S(2)}) collective-permute-start(bf16[96,1152]{1,0:T(8,128)(2,1)S(1)} %get-tuple-element.50), channel_id=1, source_target_pairs={{0,192},{64,128},{128,64},{192,0},{1,193},{65,129},{129,65},{193,1... | collective-permute-start | bytes 663560 | tf_op jit(solution)/shard_map/ppermute | solution.py:300
  30.4 4.6 %collective-permute-start.12 = (bf16[128,384]{1,0:T(8,128)(2,1)S(1)}, bf16[128,384]{1,0:T(8,128)(2,1)S(1)}, u32[]{:S(2)}, u32[]{:S(2)}) collective-permute-start(bf16[128,384]{1,0:T(8,128)(2,1)S(1)} %get-tuple-element.39), channel_id=1, source_target_pairs={{0,2},{2,0},{1,3},{3,1},{4,6},{6,4},{5,7},{7,5},{8,10},{10,8},{9,1... | collective-permute-start | bytes 294920 | tf_op jit(solution)/shard_map/ppermute | solution.py:300
  35.0 29.4 %collective-permute-start.13 = (bf16[128,384]{1,0:T(8,128)(2,1)S(1)}, bf16[128,384]{1,0:T(8,128)(2,1)S(1)}, u32[]{:S(2)}, u32[]{:S(2)}) collective-permute-start(bf16[128,384]{1,0:T(8,128)(2,1)S(1)} %collective-permute-done.12.refs_10_), channel_id=1, source_target_pairs={{0,1},{1,0},{2,3},{3,2},{4,5},{5,4},{6,7},{7,6},{8,9},{9,8},{10,11... | collective-permute-start | bytes 294920 | tf_op jit(solution)/shard_map/ppermute | solution.py:300
  43.6 8.8 %collective-permute-start.17 = (bf16[24,1152]{1,0:T(8,128)(2,1)S(1)}, bf16[24,1152]{1,0:T(8,128)(2,1)S(1)}, u32[]{:S(2)}, u32[]{:S(2)}) collective-permute-start(bf16[24,1152]{1,0:T(8,128)(2,1)S(1)} %get-tuple-element.52), channel_id=1, source_target_pairs={{0,8},{4,12},{8,0},{12,4},{16,24},{20,28},{24,16},{28,20},{1,9},{5... | collective-permute-start | bytes 165896 | tf_op jit(solution)/shard_map/ppermute | solution.py:300
  47.0 8.2 %collective-permute-start.18 = (bf16[24,1152]{1,0:T(8,128)(2,1)S(1)}, bf16[24,1152]{1,0:T(8,128)(2,1)S(1)}, u32[]{:S(2)}, u32[]{:S(2)}) collective-permute-start(bf16[24,1152]{1,0:T(8,128)(2,1)S(1)} %get-tuple-element.53), channel_id=1, source_target_pairs={{0,16},{4,20},{8,24},{12,28},{16,0},{20,4},{24,8},{28,12},{1,17},{... | collective-permute-start | bytes 165896 | tf_op jit(solution)/shard_map/ppermute | solution.py:300
  52.3 6.4 %collective-permute-start.19 = (bf16[24,1152]{1,0:T(8,128)(2,1)S(1)}, bf16[24,1152]{1,0:T(8,128)(2,1)S(1)}, u32[]{:S(2)}, u32[]{:S(2)}) collective-permute-start(bf16[24,1152]{1,0:T(8,128)(2,1)S(1)} %get-tuple-element.54), channel_id=1, source_target_pairs={{0,24},{4,28},{8,16},{12,20},{16,8},{20,12},{24,0},{28,4},{1,25},{... | collective-permute-start | bytes 165896 | tf_op jit(solution)/shard_map/ppermute | solution.py:300
  59.4 13.2 %collective-permute-start.20 = (bf16[12,576]{1,0:T(8,128)(2,1)S(1)}, bf16[12,576]{1,0:T(8,128)(2,1)S(1)}, u32[]{:S(2)}, u32[]{:S(2)}) collective-permute-start(bf16[12,576]{1,0:T(8,128)(2,1)S(1)} %get-tuple-element.56), channel_id=1, source_target_pairs={{0,32},{32,0},{1,33},{33,1},{2,34},{34,2},{3,35},{35,3},{4,36},{36... | collective-permute-start | bytes 41480 | tf_op jit(solution)/shard_map/ppermute | solution.py:300
  60.7 11.8 %collective-permute-start.21 = (bf16[12,576]{1,0:T(8,128)(2,1)S(1)}, bf16[12,576]{1,0:T(8,128)(2,1)S(1)}, u32[]{:S(2)}, u32[]{:S(2)}) collective-permute-start(bf16[12,576]{1,0:T(8,128)(2,1)S(1)} %get-tuple-element.57), channel_id=1, source_target_pairs={{0,4},{4,0},{8,12},{12,8},{16,20},{20,16},{24,28},{28,24},{1,5},{5... | collective-permute-start | bytes 41480 | tf_op jit(solution)/shard_map/ppermute | solution.py:300
  62.2 10.3 %collective-permute-start.22 = (bf16[12,576]{1,0:T(8,128)(2,1)S(1)}, bf16[12,576]{1,0:T(8,128)(2,1)S(1)}, u32[]{:S(2)}, u32[]{:S(2)}) collective-permute-start(bf16[12,576]{1,0:T(8,128)(2,1)S(1)} %get-tuple-element.58), channel_id=1, source_target_pairs={{0,36},{4,32},{8,44},{12,40},{16,52},{20,48},{24,60},{28,56},{32,4... | collective-permute-start | bytes 41480 | tf_op jit(solution)/shard_map/ppermute | solution.py:300

commit v5 on v4

--- a/solution.py
+++ b/solution.py
@@ -167,14 +167,12 @@
         out[...] = jnp.concatenate([piece[:half], piece[half:]], axis=1).astype(BF16)
 
 
-def backward_kernel(ids, *refs):
-    q, km, vm = refs[0:4], refs[4], refs[5]
-    g_whole, g_need, g_rest = refs[6:8], refs[8:10], refs[10:12]
-    soft_ref, attended_ref, acted_ref, w_ref = refs[12:16]
-    conv_ref, dq_ref, dk_ref, dv_ref = refs[16:20]
-    qm, g_pad, ga_ref, do_ref, dp_ref, ds_ref = refs[20:]
+def grads_kernel(ids, *refs):
+    g_whole, g_need, g_rest = refs[0:2], refs[2:4], refs[4:6]
+    attended_ref, acted_ref, w_ref = refs[6:9]
+    conv_ref, do_ref = refs[9:11]
+    g_pad, ga_ref = refs[11:]
     me = ids[0]
-    inverse = 1.0 / math.sqrt(HEAD_DIM)
     own = pl.multiple_of(me * ROWS, ROWS)
     conv = jnp.zeros((ROWS, 768), F32)
     for t in range(TAPS):
@@ -184,7 +182,6 @@
     g_pad[0:STEP, :] = jnp.zeros((STEP, 768), BF16)
     g_pad[STEP + 512 :, :] = jnp.zeros((STEP, 768), BF16)
     for r in range(4):
-        at = slice(r * ROWS, (r + 1) * ROWS)
         start = pl.multiple_of(block_start(me, r) + STEP, STEP)
         if r < 2:
             g_pad[pl.ds(start, ROWS), :] = g_whole[r][...]
@@ -194,8 +191,6 @@
             rest = pl.ds(pl.multiple_of((1 - side) * 384, 128), 384)
             g_pad[pl.ds(start, ROWS), need] = g_need[r - 2][...]
             g_pad[pl.ds(start, ROWS), rest] = g_rest[r - 2][...]
-        for h in range(HEADS):
-            qm[h, at, :] = masked_window(window(q[r], h), h)
     ga_ref[...] = dot(g_pad[2 * STEP : 2 * STEP + 512, :], w_ref[0], NT)
     ga_ref[...] += dot(g_pad[STEP : STEP + 512, :], w_ref[1], NT)
     ga_ref[...] += dot(g_pad[0:512, :], w_ref[2], NT)
@@ -207,6 +202,17 @@
         grad = ga_ref[pl.ds(block_start(me, r), ROWS), :] * gelu_slope(normed)
         inner = jnp.mean(grad * normed, axis=1, keepdims=True)
         do_ref[at, :] = (factor * (grad - normed * inner)).astype(BF16)
+
+
+def backward_kernel(*refs):
+    q, km, vm, soft_ref, do_ref = refs[0:4], refs[4], refs[5], refs[6], refs[7]
+    dq_ref, dk_ref, dv_ref = refs[8:11]
+    qm, dp_ref, ds_ref = refs[11:]
+    inverse = 1.0 / math.sqrt(HEAD_DIM)
+    for r in range(4):
+        at = slice(r * ROWS, (r + 1) * ROWS)
+        for h in range(HEADS):
+            qm[h, at, :] = masked_window(window(q[r], h), h)
     dq, dk, dv = [], [], []
     for h in range(HEADS):
         grad_out = window(do_ref, h)
@@ -360,20 +366,25 @@
         500_000_000,
     )
     got = [pieces[0]] + [swap(pieces[n], "x", n) for n in range(1, x_size)]
-    conv_out, grad_queries, grad_keys, grad_values = call(
+    conv_out, grad_attended = call(
+        grads_kernel,
+        [shaped((ROWS, 768)), shaped((512, 768))],
+        [pltpu.VMEM((576, 768), BF16), pltpu.VMEM((512, 768), F32)],
+        [ids, *whole, *need, *rest, attended, acted, weight],
+        2_000_000_000,
+        20,
+    )
+    grad_queries, grad_keys, grad_values = call(
         backward_kernel,
-        [shaped((ROWS, 768)) for _ in range(4)],
+        [shaped((ROWS, 768)) for _ in range(3)],
         [
             pltpu.VMEM((HEADS, 512, 256), BF16),
-            pltpu.VMEM((576, 768), BF16),
-            pltpu.VMEM((512, 768), F32),
-            pltpu.VMEM((512, 768), BF16),
             pltpu.VMEM((512, 512), F32),
             pltpu.VMEM((512, 512), BF16),
         ],
-        [ids, *q, km, vm, *whole, *need, *rest, soft, attended, acted, weight],
-        4_000_000_000,
-        24,
+        [*q, km, vm, soft, grad_attended],
+        1_000_000_000,
+        20,
     )
     few = rows // 16
     pieces = call(

time: 73.4 us -> 70.3 us (0.958)
  the two profiles are of different devices: /device:TPU:24 before, /device:TPU:8 now
where the time goes in v5:
time: 70.3 us; the launch traced here: 70.2 us
  waiting for transfers between devices  27 us (38%)
  starting transfers between devices  25.4 us (36%)
  Pallas kernels  16.9 us (24%)
  between operations  0.76 us (1%)
    ppermute x23, waiting for transfers between devices, swap(): return lax.ppermute(value, axis, [(i, i ^ mask) for i in range(count)])  27 us
    ppermute x23, starting transfers between devices, swap(): return lax.ppermute(value, axis, [(i, i ^ mask) for i in range(count)])  25.4 us
    pallas_call x10, Pallas kernels, call(): return run(*args)  16.9 us
  transfers between devices with their start and end apart: 23, of which 9 were waited for; matrix products, arithmetic and copies ran while one was open for 0% of the time, Pallas kernels for 19%

profile of v5, /device:TPU:8, one launch (start us, length us, event | category | flops | bytes accessed | tf_op | source)
XLA Modules:
  0.0 70.2 jit_solution(10174526346042676575)
XLA Ops:
  0.6 2.2 %collective-permute-start.9 = (bf16[128,768]{1,0:T(8,128)(2,1)}, bf16[128,768]{1,0:T(8,128)(2,1)S(1)}, u32[]{:S(2)}, u32[]{:S(2)}) collective-permute-start(bf16[128,768]{1,0:T(8,128)(2,1)} %bitcast.14), channel_id=1, source_target_pairs={{0,2},{2,0},{1,3},{3,1},{4,6},{6,4},{5,7},{7,5},{8,10},{10,8},{9,1... | collective-permute-start | bytes 589832 | tf_op jit(solution)/shard_map/ppermute | solution.py:306
  2.9 0.2 collective-permute-start.6
  3.1 1.8 %collective-permute-start.12 = (bf16[128,768]{1,0:T(8,128)(2,1)}, bf16[128,768]{1,0:T(8,128)(2,1)S(1)}, u32[]{:S(2)}, u32[]{:S(2)}) collective-permute-start(bf16[128,768]{1,0:T(8,128)(2,1)} %bitcast.20), channel_id=1, source_target_pairs={{0,2},{2,0},{1,3},{3,1},{4,6},{6,4},{5,7},{7,5},{8,10},{10,8},{9,1... | collective-permute-start | bytes 589832 | tf_op jit(solution)/shard_map/ppermute | solution.py:306
  5.0 1.8 %shard_map.92 = (bf16[128,768]{1,0:T(8,128)(2,1)S(1)}, bf16[128,768]{1,0:T(8,128)(2,1)S(1)}, bf16[128,768]{1,0:T(8,128)(2,1)S(1)}, bf16[128,768]{1,0:T(8,128)(2,...) custom-call(s32[4]{0:T(128)S(1)} %pad_add_fusion.ids, bf16[128,768]{1,0:T(8,128)(2,1)} %bitcast.18, ...), custom_call_target="tpu_custom_call" | custom-call | flops 1000000 | bytes 1769488 | tf_op jit(solution)/shard_map/pallas_call | solution.py:297
  6.8 0.3 collective-permute-start.1
  7.1 1.8 %collective-permute-done.9.refs_2_ = bf16[128,768]{1,0:T(8,128)(2,1)S(1)} collective-permute-done((bf16[128,768]{1,0:T(8,128)(2,1)}, bf16[128,768]{1,0:T(8,128)(2,1)S(1)}, u32[]{:S(2)}, u32[]{:S(2)}) %collective-permute-start.9) | collective-permute-done | bytes 196640 | tf_op jit(solution)/shard_map/ppermute | solution.py:306
  8.8 9.3 %collective-permute-done.1.refs_2_.g_across = bf16[128,384]{1,0:T(8,128)(2,1)S(1)} collective-permute-done((bf16[128,384]{1,0:T(8,128)(2,1)S(1)}, bf16[128,384]{1,0:T(8,128)(2,1)S(1)}, u32[]{:S(2)}, u32[]{:S(2)}) %collective-permute-start.1) | collective-permute-done | bytes 98336 | tf_op jit(solution)/shard_map/ppermute | solution.py:306
  18.1 0.5 collective-permute-start.7
  18.7 0.4 collective-permute-start.13
  19.3 0.4 collective-permute-done.5.refs_1_
  20.0 1.6 %shard_map.94 = (f32[4,512,512]{2,1,0:T(8,128)S(1)}, bf16[4,512,512]{2,1,0:T(8,128)(2,1)S(1)}) custom-call(bf16[128,768]{1,0:T(8,128)(2,1)S(1)} %get-tuple-element.36.refs_0_, bf16[128,768]{1,0:T(8,128)(2,1)S(1)} %collective-permute-done.5.refs_1_, bf16[128,768]{1,0:T(8,128)(2,1)S(1)} %collective-permute-done.6.refs_2_, ...), custom_call_target="tpu_custom_call" | custom-call | flops 1000000000 | bytes 8126464 | tf_op jit(solution)/shard_map/pallas_call | solution.py:297
  21.7 1.9 %shard_map.95 = (bf16[512,768]{1,0:T(8,128)(2,1)S(1)}, bf16[576,768]{1,0:T(8,128)(2,1)S(1)}, bf16[4,512,256]{2,1,0:T(8,128)(2,1)S(1)}) custom-call(s32[4]{0:T(128)S(1)} %pad_add_fusion.ids, bf16[4,512,512]{2,1,0:T(8,128)(2,1)S(1)} %get-tuple-element.38.refs_0_, bf16[128,768]{1,0:T(8,128)(2,1)S(1)} %get-tuple-element.39.refs_1_, ...), custom_call_target="tpu_custom_call" | custom-call | flops 1000000000 | bytes 5603344 | tf_op jit(solution)/shard_map/pallas_call | solution.py:297
  23.6 2.0 %shard_map.98 = (bf16[96,1152]{1,0:T(8,128)(2,1)S(1)}, bf16[96,1152]{1,0:T(8,128)(2,1)S(1)}, bf16[96,1152]{1,0:T(8,128)(2,1)S(1)}, bf16[96,1152]{1,0:T(8,128)(2,1)S(1)}) custom-call(s32[4]{0:T(128)S(1)} %pad_add_fusion.ids, bf16[576,768]{1,0:T(8,128)(2,1)S(1)} %get-tuple-element.41.refs_7_.acted_ref, bf16[128,768]{1,0:T(8,128)(2,1)S(1)} %get-tuple-element.33.refs_0_.g_own, ...), custom_call_target="tpu_custom_call" | custom-call | flops 500000000 | bytes 2359312 | tf_op jit(solution)/shard_map/pallas_call | solution.py:297
  25.6 1.6 %collective-permute-start.14 = (bf16[96,1152]{1,0:T(8,128)(2,1)S(1)}, bf16[96,1152]{1,0:T(8,128)(2,1)S(1)}, u32[]{:S(2)}, u32[]{:S(2)}) collective-permute-start(bf16[96,1152]{1,0:T(8,128)(2,1)S(1)} %get-tuple-element.50), channel_id=1, source_target_pairs={{0,64},{64,0},{128,192},{192,128},{1,65},{65,1},{129,193},{193,129... | collective-permute-start | bytes 663560 | tf_op jit(solution)/shard_map/ppermute | solution.py:306
  27.2 2.7 %collective-permute-start.15 = (bf16[96,1152]{1,0:T(8,128)(2,1)S(1)}, bf16[96,1152]{1,0:T(8,128)(2,1)S(1)}, u32[]{:S(2)}, u32[]{:S(2)}) collective-permute-start(bf16[96,1152]{1,0:T(8,128)(2,1)S(1)} %get-tuple-element.51), channel_id=1, source_target_pairs={{0,128},{64,192},{128,0},{192,64},{1,129},{65,193},{129,1},{193,65... | collective-permute-start | bytes 663560 | tf_op jit(solution)/shard_map/ppermute | solution.py:306
  29.9 0.5 collective-permute-start.16
  30.4 1.0 %collective-permute-start.3 = (bf16[128,384]{1,0:T(8,128)(2,1)S(1)}, bf16[128,384]{1,0:T(8,128)(2,1)S(1)}, u32[]{:S(2)}, u32[]{:S(2)}) collective-permute-start(bf16[128,384]{1,0:T(8,128)(2,1)S(1)} %get-tuple-element.35), channel_id=1, source_target_pairs={{0,2},{2,0},{1,3},{3,1},{4,6},{6,4},{5,7},{7,5},{8,10},{10,8},{9,1... | collective-permute-start | bytes 294920 | tf_op jit(solution)/shard_map/ppermute | solution.py:306
  31.4 3.6 %collective-permute-done.3.refs_4_ = bf16[128,384]{1,0:T(8,128)(2,1)S(1)} collective-permute-done((bf16[128,384]{1,0:T(8,128)(2,1)S(1)}, bf16[128,384]{1,0:T(8,128)(2,1)S(1)}, u32[]{:S(2)}, u32[]{:S(2)}) %collective-permute-start.3) | collective-permute-done | bytes 98336 | tf_op jit(solution)/shard_map/ppermute | solution.py:306
  35.0 5.3 %collective-permute-done.15.refs_2_ = bf16[96,1152]{1,0:T(8,128)(2,1)S(1)} collective-permute-done((bf16[96,1152]{1,0:T(8,128)(2,1)S(1)}, bf16[96,1152]{1,0:T(8,128)(2,1)S(1)}, u32[]{:S(2)}, u32[]{:S(2)}) %collective-permute-start.15) | collective-permute-done | bytes 221216 | tf_op jit(solution)/shard_map/ppermute | solution.py:306
  40.3 2.6 %collective-permute-done.16.refs_3_ = bf16[96,1152]{1,0:T(8,128)(2,1)S(1)} collective-permute-done((bf16[96,1152]{1,0:T(8,128)(2,1)S(1)}, bf16[96,1152]{1,0:T(8,128)(2,1)S(1)}, u32[]{:S(2)}, u32[]{:S(2)}) %collective-permute-start.16) | collective-permute-done | bytes 221216 | tf_op jit(solution)/shard_map/ppermute | solution.py:306
  42.9 0.7 %shard_map.99 = (f32[24,1152]{1,0:T(8,128)S(1)}, bf16[24,1152]{1,0:T(8,128)(2,1)S(1)}, bf16[24,1152]{1,0:T(8,128)(2,1)S(1)}, bf16[24,1152]{1,0:T(8,128)(2,1)S(1)}) custom-call(s32[4]{0:T(128)S(1)} %pad_add_fusion.ids, bf16[96,1152]{1,0:T(8,128)(2,1)S(1)} %get-tuple-element.49.refs_0_, bf16[96,1152]{1,0:T(8,128)(2,1)S(1)} %collective-permute-done.14.refs_1_, ...), custom_call_target="tpu_custom_call" | custom-call | flops 1000000 | bytes 1161232 | tf_op jit(solution)/shard_map/pallas_call | solution.py:297
  43.6 3.4 %collective-permute-start.17 = (bf16[24,1152]{1,0:T(8,128)(2,1)S(1)}, bf16[24,1152]{1,0:T(8,128)(2,1)S(1)}, u32[]{:S(2)}, u32[]{:S(2)}) collective-permute-start(bf16[24,1152]{1,0:T(8,128)(2,1)S(1)} %get-tuple-element.54), channel_id=1, source_target_pairs={{0,8},{4,12},{8,0},{12,4},{16,24},{20,28},{24,16},{28,20},{1,9},{5... | collective-permute-start | bytes 165896 | tf_op jit(solution)/shard_map/ppermute | solution.py:306
  46.9 5.4 %collective-permute-start.18 = (bf16[24,1152]{1,0:T(8,128)(2,1)S(1)}, bf16[24,1152]{1,0:T(8,128)(2,1)S(1)}, u32[]{:S(2)}, u32[]{:S(2)}) collective-permute-start(bf16[24,1152]{1,0:T(8,128)(2,1)S(1)} %get-tuple-element.55), channel_id=1, source_target_pairs={{0,16},{4,20},{8,24},{12,28},{16,0},{20,4},{24,8},{28,12},{1,17},{... | collective-permute-start | bytes 165896 | tf_op jit(solution)/shard_map/ppermute | solution.py:306
  52.4 4.3 %shard_map.96 = (bf16[128,768]{1,0:T(8,128)(2,1)}, bf16[512,768]{1,0:T(8,128)(2,1)S(1)}) custom-call(s32[4]{0:T(128)S(1)} %pad_add_fusion.ids, bf16[128,768]{1,0:T(8,128)(2,1)S(1)} %get-tuple-element.33.refs_0_.g_own, bf16[128,768]{1,0:T(8,128)(2,1)S(1)} %collective-permute-done.refs_1_.g_core, bf16[128,384]{1,0:T(8,128)(2,1)S(1)} %collective-permute-done.1.refs_2_.g_across, ...), custom_call_target="tpu_custom_call" | custom-call | flops 2000000000 | bytes 6979600 | tf_op jit(solution)/shard_map/pallas_call | solution.py:297
  56.7 2.0 %collective-permute-done.19.refs_3_ = bf16[24,1152]{1,0:T(8,128)(2,1)S(1)} collective-permute-done((bf16[24,1152]{1,0:T(8,128)(2,1)S(1)}, bf16[24,1152]{1,0:T(8,128)(2,1)S(1)}, u32[]{:S(2)}, u32[]{:S(2)}) %collective-permute-start.19) | collective-permute-done | bytes 55328 | tf_op jit(solution)/shard_map/ppermute | solution.py:306
  58.7 0.6 shard_map.100
  59.4 2.4 %collective-permute-start.20 = (bf16[12,576]{1,0:T(8,128)(2,1)S(1)}, bf16[12,576]{1,0:T(8,128)(2,1)S(1)}, u32[]{:S(2)}, u32[]{:S(2)}) collective-permute-start(bf16[12,576]{1,0:T(8,128)(2,1)S(1)} %get-tuple-element.58), channel_id=1, source_target_pairs={{0,32},{32,0},{1,33},{33,1},{2,34},{34,2},{3,35},{35,3},{4,36},{36... | collective-permute-start | bytes 41480 | tf_op jit(solution)/shard_map/ppermute | solution.py:306
  61.7 1.5 %collective-permute-start.21 = (bf16[12,576]{1,0:T(8,128)(2,1)S(1)}, bf16[12,576]{1,0:T(8,128)(2,1)S(1)}, u32[]{:S(2)}, u32[]{:S(2)}) collective-permute-start(bf16[12,576]{1,0:T(8,128)(2,1)S(1)} %get-tuple-element.59), channel_id=1, source_target_pairs={{0,4},{4,0},{8,12},{12,8},{16,20},{20,16},{24,28},{28,24},{1,5},{5... | collective-permute-start | bytes 41480 | tf_op jit(solution)/shard_map/ppermute | solution.py:306
  63.2 1.2 %collective-permute-start.22 = (bf16[12,576]{1,0:T(8,128)(2,1)S(1)}, bf16[12,576]{1,0:T(8,128)(2,1)S(1)}, u32[]{:S(2)}, u32[]{:S(2)}) collective-permute-start(bf16[12,576]{1,0:T(8,128)(2,1)S(1)} %get-tuple-element.60), channel_id=1, source_target_pairs={{0,36},{4,32},{8,44},{12,40},{16,52},{20,48},{24,60},{28,56},{32,4... | collective-permute-start | bytes 41480 | tf_op jit(solution)/shard_map/ppermute | solution.py:306
  64.4 3.1 %shard_map.97 = (bf16[128,768]{1,0:T(8,128)(2,1)}, bf16[128,768]{1,0:T(8,128)(2,1)}, bf16[128,768]{1,0:T(8,128)(2,1)}) custom-call(bf16[128,768]{1,0:T(8,128)(2,1)S(1)} %get-tuple-element.36.refs_0_, bf16[128,768]{1,0:T(8,128)(2,1)S(1)} %collective-permute-done.5.refs_1_, bf16[128,768]{1,0:T(8,128)(2,1)S(1)} %collective-permute-done.6.refs_2_, ...), custom_call_target="tpu_custom_call" | custom-call | flops 1000000000 | bytes 8454144 | tf_op jit(solution)/shard_map/pallas_call | solution.py:297
  67.5 1.9 %collective-permute-done.22.refs_3_ = bf16[12,576]{1,0:T(8,128)(2,1)S(1)} collective-permute-done((bf16[12,576]{1,0:T(8,128)(2,1)S(1)}, bf16[12,576]{1,0:T(8,128)(2,1)S(1)}, u32[]{:S(2)}, u32[]{:S(2)}) %collective-permute-start.22) | collective-permute-done | bytes 13856 | tf_op jit(solution)/shard_map/ppermute | solution.py:306
  69.4 0.7 %shard_map.101 = f32[12,3,192]{2,1,0:T(4,128)} custom-call(f32[12,576]{1,0:T(8,128)S(1)} %get-tuple-element.57.refs_0_, bf16[12,576]{1,0:T(8,128)(2,1)S(1)} %collective-permute-done.20.refs_1_, bf16[12,576]{1,0:T(8,128)(2,1)S(1)} %collective-permute-done.21.refs_2_, bf16[12,576]{1,0:T(8,128)(2,1)S(1)} %collective-permute-done.22.refs_3_), custom_call_target="tpu_custom_call" | custom-call | flops 1000000 | bytes 96768 | tf_op jit(solution)/shard_map/pallas_call | solution.py:297
  (27 shorter events, 0.7 us)
Async XLA Ops:
  0.6 8.2 %collective-permute-start.9 = (bf16[128,768]{1,0:T(8,128)(2,1)}, bf16[128,768]{1,0:T(8,128)(2,1)S(1)}, u32[]{:S(2)}, u32[]{:S(2)}) collective-permute-start(bf16[128,768]{1,0:T(8,128)(2,1)} %bitcast.14), channel_id=1, source_target_pairs={{0,2},{2,0},{1,3},{3,1},{4,6},{6,4},{5,7},{7,5},{8,10},{10,8},{9,1... | collective-permute-start | bytes 589832 | tf_op jit(solution)/shard_map/ppermute | solution.py:306
  2.9 15.7 %collective-permute-start.8 = (bf16[128,768]{1,0:T(8,128)(2,1)}, bf16[128,768]{1,0:T(8,128)(2,1)S(1)}, u32[]{:S(2)}, u32[]{:S(2)}) collective-permute-start(bf16[128,768]{1,0:T(8,128)(2,1)} %bitcast.15), channel_id=1, source_target_pairs={{0,1},{1,0},{2,3},{3,2},{4,5},{5,4},{6,7},{7,6},{8,9},{9,8},{10,11... | collective-permute-start | bytes 589832 | tf_op jit(solution)/shard_map/ppermute | solution.py:306
  2.9 15.2 %collective-permute-start.6 = (bf16[128,768]{1,0:T(8,128)(2,1)}, bf16[128,768]{1,0:T(8,128)(2,1)S(1)}, u32[]{:S(2)}, u32[]{:S(2)}) collective-permute-start(bf16[128,768]{1,0:T(8,128)(2,1)} %bitcast.17), channel_id=1, source_target_pairs={{0,2},{2,0},{1,3},{3,1},{4,6},{6,4},{5,7},{7,5},{8,10},{10,8},{9,1... | collective-permute-start | bytes 589832 | tf_op jit(solution)/shard_map/ppermute | solution.py:306
  3.1 15.6 %collective-permute-start.12 = (bf16[128,768]{1,0:T(8,128)(2,1)}, bf16[128,768]{1,0:T(8,128)(2,1)S(1)}, u32[]{:S(2)}, u32[]{:S(2)}) collective-permute-start(bf16[128,768]{1,0:T(8,128)(2,1)} %bitcast.20), channel_id=1, source_target_pairs={{0,2},{2,0},{1,3},{3,1},{4,6},{6,4},{5,7},{7,5},{8,10},{10,8},{9,1... | collective-permute-start | bytes 589832 | tf_op jit(solution)/shard_map/ppermute | solution.py:306
  6.8 11.3 %collective-permute-start.1 = (bf16[128,384]{1,0:T(8,128)(2,1)S(1)}, bf16[128,384]{1,0:T(8,128)(2,1)S(1)}, u32[]{:S(2)}, u32[]{:S(2)}) collective-permute-start(bf16[128,384]{1,0:T(8,128)(2,1)S(1)} %get-tuple-element.34), channel_id=1, source_target_pairs={{0,2},{2,0},{1,3},{3,1},{4,6},{6,4},{5,7},{7,5},{8,10},{10,8},{9,1... | collective-permute-start | bytes 294920 | tf_op jit(solution)/shard_map/ppermute | solution.py:306
  8.8 10.3 %collective-permute-start.10 = (bf16[128,768]{1,0:T(8,128)(2,1)S(1)}, bf16[128,768]{1,0:T(8,128)(2,1)S(1)}, u32[]{:S(2)}, u32[]{:S(2)}) collective-permute-start(bf16[128,768]{1,0:T(8,128)(2,1)S(1)} %collective-permute-done.9.refs_2_), channel_id=1, source_target_pairs={{0,1},{1,0},{2,3},{3,2},{4,5},{5,4},{6,7},{7,6},{8,9},{9,8},{10,11... | collective-permute-start | bytes 589832 | tf_op jit(solution)/shard_map/ppermute | solution.py:306
  18.1 1.7 %collective-permute-start.5 = (bf16[128,768]{1,0:T(8,128)(2,1)}, bf16[128,768]{1,0:T(8,128)(2,1)S(1)}, u32[]{:S(2)}, u32[]{:S(2)}) collective-permute-start(bf16[128,768]{1,0:T(8,128)(2,1)} %bitcast.19), channel_id=1, source_target_pairs={{0,1},{1,0},{2,3},{3,2},{4,5},{5,4},{6,7},{7,6},{8,9},{9,8},{10,11... | collective-permute-start | bytes 589832 | tf_op jit(solution)/shard_map/ppermute | solution.py:306
  18.1 1.9 %collective-permute-start.7 = (bf16[128,768]{1,0:T(8,128)(2,1)S(1)}, bf16[128,768]{1,0:T(8,128)(2,1)S(1)}, u32[]{:S(2)}, u32[]{:S(2)}) collective-permute-start(bf16[128,768]{1,0:T(8,128)(2,1)S(1)} %collective-permute-done.6.refs_2_), channel_id=1, source_target_pairs={{0,1},{1,0},{2,3},{3,2},{4,5},{5,4},{6,7},{7,6},{8,9},{9,8},{10,11... | collective-permute-start | bytes 589832 | tf_op jit(solution)/shard_map/ppermute | solution.py:306
  18.6 3.1 %collective-permute-start.11 = (bf16[128,768]{1,0:T(8,128)(2,1)}, bf16[128,768]{1,0:T(8,128)(2,1)S(1)}, u32[]{:S(2)}, u32[]{:S(2)}) collective-permute-start(bf16[128,768]{1,0:T(8,128)(2,1)} %bitcast.22), channel_id=1, source_target_pairs={{0,1},{1,0},{2,3},{3,2},{4,5},{5,4},{6,7},{7,6},{8,9},{9,8},{10,11... | collective-permute-start | bytes 589832 | tf_op jit(solution)/shard_map/ppermute | solution.py:306
  18.7 3.0 %collective-permute-start.13 = (bf16[128,768]{1,0:T(8,128)(2,1)S(1)}, bf16[128,768]{1,0:T(8,128)(2,1)S(1)}, u32[]{:S(2)}, u32[]{:S(2)}) collective-permute-start(bf16[128,768]{1,0:T(8,128)(2,1)S(1)} %collective-permute-done.12.refs_3_), channel_id=1, source_target_pairs={{0,1},{1,0},{2,3},{3,2},{4,5},{5,4},{6,7},{7,6},{8,9},{9,8},{10,11... | collective-permute-start | bytes 589832 | tf_op jit(solution)/shard_map/ppermute | solution.py:306
  19.1 4.5 %collective-permute-start = (bf16[128,768]{1,0:T(8,128)(2,1)}, bf16[128,768]{1,0:T(8,128)(2,1)S(1)}, u32[]{:S(2)}, u32[]{:S(2)}) collective-permute-start(bf16[128,768]{1,0:T(8,128)(2,1)} %bitcast.24), channel_id=1, source_target_pairs={{0,1},{1,0},{2,3},{3,2},{4,5},{5,4},{6,7},{7,6},{8,9},{9,8},{10,11... | collective-permute-start | bytes 589832 | tf_op jit(solution)/shard_map/ppermute | solution.py:306
  19.8 3.8 %collective-permute-start.2 = (bf16[128,384]{1,0:T(8,128)(2,1)S(1)}, bf16[128,384]{1,0:T(8,128)(2,1)S(1)}, u32[]{:S(2)}, u32[]{:S(2)}) collective-permute-start(bf16[128,384]{1,0:T(8,128)(2,1)S(1)} %collective-permute-done.1.refs_2_.g_across), channel_id=1, source_target_pairs={{0,1},{1,0},{2,3},{3,2},{4,5},{5,4},{6,7},{7,6},{8,9},{9,8},{10,11... | collective-permute-start | bytes 294920 | tf_op jit(solution)/shard_map/ppermute | solution.py:306
  21.7 30.7 %copy-start = (bf16[768,3,768]{2,0,1:T(8,128)(2,1)S(1)}, bf16[768,3,768]{2,0,1:T(8,128)(2,1)}, u32[]{:S(2)}) copy-start(bf16[768,3,768]{2,0,1:T(8,128)(2,1)} %param.8) | copy-start | bytes 10616836
  25.6 9.4 %collective-permute-start.14 = (bf16[96,1152]{1,0:T(8,128)(2,1)S(1)}, bf16[96,1152]{1,0:T(8,128)(2,1)S(1)}, u32[]{:S(2)}, u32[]{:S(2)}) collective-permute-start(bf16[96,1152]{1,0:T(8,128)(2,1)S(1)} %get-tuple-element.50), channel_id=1, source_target_pairs={{0,64},{64,0},{128,192},{192,128},{1,65},{65,1},{129,193},{193,129... | collective-permute-start | bytes 663560 | tf_op jit(solution)/shard_map/ppermute | solution.py:306
  27.2 13.1 %collective-permute-start.15 = (bf16[96,1152]{1,0:T(8,128)(2,1)S(1)}, bf16[96,1152]{1,0:T(8,128)(2,1)S(1)}, u32[]{:S(2)}, u32[]{:S(2)}) collective-permute-start(bf16[96,1152]{1,0:T(8,128)(2,1)S(1)} %get-tuple-element.51), channel_id=1, source_target_pairs={{0,128},{64,192},{128,0},{192,64},{1,129},{65,193},{129,1},{193,65... | collective-permute-start | bytes 663560 | tf_op jit(solution)/shard_map/ppermute | solution.py:306
  29.9 13.0 %collective-permute-start.16 = (bf16[96,1152]{1,0:T(8,128)(2,1)S(1)}, bf16[96,1152]{1,0:T(8,128)(2,1)S(1)}, u32[]{:S(2)}, u32[]{:S(2)}) collective-permute-start(bf16[96,1152]{1,0:T(8,128)(2,1)S(1)} %get-tuple-element.52), channel_id=1, source_target_pairs={{0,192},{64,128},{128,64},{192,0},{1,193},{65,129},{129,65},{193,1... | collective-permute-start | bytes 663560 | tf_op jit(solution)/shard_map/ppermute | solution.py:306
  30.4 4.6 %collective-permute-start.3 = (bf16[128,384]{1,0:T(8,128)(2,1)S(1)}, bf16[128,384]{1,0:T(8,128)(2,1)S(1)}, u32[]{:S(2)}, u32[]{:S(2)}) collective-permute-start(bf16[128,384]{1,0:T(8,128)(2,1)S(1)} %get-tuple-element.35), channel_id=1, source_target_pairs={{0,2},{2,0},{1,3},{3,1},{4,6},{6,4},{5,7},{7,5},{8,10},{10,8},{9,1... | collective-permute-start | bytes 294920 | tf_op jit(solution)/shard_map/ppermute | solution.py:306
  35.0 17.3 %collective-permute-start.4 = (bf16[128,384]{1,0:T(8,128)(2,1)S(1)}, bf16[128,384]{1,0:T(8,128)(2,1)S(1)}, u32[]{:S(2)}, u32[]{:S(2)}) collective-permute-start(bf16[128,384]{1,0:T(8,128)(2,1)S(1)} %collective-permute-done.3.refs_4_), channel_id=1, source_target_pairs={{0,1},{1,0},{2,3},{3,2},{4,5},{5,4},{6,7},{7,6},{8,9},{9,8},{10,11... | collective-permute-start | bytes 294920 | tf_op jit(solution)/shard_map/ppermute | solution.py:306
  43.6 13.1 %collective-permute-start.17 = (bf16[24,1152]{1,0:T(8,128)(2,1)S(1)}, bf16[24,1152]{1,0:T(8,128)(2,1)S(1)}, u32[]{:S(2)}, u32[]{:S(2)}) collective-permute-start(bf16[24,1152]{1,0:T(8,128)(2,1)S(1)} %get-tuple-element.54), channel_id=1, source_target_pairs={{0,8},{4,12},{8,0},{12,4},{16,24},{20,28},{24,16},{28,20},{1,9},{5... | collective-permute-start | bytes 165896 | tf_op jit(solution)/shard_map/ppermute | solution.py:306
  46.9 9.8 %collective-permute-start.18 = (bf16[24,1152]{1,0:T(8,128)(2,1)S(1)}, bf16[24,1152]{1,0:T(8,128)(2,1)S(1)}, u32[]{:S(2)}, u32[]{:S(2)}) collective-permute-start(bf16[24,1152]{1,0:T(8,128)(2,1)S(1)} %get-tuple-element.55), channel_id=1, source_target_pairs={{0,16},{4,20},{8,24},{12,28},{16,0},{20,4},{24,8},{28,12},{1,17},{... | collective-permute-start | bytes 165896 | tf_op jit(solution)/shard_map/ppermute | solution.py:306
  52.3 6.4 %collective-permute-start.19 = (bf16[24,1152]{1,0:T(8,128)(2,1)S(1)}, bf16[24,1152]{1,0:T(8,128)(2,1)S(1)}, u32[]{:S(2)}, u32[]{:S(2)}) collective-permute-start(bf16[24,1152]{1,0:T(8,128)(2,1)S(1)} %get-tuple-element.56), channel_id=1, source_target_pairs={{0,24},{4,28},{8,16},{12,20},{16,8},{20,12},{24,0},{28,4},{1,25},{... | collective-permute-start | bytes 165896 | tf_op jit(solution)/shard_map/ppermute | solution.py:306
  59.4 8.2 %collective-permute-start.20 = (bf16[12,576]{1,0:T(8,128)(2,1)S(1)}, bf16[12,576]{1,0:T(8,128)(2,1)S(1)}, u32[]{:S(2)}, u32[]{:S(2)}) collective-permute-start(bf16[12,576]{1,0:T(8,128)(2,1)S(1)} %get-tuple-element.58), channel_id=1, source_target_pairs={{0,32},{32,0},{1,33},{33,1},{2,34},{34,2},{3,35},{35,3},{4,36},{36... | collective-permute-start | bytes 41480 | tf_op jit(solution)/shard_map/ppermute | solution.py:306
  61.7 5.8 %collective-permute-start.21 = (bf16[12,576]{1,0:T(8,128)(2,1)S(1)}, bf16[12,576]{1,0:T(8,128)(2,1)S(1)}, u32[]{:S(2)}, u32[]{:S(2)}) collective-permute-start(bf16[12,576]{1,0:T(8,128)(2,1)S(1)} %get-tuple-element.59), channel_id=1, source_target_pairs={{0,4},{4,0},{8,12},{12,8},{16,20},{20,16},{24,28},{28,24},{1,5},{5... | collective-permute-start | bytes 41480 | tf_op jit(solution)/shard_map/ppermute | solution.py:306
  63.2 6.2 %collective-permute-start.22 = (bf16[12,576]{1,0:T(8,128)(2,1)S(1)}, bf16[12,576]{1,0:T(8,128)(2,1)S(1)}, u32[]{:S(2)}, u32[]{:S(2)}) collective-permute-start(bf16[12,576]{1,0:T(8,128)(2,1)S(1)} %get-tuple-element.60), channel_id=1, source_target_pairs={{0,36},{4,32},{8,44},{12,40},{16,52},{20,48},{24,60},{28,56},{32,4... | collective-permute-start | bytes 41480 | tf_op jit(solution)/shard_map/ppermute | solution.py:306

commit v6 on v5

--- a/solution.py
+++ b/solution.py
@@ -161,10 +161,10 @@
     rows = 768 // parts
     half = rows // 2
     for j in range(parts):
-        total[j] = result[j * rows : (j + 1) * rows]
+        piece = result[j * rows : (j + 1) * rows]
+        total[j] = jnp.concatenate([piece[:half], piece[half:]], axis=1).astype(BF16)
     for n, out in enumerate(outs):
-        piece = total[jnp.bitwise_xor(mx, n)]
-        out[...] = jnp.concatenate([piece[:half], piece[half:]], axis=1).astype(BF16)
+        out[...] = total[jnp.bitwise_xor(mx, n)]
 
 
 def grads_kernel(ids, *refs):
@@ -360,7 +360,7 @@
         [
             pltpu.VMEM((576, HEAD_DIM), BF16),
             pltpu.VMEM((512, 576), BF16),
-            pltpu.VMEM((x_size, rows, 576), F32),
+            pltpu.VMEM((x_size, rows // 2, 1152), BF16),
         ],
         [ids, acted, *whole, *need],
         500_000_000,

time: 70.3 us -> 70.2 us (level)
  no operation moved by 1% of the time
where the time goes in v6:
time: 70.2 us; the launch traced here: 70.1 us
  waiting for transfers between devices  27 us (38%)
  starting transfers between devices  25.4 us (36%)
  Pallas kernels  16.8 us (24%)
  between operations  0.76 us (1%)
    ppermute x23, waiting for transfers between devices, swap(): return lax.ppermute(value, axis, [(i, i ^ mask) for i in range(count)])  27 us
    ppermute x23, starting transfers between devices, swap(): return lax.ppermute(value, axis, [(i, i ^ mask) for i in range(count)])  25.4 us
    pallas_call x10, Pallas kernels, call(): return run(*args)  16.8 us
  transfers between devices with their start and end apart: 23, of which 9 were waited for; matrix products, arithmetic and copies ran while one was open for 0% of the time, Pallas kernels for 19%

profile of v6, /device:TPU:8, one launch (start us, length us, event | category | flops | bytes accessed | tf_op | source)
XLA Modules:
  0.0 70.1 jit_solution(13225492288937385384)
XLA Ops:
  0.6 2.2 %collective-permute-start.9 = (bf16[128,768]{1,0:T(8,128)(2,1)}, bf16[128,768]{1,0:T(8,128)(2,1)S(1)}, u32[]{:S(2)}, u32[]{:S(2)}) collective-permute-start(bf16[128,768]{1,0:T(8,128)(2,1)} %bitcast.14), channel_id=1, source_target_pairs={{0,2},{2,0},{1,3},{3,1},{4,6},{6,4},{5,7},{7,5},{8,10},{10,8},{9,1... | collective-permute-start | bytes 589832 | tf_op jit(solution)/shard_map/ppermute | solution.py:306
  2.9 0.2 collective-permute-start.6
  3.1 1.8 %collective-permute-start.12 = (bf16[128,768]{1,0:T(8,128)(2,1)}, bf16[128,768]{1,0:T(8,128)(2,1)S(1)}, u32[]{:S(2)}, u32[]{:S(2)}) collective-permute-start(bf16[128,768]{1,0:T(8,128)(2,1)} %bitcast.20), channel_id=1, source_target_pairs={{0,2},{2,0},{1,3},{3,1},{4,6},{6,4},{5,7},{7,5},{8,10},{10,8},{9,1... | collective-permute-start | bytes 589832 | tf_op jit(solution)/shard_map/ppermute | solution.py:306
  5.0 1.8 %shard_map.92 = (bf16[128,768]{1,0:T(8,128)(2,1)S(1)}, bf16[128,768]{1,0:T(8,128)(2,1)S(1)}, bf16[128,768]{1,0:T(8,128)(2,1)S(1)}, bf16[128,768]{1,0:T(8,128)(2,...) custom-call(s32[4]{0:T(128)S(1)} %pad_add_fusion.ids, bf16[128,768]{1,0:T(8,128)(2,1)} %bitcast.18, ...), custom_call_target="tpu_custom_call" | custom-call | flops 1000000 | bytes 1769488 | tf_op jit(solution)/shard_map/pallas_call | solution.py:297
  6.8 0.3 collective-permute-start.1
  7.1 1.8 %collective-permute-done.9.refs_2_ = bf16[128,768]{1,0:T(8,128)(2,1)S(1)} collective-permute-done((bf16[128,768]{1,0:T(8,128)(2,1)}, bf16[128,768]{1,0:T(8,128)(2,1)S(1)}, u32[]{:S(2)}, u32[]{:S(2)}) %collective-permute-start.9) | collective-permute-done | bytes 196640 | tf_op jit(solution)/shard_map/ppermute | solution.py:306
  8.8 9.3 %collective-permute-done.1.refs_2_.g_across = bf16[128,384]{1,0:T(8,128)(2,1)S(1)} collective-permute-done((bf16[128,384]{1,0:T(8,128)(2,1)S(1)}, bf16[128,384]{1,0:T(8,128)(2,1)S(1)}, u32[]{:S(2)}, u32[]{:S(2)}) %collective-permute-start.1) | collective-permute-done | bytes 98336 | tf_op jit(solution)/shard_map/ppermute | solution.py:306
  18.1 0.5 collective-permute-start.7
  18.7 0.4 collective-permute-start.13
  19.3 0.4 collective-permute-done.5.refs_1_
  20.0 1.6 %shard_map.94 = (f32[4,512,512]{2,1,0:T(8,128)S(1)}, bf16[4,512,512]{2,1,0:T(8,128)(2,1)S(1)}) custom-call(bf16[128,768]{1,0:T(8,128)(2,1)S(1)} %get-tuple-element.36.refs_0_, bf16[128,768]{1,0:T(8,128)(2,1)S(1)} %collective-permute-done.5.refs_1_, bf16[128,768]{1,0:T(8,128)(2,1)S(1)} %collective-permute-done.6.refs_2_, ...), custom_call_target="tpu_custom_call" | custom-call | flops 1000000000 | bytes 8126464 | tf_op jit(solution)/shard_map/pallas_call | solution.py:297
  21.7 1.9 %shard_map.95 = (bf16[512,768]{1,0:T(8,128)(2,1)S(1)}, bf16[576,768]{1,0:T(8,128)(2,1)S(1)}, bf16[4,512,256]{2,1,0:T(8,128)(2,1)S(1)}) custom-call(s32[4]{0:T(128)S(1)} %pad_add_fusion.ids, bf16[4,512,512]{2,1,0:T(8,128)(2,1)S(1)} %get-tuple-element.38.refs_0_, bf16[128,768]{1,0:T(8,128)(2,1)S(1)} %get-tuple-element.39.refs_1_, ...), custom_call_target="tpu_custom_call" | custom-call | flops 1000000000 | bytes 5603344 | tf_op jit(solution)/shard_map/pallas_call | solution.py:297
  23.6 1.9 %shard_map.98 = (bf16[96,1152]{1,0:T(8,128)(2,1)S(1)}, bf16[96,1152]{1,0:T(8,128)(2,1)S(1)}, bf16[96,1152]{1,0:T(8,128)(2,1)S(1)}, bf16[96,1152]{1,0:T(8,128)(2,1)S(1)}) custom-call(s32[4]{0:T(128)S(1)} %pad_add_fusion.ids, bf16[576,768]{1,0:T(8,128)(2,1)S(1)} %get-tuple-element.41.refs_7_.acted_ref, bf16[128,768]{1,0:T(8,128)(2,1)S(1)} %get-tuple-element.33.refs_0_.g_own, ...), custom_call_target="tpu_custom_call" | custom-call | flops 500000000 | bytes 2359312 | tf_op jit(solution)/shard_map/pallas_call | solution.py:297
  25.5 1.6 %collective-permute-start.14 = (bf16[96,1152]{1,0:T(8,128)(2,1)S(1)}, bf16[96,1152]{1,0:T(8,128)(2,1)S(1)}, u32[]{:S(2)}, u32[]{:S(2)}) collective-permute-start(bf16[96,1152]{1,0:T(8,128)(2,1)S(1)} %get-tuple-element.50), channel_id=1, source_target_pairs={{0,64},{64,0},{128,192},{192,128},{1,65},{65,1},{129,193},{193,129... | collective-permute-start | bytes 663560 | tf_op jit(solution)/shard_map/ppermute | solution.py:306
  27.1 2.7 %collective-permute-start.15 = (bf16[96,1152]{1,0:T(8,128)(2,1)S(1)}, bf16[96,1152]{1,0:T(8,128)(2,1)S(1)}, u32[]{:S(2)}, u32[]{:S(2)}) collective-permute-start(bf16[96,1152]{1,0:T(8,128)(2,1)S(1)} %get-tuple-element.51), channel_id=1, source_target_pairs={{0,128},{64,192},{128,0},{192,64},{1,129},{65,193},{129,1},{193,65... | collective-permute-start | bytes 663560 | tf_op jit(solution)/shard_map/ppermute | solution.py:306
  29.8 0.5 collective-permute-start.16
  30.3 1.0 %collective-permute-start.3 = (bf16[128,384]{1,0:T(8,128)(2,1)S(1)}, bf16[128,384]{1,0:T(8,128)(2,1)S(1)}, u32[]{:S(2)}, u32[]{:S(2)}) collective-permute-start(bf16[128,384]{1,0:T(8,128)(2,1)S(1)} %get-tuple-element.35), channel_id=1, source_target_pairs={{0,2},{2,0},{1,3},{3,1},{4,6},{6,4},{5,7},{7,5},{8,10},{10,8},{9,1... | collective-permute-start | bytes 294920 | tf_op jit(solution)/shard_map/ppermute | solution.py:306
  31.3 3.6 %collective-permute-done.3.refs_4_ = bf16[128,384]{1,0:T(8,128)(2,1)S(1)} collective-permute-done((bf16[128,384]{1,0:T(8,128)(2,1)S(1)}, bf16[128,384]{1,0:T(8,128)(2,1)S(1)}, u32[]{:S(2)}, u32[]{:S(2)}) %collective-permute-start.3) | collective-permute-done | bytes 98336 | tf_op jit(solution)/shard_map/ppermute | solution.py:306
  34.9 5.3 %collective-permute-done.15.refs_2_ = bf16[96,1152]{1,0:T(8,128)(2,1)S(1)} collective-permute-done((bf16[96,1152]{1,0:T(8,128)(2,1)S(1)}, bf16[96,1152]{1,0:T(8,128)(2,1)S(1)}, u32[]{:S(2)}, u32[]{:S(2)}) %collective-permute-start.15) | collective-permute-done | bytes 221216 | tf_op jit(solution)/shard_map/ppermute | solution.py:306
  40.2 2.6 %collective-permute-done.16.refs_3_ = bf16[96,1152]{1,0:T(8,128)(2,1)S(1)} collective-permute-done((bf16[96,1152]{1,0:T(8,128)(2,1)S(1)}, bf16[96,1152]{1,0:T(8,128)(2,1)S(1)}, u32[]{:S(2)}, u32[]{:S(2)}) %collective-permute-start.16) | collective-permute-done | bytes 221216 | tf_op jit(solution)/shard_map/ppermute | solution.py:306
  42.8 0.7 %shard_map.99 = (f32[24,1152]{1,0:T(8,128)S(1)}, bf16[24,1152]{1,0:T(8,128)(2,1)S(1)}, bf16[24,1152]{1,0:T(8,128)(2,1)S(1)}, bf16[24,1152]{1,0:T(8,128)(2,1)S(1)}) custom-call(s32[4]{0:T(128)S(1)} %pad_add_fusion.ids, bf16[96,1152]{1,0:T(8,128)(2,1)S(1)} %get-tuple-element.49.refs_0_, bf16[96,1152]{1,0:T(8,128)(2,1)S(1)} %collective-permute-done.14.refs_1_, ...), custom_call_target="tpu_custom_call" | custom-call | flops 1000000 | bytes 1161232 | tf_op jit(solution)/shard_map/pallas_call | solution.py:297
  43.5 3.4 %collective-permute-start.17 = (bf16[24,1152]{1,0:T(8,128)(2,1)S(1)}, bf16[24,1152]{1,0:T(8,128)(2,1)S(1)}, u32[]{:S(2)}, u32[]{:S(2)}) collective-permute-start(bf16[24,1152]{1,0:T(8,128)(2,1)S(1)} %get-tuple-element.54), channel_id=1, source_target_pairs={{0,8},{4,12},{8,0},{12,4},{16,24},{20,28},{24,16},{28,20},{1,9},{5... | collective-permute-start | bytes 165896 | tf_op jit(solution)/shard_map/ppermute | solution.py:306
  46.9 5.4 %collective-permute-start.18 = (bf16[24,1152]{1,0:T(8,128)(2,1)S(1)}, bf16[24,1152]{1,0:T(8,128)(2,1)S(1)}, u32[]{:S(2)}, u32[]{:S(2)}) collective-permute-start(bf16[24,1152]{1,0:T(8,128)(2,1)S(1)} %get-tuple-element.55), channel_id=1, source_target_pairs={{0,16},{4,20},{8,24},{12,28},{16,0},{20,4},{24,8},{28,12},{1,17},{... | collective-permute-start | bytes 165896 | tf_op jit(solution)/shard_map/ppermute | solution.py:306
  52.3 4.4 %shard_map.96 = (bf16[128,768]{1,0:T(8,128)(2,1)}, bf16[512,768]{1,0:T(8,128)(2,1)S(1)}) custom-call(s32[4]{0:T(128)S(1)} %pad_add_fusion.ids, bf16[128,768]{1,0:T(8,128)(2,1)S(1)} %get-tuple-element.33.refs_0_.g_own, bf16[128,768]{1,0:T(8,128)(2,1)S(1)} %collective-permute-done.refs_1_.g_core, bf16[128,384]{1,0:T(8,128)(2,1)S(1)} %collective-permute-done.1.refs_2_.g_across, ...), custom_call_target="tpu_custom_call" | custom-call | flops 2000000000 | bytes 6979600 | tf_op jit(solution)/shard_map/pallas_call | solution.py:297
  56.7 2.0 %collective-permute-done.19.refs_3_ = bf16[24,1152]{1,0:T(8,128)(2,1)S(1)} collective-permute-done((bf16[24,1152]{1,0:T(8,128)(2,1)S(1)}, bf16[24,1152]{1,0:T(8,128)(2,1)S(1)}, u32[]{:S(2)}, u32[]{:S(2)}) %collective-permute-start.19) | collective-permute-done | bytes 55328 | tf_op jit(solution)/shard_map/ppermute | solution.py:306
  58.6 0.6 shard_map.100
  59.3 2.4 %collective-permute-start.20 = (bf16[12,576]{1,0:T(8,128)(2,1)S(1)}, bf16[12,576]{1,0:T(8,128)(2,1)S(1)}, u32[]{:S(2)}, u32[]{:S(2)}) collective-permute-start(bf16[12,576]{1,0:T(8,128)(2,1)S(1)} %get-tuple-element.58), channel_id=1, source_target_pairs={{0,32},{32,0},{1,33},{33,1},{2,34},{34,2},{3,35},{35,3},{4,36},{36... | collective-permute-start | bytes 41480 | tf_op jit(solution)/shard_map/ppermute | solution.py:306
  61.7 1.5 %collective-permute-start.21 = (bf16[12,576]{1,0:T(8,128)(2,1)S(1)}, bf16[12,576]{1,0:T(8,128)(2,1)S(1)}, u32[]{:S(2)}, u32[]{:S(2)}) collective-permute-start(bf16[12,576]{1,0:T(8,128)(2,1)S(1)} %get-tuple-element.59), channel_id=1, source_target_pairs={{0,4},{4,0},{8,12},{12,8},{16,20},{20,16},{24,28},{28,24},{1,5},{5... | collective-permute-start | bytes 41480 | tf_op jit(solution)/shard_map/ppermute | solution.py:306
  63.2 1.2 %collective-permute-start.22 = (bf16[12,576]{1,0:T(8,128)(2,1)S(1)}, bf16[12,576]{1,0:T(8,128)(2,1)S(1)}, u32[]{:S(2)}, u32[]{:S(2)}) collective-permute-start(bf16[12,576]{1,0:T(8,128)(2,1)S(1)} %get-tuple-element.60), channel_id=1, source_target_pairs={{0,36},{4,32},{8,44},{12,40},{16,52},{20,48},{24,60},{28,56},{32,4... | collective-permute-start | bytes 41480 | tf_op jit(solution)/shard_map/ppermute | solution.py:306
  64.4 3.1 %shard_map.97 = (bf16[128,768]{1,0:T(8,128)(2,1)}, bf16[128,768]{1,0:T(8,128)(2,1)}, bf16[128,768]{1,0:T(8,128)(2,1)}) custom-call(bf16[128,768]{1,0:T(8,128)(2,1)S(1)} %get-tuple-element.36.refs_0_, bf16[128,768]{1,0:T(8,128)(2,1)S(1)} %collective-permute-done.5.refs_1_, bf16[128,768]{1,0:T(8,128)(2,1)S(1)} %collective-permute-done.6.refs_2_, ...), custom_call_target="tpu_custom_call" | custom-call | flops 1000000000 | bytes 8454144 | tf_op jit(solution)/shard_map/pallas_call | solution.py:297
  67.5 1.9 %collective-permute-done.22.refs_3_ = bf16[12,576]{1,0:T(8,128)(2,1)S(1)} collective-permute-done((bf16[12,576]{1,0:T(8,128)(2,1)S(1)}, bf16[12,576]{1,0:T(8,128)(2,1)S(1)}, u32[]{:S(2)}, u32[]{:S(2)}) %collective-permute-start.22) | collective-permute-done | bytes 13856 | tf_op jit(solution)/shard_map/ppermute | solution.py:306
  69.4 0.7 %shard_map.101 = f32[12,3,192]{2,1,0:T(4,128)} custom-call(f32[12,576]{1,0:T(8,128)S(1)} %get-tuple-element.57.refs_0_, bf16[12,576]{1,0:T(8,128)(2,1)S(1)} %collective-permute-done.20.refs_1_, bf16[12,576]{1,0:T(8,128)(2,1)S(1)} %collective-permute-done.21.refs_2_, bf16[12,576]{1,0:T(8,128)(2,1)S(1)} %collective-permute-done.22.refs_3_), custom_call_target="tpu_custom_call" | custom-call | flops 1000000 | bytes 96768 | tf_op jit(solution)/shard_map/pallas_call | solution.py:297
  (27 shorter events, 0.7 us)
Async XLA Ops:
  0.6 8.2 %collective-permute-start.9 = (bf16[128,768]{1,0:T(8,128)(2,1)}, bf16[128,768]{1,0:T(8,128)(2,1)S(1)}, u32[]{:S(2)}, u32[]{:S(2)}) collective-permute-start(bf16[128,768]{1,0:T(8,128)(2,1)} %bitcast.14), channel_id=1, source_target_pairs={{0,2},{2,0},{1,3},{3,1},{4,6},{6,4},{5,7},{7,5},{8,10},{10,8},{9,1... | collective-permute-start | bytes 589832 | tf_op jit(solution)/shard_map/ppermute | solution.py:306
  2.9 15.7 %collective-permute-start.8 = (bf16[128,768]{1,0:T(8,128)(2,1)}, bf16[128,768]{1,0:T(8,128)(2,1)S(1)}, u32[]{:S(2)}, u32[]{:S(2)}) collective-permute-start(bf16[128,768]{1,0:T(8,128)(2,1)} %bitcast.15), channel_id=1, source_target_pairs={{0,1},{1,0},{2,3},{3,2},{4,5},{5,4},{6,7},{7,6},{8,9},{9,8},{10,11... | collective-permute-start | bytes 589832 | tf_op jit(solution)/shard_map/ppermute | solution.py:306
  2.9 15.2 %collective-permute-start.6 = (bf16[128,768]{1,0:T(8,128)(2,1)}, bf16[128,768]{1,0:T(8,128)(2,1)S(1)}, u32[]{:S(2)}, u32[]{:S(2)}) collective-permute-start(bf16[128,768]{1,0:T(8,128)(2,1)} %bitcast.17), channel_id=1, source_target_pairs={{0,2},{2,0},{1,3},{3,1},{4,6},{6,4},{5,7},{7,5},{8,10},{10,8},{9,1... | collective-permute-start | bytes 589832 | tf_op jit(solution)/shard_map/ppermute | solution.py:306
  3.1 15.6 %collective-permute-start.12 = (bf16[128,768]{1,0:T(8,128)(2,1)}, bf16[128,768]{1,0:T(8,128)(2,1)S(1)}, u32[]{:S(2)}, u32[]{:S(2)}) collective-permute-start(bf16[128,768]{1,0:T(8,128)(2,1)} %bitcast.20), channel_id=1, source_target_pairs={{0,2},{2,0},{1,3},{3,1},{4,6},{6,4},{5,7},{7,5},{8,10},{10,8},{9,1... | collective-permute-start | bytes 589832 | tf_op jit(solution)/shard_map/ppermute | solution.py:306
  6.8 11.3 %collective-permute-start.1 = (bf16[128,384]{1,0:T(8,128)(2,1)S(1)}, bf16[128,384]{1,0:T(8,128)(2,1)S(1)}, u32[]{:S(2)}, u32[]{:S(2)}) collective-permute-start(bf16[128,384]{1,0:T(8,128)(2,1)S(1)} %get-tuple-element.34), channel_id=1, source_target_pairs={{0,2},{2,0},{1,3},{3,1},{4,6},{6,4},{5,7},{7,5},{8,10},{10,8},{9,1... | collective-permute-start | bytes 294920 | tf_op jit(solution)/shard_map/ppermute | solution.py:306
  8.8 10.3 %collective-permute-start.10 = (bf16[128,768]{1,0:T(8,128)(2,1)S(1)}, bf16[128,768]{1,0:T(8,128)(2,1)S(1)}, u32[]{:S(2)}, u32[]{:S(2)}) collective-permute-start(bf16[128,768]{1,0:T(8,128)(2,1)S(1)} %collective-permute-done.9.refs_2_), channel_id=1, source_target_pairs={{0,1},{1,0},{2,3},{3,2},{4,5},{5,4},{6,7},{7,6},{8,9},{9,8},{10,11... | collective-permute-start | bytes 589832 | tf_op jit(solution)/shard_map/ppermute | solution.py:306
  18.1 1.7 %collective-permute-start.5 = (bf16[128,768]{1,0:T(8,128)(2,1)}, bf16[128,768]{1,0:T(8,128)(2,1)S(1)}, u32[]{:S(2)}, u32[]{:S(2)}) collective-permute-start(bf16[128,768]{1,0:T(8,128)(2,1)} %bitcast.19), channel_id=1, source_target_pairs={{0,1},{1,0},{2,3},{3,2},{4,5},{5,4},{6,7},{7,6},{8,9},{9,8},{10,11... | collective-permute-start | bytes 589832 | tf_op jit(solution)/shard_map/ppermute | solution.py:306
  18.1 1.9 %collective-permute-start.7 = (bf16[128,768]{1,0:T(8,128)(2,1)S(1)}, bf16[128,768]{1,0:T(8,128)(2,1)S(1)}, u32[]{:S(2)}, u32[]{:S(2)}) collective-permute-start(bf16[128,768]{1,0:T(8,128)(2,1)S(1)} %collective-permute-done.6.refs_2_), channel_id=1, source_target_pairs={{0,1},{1,0},{2,3},{3,2},{4,5},{5,4},{6,7},{7,6},{8,9},{9,8},{10,11... | collective-permute-start | bytes 589832 | tf_op jit(solution)/shard_map/ppermute | solution.py:306
  18.6 3.1 %collective-permute-start.11 = (bf16[128,768]{1,0:T(8,128)(2,1)}, bf16[128,768]{1,0:T(8,128)(2,1)S(1)}, u32[]{:S(2)}, u32[]{:S(2)}) collective-permute-start(bf16[128,768]{1,0:T(8,128)(2,1)} %bitcast.22), channel_id=1, source_target_pairs={{0,1},{1,0},{2,3},{3,2},{4,5},{5,4},{6,7},{7,6},{8,9},{9,8},{10,11... | collective-permute-start | bytes 589832 | tf_op jit(solution)/shard_map/ppermute | solution.py:306
  18.7 3.0 %collective-permute-start.13 = (bf16[128,768]{1,0:T(8,128)(2,1)S(1)}, bf16[128,768]{1,0:T(8,128)(2,1)S(1)}, u32[]{:S(2)}, u32[]{:S(2)}) collective-permute-start(bf16[128,768]{1,0:T(8,128)(2,1)S(1)} %collective-permute-done.12.refs_3_), channel_id=1, source_target_pairs={{0,1},{1,0},{2,3},{3,2},{4,5},{5,4},{6,7},{7,6},{8,9},{9,8},{10,11... | collective-permute-start | bytes 589832 | tf_op jit(solution)/shard_map/ppermute | solution.py:306
  19.1 4.5 %collective-permute-start = (bf16[128,768]{1,0:T(8,128)(2,1)}, bf16[128,768]{1,0:T(8,128)(2,1)S(1)}, u32[]{:S(2)}, u32[]{:S(2)}) collective-permute-start(bf16[128,768]{1,0:T(8,128)(2,1)} %bitcast.24), channel_id=1, source_target_pairs={{0,1},{1,0},{2,3},{3,2},{4,5},{5,4},{6,7},{7,6},{8,9},{9,8},{10,11... | collective-permute-start | bytes 589832 | tf_op jit(solution)/shard_map/ppermute | solution.py:306
  19.8 3.8 %collective-permute-start.2 = (bf16[128,384]{1,0:T(8,128)(2,1)S(1)}, bf16[128,384]{1,0:T(8,128)(2,1)S(1)}, u32[]{:S(2)}, u32[]{:S(2)}) collective-permute-start(bf16[128,384]{1,0:T(8,128)(2,1)S(1)} %collective-permute-done.1.refs_2_.g_across), channel_id=1, source_target_pairs={{0,1},{1,0},{2,3},{3,2},{4,5},{5,4},{6,7},{7,6},{8,9},{9,8},{10,11... | collective-permute-start | bytes 294920 | tf_op jit(solution)/shard_map/ppermute | solution.py:306
  21.7 30.6 %copy-start = (bf16[768,3,768]{2,0,1:T(8,128)(2,1)S(1)}, bf16[768,3,768]{2,0,1:T(8,128)(2,1)}, u32[]{:S(2)}) copy-start(bf16[768,3,768]{2,0,1:T(8,128)(2,1)} %param.8) | copy-start | bytes 10616836
  25.5 9.4 %collective-permute-start.14 = (bf16[96,1152]{1,0:T(8,128)(2,1)S(1)}, bf16[96,1152]{1,0:T(8,128)(2,1)S(1)}, u32[]{:S(2)}, u32[]{:S(2)}) collective-permute-start(bf16[96,1152]{1,0:T(8,128)(2,1)S(1)} %get-tuple-element.50), channel_id=1, source_target_pairs={{0,64},{64,0},{128,192},{192,128},{1,65},{65,1},{129,193},{193,129... | collective-permute-start | bytes 663560 | tf_op jit(solution)/shard_map/ppermute | solution.py:306
  27.1 13.1 %collective-permute-start.15 = (bf16[96,1152]{1,0:T(8,128)(2,1)S(1)}, bf16[96,1152]{1,0:T(8,128)(2,1)S(1)}, u32[]{:S(2)}, u32[]{:S(2)}) collective-permute-start(bf16[96,1152]{1,0:T(8,128)(2,1)S(1)} %get-tuple-element.51), channel_id=1, source_target_pairs={{0,128},{64,192},{128,0},{192,64},{1,129},{65,193},{129,1},{193,65... | collective-permute-start | bytes 663560 | tf_op jit(solution)/shard_map/ppermute | solution.py:306
  29.8 13.0 %collective-permute-start.16 = (bf16[96,1152]{1,0:T(8,128)(2,1)S(1)}, bf16[96,1152]{1,0:T(8,128)(2,1)S(1)}, u32[]{:S(2)}, u32[]{:S(2)}) collective-permute-start(bf16[96,1152]{1,0:T(8,128)(2,1)S(1)} %get-tuple-element.52), channel_id=1, source_target_pairs={{0,192},{64,128},{128,64},{192,0},{1,193},{65,129},{129,65},{193,1... | collective-permute-start | bytes 663560 | tf_op jit(solution)/shard_map/ppermute | solution.py:306
  30.3 4.6 %collective-permute-start.3 = (bf16[128,384]{1,0:T(8,128)(2,1)S(1)}, bf16[128,384]{1,0:T(8,128)(2,1)S(1)}, u32[]{:S(2)}, u32[]{:S(2)}) collective-permute-start(bf16[128,384]{1,0:T(8,128)(2,1)S(1)} %get-tuple-element.35), channel_id=1, source_target_pairs={{0,2},{2,0},{1,3},{3,1},{4,6},{6,4},{5,7},{7,5},{8,10},{10,8},{9,1... | collective-permute-start | bytes 294920 | tf_op jit(solution)/shard_map/ppermute | solution.py:306
  34.9 17.3 %collective-permute-start.4 = (bf16[128,384]{1,0:T(8,128)(2,1)S(1)}, bf16[128,384]{1,0:T(8,128)(2,1)S(1)}, u32[]{:S(2)}, u32[]{:S(2)}) collective-permute-start(bf16[128,384]{1,0:T(8,128)(2,1)S(1)} %collective-permute-done.3.refs_4_), channel_id=1, source_target_pairs={{0,1},{1,0},{2,3},{3,2},{4,5},{5,4},{6,7},{7,6},{8,9},{9,8},{10,11... | collective-permute-start | bytes 294920 | tf_op jit(solution)/shard_map/ppermute | solution.py:306
  43.5 13.1 %collective-permute-start.17 = (bf16[24,1152]{1,0:T(8,128)(2,1)S(1)}, bf16[24,1152]{1,0:T(8,128)(2,1)S(1)}, u32[]{:S(2)}, u32[]{:S(2)}) collective-permute-start(bf16[24,1152]{1,0:T(8,128)(2,1)S(1)} %get-tuple-element.54), channel_id=1, source_target_pairs={{0,8},{4,12},{8,0},{12,4},{16,24},{20,28},{24,16},{28,20},{1,9},{5... | collective-permute-start | bytes 165896 | tf_op jit(solution)/shard_map/ppermute | solution.py:306
  46.9 9.8 %collective-permute-start.18 = (bf16[24,1152]{1,0:T(8,128)(2,1)S(1)}, bf16[24,1152]{1,0:T(8,128)(2,1)S(1)}, u32[]{:S(2)}, u32[]{:S(2)}) collective-permute-start(bf16[24,1152]{1,0:T(8,128)(2,1)S(1)} %get-tuple-element.55), channel_id=1, source_target_pairs={{0,16},{4,20},{8,24},{12,28},{16,0},{20,4},{24,8},{28,12},{1,17},{... | collective-permute-start | bytes 165896 | tf_op jit(solution)/shard_map/ppermute | solution.py:306
  52.3 6.4 %collective-permute-start.19 = (bf16[24,1152]{1,0:T(8,128)(2,1)S(1)}, bf16[24,1152]{1,0:T(8,128)(2,1)S(1)}, u32[]{:S(2)}, u32[]{:S(2)}) collective-permute-start(bf16[24,1152]{1,0:T(8,128)(2,1)S(1)} %get-tuple-element.56), channel_id=1, source_target_pairs={{0,24},{4,28},{8,16},{12,20},{16,8},{20,12},{24,0},{28,4},{1,25},{... | collective-permute-start | bytes 165896 | tf_op jit(solution)/shard_map/ppermute | solution.py:306
  59.3 8.2 %collective-permute-start.20 = (bf16[12,576]{1,0:T(8,128)(2,1)S(1)}, bf16[12,576]{1,0:T(8,128)(2,1)S(1)}, u32[]{:S(2)}, u32[]{:S(2)}) collective-permute-start(bf16[12,576]{1,0:T(8,128)(2,1)S(1)} %get-tuple-element.58), channel_id=1, source_target_pairs={{0,32},{32,0},{1,33},{33,1},{2,34},{34,2},{3,35},{35,3},{4,36},{36... | collective-permute-start | bytes 41480 | tf_op jit(solution)/shard_map/ppermute | solution.py:306
  61.7 5.8 %collective-permute-start.21 = (bf16[12,576]{1,0:T(8,128)(2,1)S(1)}, bf16[12,576]{1,0:T(8,128)(2,1)S(1)}, u32[]{:S(2)}, u32[]{:S(2)}) collective-permute-start(bf16[12,576]{1,0:T(8,128)(2,1)S(1)} %get-tuple-element.59), channel_id=1, source_target_pairs={{0,4},{4,0},{8,12},{12,8},{16,20},{20,16},{24,28},{28,24},{1,5},{5... | collective-permute-start | bytes 41480 | tf_op jit(solution)/shard_map/ppermute | solution.py:306
  63.2 6.2 %collective-permute-start.22 = (bf16[12,576]{1,0:T(8,128)(2,1)S(1)}, bf16[12,576]{1,0:T(8,128)(2,1)S(1)}, u32[]{:S(2)}, u32[]{:S(2)}) collective-permute-start(bf16[12,576]{1,0:T(8,128)(2,1)S(1)} %get-tuple-element.60), channel_id=1, source_target_pairs={{0,36},{4,32},{8,44},{12,40},{16,52},{20,48},{24,60},{28,56},{32,4... | collective-permute-start | bytes 41480 | tf_op jit(solution)/shard_map/ppermute | solution.py:306

commit v7 on v6

--- a/solution.py
+++ b/solution.py
@@ -100,15 +100,14 @@
 
 
 def score_kernel(*refs):
-    q, km = refs[0:4], refs[4]
-    soft_ref, rounded_ref = refs[5:7]
-    q_all, s_ref = refs[7:]
+    q, km = refs[:-5], refs[-5]
+    soft_ref, rounded_ref, q_all, s_ref = refs[-4:]
     inverse = 1.0 / math.sqrt(HEAD_DIM)
-    for r in range(4):
-        q_all[r * ROWS : (r + 1) * ROWS, :] = q[r][...]
+    for r, block in enumerate(q):
+        q_all[r * ROWS : (r + 1) * ROWS, :] = block[...]
     for h in range(HEADS):
         s_ref[...] = dot(window(q_all, h), km[h], NT)
-        for c in range(8):
+        for c in range(2 * len(q)):
             at = slice(c * 64, (c + 1) * 64)
             s = s_ref[at, :] * inverse
             e = jnp.exp(s - jnp.max(s, axis=1, keepdims=True))
@@ -118,16 +117,17 @@
 
 
 def attend_kernel(ids, *refs):
-    rounded_ref, v = refs[0], refs[1:5]
-    attended_ref, acted_ref, vm = refs[5:8]
-    o_ref = refs[8]
+    rounded, v = refs[0:2], refs[2:6]
+    attended_ref, acted_ref, vm = refs[6:9]
+    o_ref = refs[9]
     me = ids[0]
     for r in range(4):
         at = slice(r * ROWS, (r + 1) * ROWS)
         for h in range(HEADS):
             vm[h, at, :] = masked_window(window(v[r], h), h)
     for h in range(HEADS):
-        o_ref[h] = dot(rounded_ref[h], vm[h])
+        weights = jnp.concatenate([part[h] for part in rounded], axis=0)
+        o_ref[h] = dot(weights, vm[h])
     acted_ref[0:STEP, :] = jnp.zeros((STEP, 768), BF16)
     acted_ref[STEP + 512 :, :] = jnp.zeros((STEP, 768), BF16)
     for r in range(4):
@@ -205,9 +205,9 @@
 
 
 def backward_kernel(*refs):
-    q, km, vm, soft_ref, do_ref = refs[0:4], refs[4], refs[5], refs[6], refs[7]
-    dq_ref, dk_ref, dv_ref = refs[8:11]
-    qm, dp_ref, ds_ref = refs[11:]
+    q, km, vm, soft, do_ref = refs[0:4], refs[4], refs[5], refs[6:8], refs[8]
+    dq_ref, dk_ref, dv_ref = refs[9:12]
+    qm, dp_ref, ds_ref = refs[12:]
     inverse = 1.0 / math.sqrt(HEAD_DIM)
     for r in range(4):
         at = slice(r * ROWS, (r + 1) * ROWS)
@@ -219,14 +219,15 @@
         dp_ref[...] = dot(grad_out, vm[h], NT)
         for c in range(8):
             at = slice(c * 64, (c + 1) * 64)
-            p = soft_ref[h, at, :]
+            p = soft[c // 6][h, (c % 6) * 64 : (c % 6) * 64 + 64, :]
             dp = dp_ref[at, :]
             inner = jnp.sum(dp * p, axis=1, keepdims=True)
             wide = 512 if c < 2 else ROWS
             ds_ref[at, 0:wide] = (p[:, :wide] * (dp[:, :wide] - inner) * inverse).astype(BF16)
         dq.append(dot(ds_ref[0:ROWS, :], km[h]))
         dk.append(dot(ds_ref[:, 0:ROWS], qm[h], TN))
-        dv.append(dot(soft_ref[h, :, 0:ROWS].astype(BF16), masked_window(grad_out, h), TN))
+        weights = jnp.concatenate([part[h, :, 0:ROWS].astype(BF16) for part in soft], axis=0)
+        dv.append(dot(weights, masked_window(grad_out, h), TN))
     dq_ref[...] = place(dq).astype(BF16)
     dk_ref[...] = place(dk).astype(BF16)
     dv_ref[...] = place(dv).astype(BF16)
@@ -336,21 +337,23 @@
     need = (across["need"], diag["need"])
     rest = (across["rest"], diag["rest"])
     (km,) = call(keys_kernel, [shaped((HEADS, 512, 256))], [], k, 1_000_000)
-    soft, rounded = call(
-        score_kernel,
-        [shaped((HEADS, 512, 512), F32), shaped((HEADS, 512, 512))],
-        [
-            pltpu.VMEM((512, 768), BF16),
-            pltpu.VMEM((512, 512), F32),
-        ],
-        [*q, km],
-        1_000_000_000,
-    )
+    soft, rounded = [], []
+    for part in (q[:3], q[3:]):
+        rows = ROWS * len(part)
+        exact, low = call(
+            score_kernel,
+            [shaped((HEADS, rows, 512), F32), shaped((HEADS, rows, 512))],
+            [pltpu.VMEM((rows, 768), BF16), pltpu.VMEM((rows, 512), F32)],
+            [*part, km],
+            2_000_000 * rows,
+        )
+        soft.append(exact)
+        rounded.append(low)
     attended, acted, vm = call(
         attend_kernel,
         [shaped((512, 768)), shaped((576, 768)), shaped((HEADS, 512, 256))],
         [pltpu.VMEM((HEADS, 512, 256), F32)],
-        [ids, rounded, *v],
+        [ids, *rounded, *v],
         1_000_000_000,
     )
     rows = 768 // x_size
@@ -382,7 +385,7 @@
             pltpu.VMEM((512, 512), F32),
             pltpu.VMEM((512, 512), BF16),
         ],
-        [*q, km, vm, soft, grad_attended],
+        [*q, km, vm, *soft, grad_attended],
         1_000_000_000,
         20,
     )

time: 70.2 us -> 70.5 us (level)
    pallas_call x10 -> x11, Pallas kernels: 16.8 us -> 17.2 us  [call(): return run(*args)]
  transfers between devices with their start and end apart: 23 -> 23, of which waited for: 9 -> 8; matrix products, arithmetic and copies ran while one was open for 0% -> 0% of each run, Pallas kernels for 19% -> 20%
where the time goes in v7:
time: 70.5 us; the launch traced here: 70.4 us
  waiting for transfers between devices  27 us (38%)
  starting transfers between devices  25.4 us (36%)
  Pallas kernels  17.2 us (24%)
  between operations  0.77 us (1%)
    ppermute x23, waiting for transfers between devices, swap(): return lax.ppermute(value, axis, [(i, i ^ mask) for i in range(count)])  27 us
    ppermute x23, starting transfers between devices, swap(): return lax.ppermute(value, axis, [(i, i ^ mask) for i in range(count)])  25.4 us
    pallas_call x11, Pallas kernels, call(): return run(*args)  17.2 us
  transfers between devices with their start and end apart: 23, of which 8 were waited for; matrix products, arithmetic and copies ran while one was open for 0% of the time, Pallas kernels for 20%

profile of v7, /device:TPU:8, one launch (start us, length us, event | category | flops | bytes accessed | tf_op | source)
XLA Modules:
  0.0 70.4 jit_solution(12797595619563146316)
XLA Ops:
  0.6 2.2 %collective-permute-start.8 = (bf16[128,768]{1,0:T(8,128)(2,1)}, bf16[128,768]{1,0:T(8,128)(2,1)S(1)}, u32[]{:S(2)}, u32[]{:S(2)}) collective-permute-start(bf16[128,768]{1,0:T(8,128)(2,1)} %bitcast.14), channel_id=1, source_target_pairs={{0,2},{2,0},{1,3},{3,1},{4,6},{6,4},{5,7},{7,5},{8,10},{10,8},{9,1... | collective-permute-start | bytes 589832 | tf_op jit(solution)/shard_map/ppermute | solution.py:307
  3.1 1.8 %collective-permute-start.12 = (bf16[128,768]{1,0:T(8,128)(2,1)}, bf16[128,768]{1,0:T(8,128)(2,1)S(1)}, u32[]{:S(2)}, u32[]{:S(2)}) collective-permute-start(bf16[128,768]{1,0:T(8,128)(2,1)} %bitcast.20), channel_id=1, source_target_pairs={{0,2},{2,0},{1,3},{3,1},{4,6},{6,4},{5,7},{7,5},{8,10},{10,8},{9,1... | collective-permute-start | bytes 589832 | tf_op jit(solution)/shard_map/ppermute | solution.py:307
  5.0 1.8 %shard_map.92 = (bf16[128,768]{1,0:T(8,128)(2,1)S(1)}, bf16[128,768]{1,0:T(8,128)(2,1)S(1)}, bf16[128,768]{1,0:T(8,128)(2,1)S(1)}, bf16[128,768]{1,0:T(8,128)(2,...) custom-call(s32[4]{0:T(128)S(1)} %pad_add_fusion.ids, bf16[128,768]{1,0:T(8,128)(2,1)} %bitcast.18, ...), custom_call_target="tpu_custom_call" | custom-call | flops 1000000 | bytes 1769488 | tf_op jit(solution)/shard_map/pallas_call | solution.py:298
  6.8 0.3 collective-permute-start.1
  7.1 1.8 %collective-permute-done.8.refs_2_ = bf16[128,768]{1,0:T(8,128)(2,1)S(1)} collective-permute-done((bf16[128,768]{1,0:T(8,128)(2,1)}, bf16[128,768]{1,0:T(8,128)(2,1)S(1)}, u32[]{:S(2)}, u32[]{:S(2)}) %collective-permute-start.8) | collective-permute-done | bytes 196640 | tf_op jit(solution)/shard_map/ppermute | solution.py:307
  8.8 9.3 %collective-permute-done.1.refs_2_.g_across = bf16[128,384]{1,0:T(8,128)(2,1)S(1)} collective-permute-done((bf16[128,384]{1,0:T(8,128)(2,1)S(1)}, bf16[128,384]{1,0:T(8,128)(2,1)S(1)}, u32[]{:S(2)}, u32[]{:S(2)}) %collective-permute-start.1) | collective-permute-done | bytes 98336 | tf_op jit(solution)/shard_map/ppermute | solution.py:307
  18.1 0.5 collective-permute-start.10
  18.7 0.4 collective-permute-start.13
  19.3 0.4 collective-permute-done.5.refs_1_
  19.9 1.3 %shard_map.94 = (f32[4,384,512]{2,1,0:T(8,128)S(1)}, bf16[4,384,512]{2,1,0:T(8,128)(2,1)S(1)}) custom-call(bf16[128,768]{1,0:T(8,128)(2,1)S(1)} %get-tuple-element.38.refs_0_, bf16[128,768]{1,0:T(8,128)(2,1)S(1)} %collective-permute-done.5.refs_1_, bf16[128,768]{1,0:T(8,128)(2,1)S(1)} %collective-permute-done.6.refs_2_, ...), custom_call_target="tpu_custom_call" | custom-call | flops 768000000 | bytes 6356992 | tf_op jit(solution)/shard_map/pallas_call | solution.py:298
  21.2 0.7 shard_map.95
  21.9 1.9 %shard_map.96 = (bf16[512,768]{1,0:T(8,128)(2,1)S(1)}, bf16[576,768]{1,0:T(8,128)(2,1)S(1)}, bf16[4,512,256]{2,1,0:T(8,128)(2,1)S(1)}) custom-call(s32[4]{0:T(128)S(1)} %pad_add_fusion.ids, bf16[4,384,512]{2,1,0:T(8,128)(2,1)S(1)} %get-tuple-element.40.refs_0_, bf16[4,128,512]{2,1,0:T(8,128)(2,1)S(1)} %get-tuple-element.41.refs_1_, ...), custom_call_target="tpu_custom_call" | custom-call | flops 1000000000 | bytes 5603344 | tf_op jit(solution)/shard_map/pallas_call | solution.py:298
  23.8 1.9 %shard_map.99 = (bf16[96,1152]{1,0:T(8,128)(2,1)S(1)}, bf16[96,1152]{1,0:T(8,128)(2,1)S(1)}, bf16[96,1152]{1,0:T(8,128)(2,1)S(1)}, bf16[96,1152]{1,0:T(8,128)(2,1)S(1)}) custom-call(s32[4]{0:T(128)S(1)} %pad_add_fusion.ids, bf16[576,768]{1,0:T(8,128)(2,1)S(1)} %get-tuple-element.44.refs_7_.acted_ref, bf16[128,768]{1,0:T(8,128)(2,1)S(1)} %get-tuple-element.35.refs_0_.g_own, ...), custom_call_target="tpu_custom_call" | custom-call | flops 500000000 | bytes 2359312 | tf_op jit(solution)/shard_map/pallas_call | solution.py:298
  25.7 1.6 %collective-permute-start.14 = (bf16[96,1152]{1,0:T(8,128)(2,1)S(1)}, bf16[96,1152]{1,0:T(8,128)(2,1)S(1)}, u32[]{:S(2)}, u32[]{:S(2)}) collective-permute-start(bf16[96,1152]{1,0:T(8,128)(2,1)S(1)} %get-tuple-element.54), channel_id=1, source_target_pairs={{0,64},{64,0},{128,192},{192,128},{1,65},{65,1},{129,193},{193,129... | collective-permute-start | bytes 663560 | tf_op jit(solution)/shard_map/ppermute | solution.py:307
  27.3 2.7 %collective-permute-start.15 = (bf16[96,1152]{1,0:T(8,128)(2,1)S(1)}, bf16[96,1152]{1,0:T(8,128)(2,1)S(1)}, u32[]{:S(2)}, u32[]{:S(2)}) collective-permute-start(bf16[96,1152]{1,0:T(8,128)(2,1)S(1)} %get-tuple-element.55), channel_id=1, source_target_pairs={{0,128},{64,192},{128,0},{192,64},{1,129},{65,193},{129,1},{193,65... | collective-permute-start | bytes 663560 | tf_op jit(solution)/shard_map/ppermute | solution.py:307
  30.0 0.5 collective-permute-start.16
  30.5 1.0 %collective-permute-start.3 = (bf16[128,384]{1,0:T(8,128)(2,1)S(1)}, bf16[128,384]{1,0:T(8,128)(2,1)S(1)}, u32[]{:S(2)}, u32[]{:S(2)}) collective-permute-start(bf16[128,384]{1,0:T(8,128)(2,1)S(1)} %get-tuple-element.37), channel_id=1, source_target_pairs={{0,2},{2,0},{1,3},{3,1},{4,6},{6,4},{5,7},{7,5},{8,10},{10,8},{9,1... | collective-permute-start | bytes 294920 | tf_op jit(solution)/shard_map/ppermute | solution.py:307
  31.5 3.6 %collective-permute-done.3.refs_4_ = bf16[128,384]{1,0:T(8,128)(2,1)S(1)} collective-permute-done((bf16[128,384]{1,0:T(8,128)(2,1)S(1)}, bf16[128,384]{1,0:T(8,128)(2,1)S(1)}, u32[]{:S(2)}, u32[]{:S(2)}) %collective-permute-start.3) | collective-permute-done | bytes 98336 | tf_op jit(solution)/shard_map/ppermute | solution.py:307
  35.1 5.4 %collective-permute-done.15.refs_2_ = bf16[96,1152]{1,0:T(8,128)(2,1)S(1)} collective-permute-done((bf16[96,1152]{1,0:T(8,128)(2,1)S(1)}, bf16[96,1152]{1,0:T(8,128)(2,1)S(1)}, u32[]{:S(2)}, u32[]{:S(2)}) %collective-permute-start.15) | collective-permute-done | bytes 221216 | tf_op jit(solution)/shard_map/ppermute | solution.py:307
  40.6 2.6 %collective-permute-done.16.refs_3_ = bf16[96,1152]{1,0:T(8,128)(2,1)S(1)} collective-permute-done((bf16[96,1152]{1,0:T(8,128)(2,1)S(1)}, bf16[96,1152]{1,0:T(8,128)(2,1)S(1)}, u32[]{:S(2)}, u32[]{:S(2)}) %collective-permute-start.16) | collective-permute-done | bytes 221216 | tf_op jit(solution)/shard_map/ppermute | solution.py:307
  43.1 0.7 %shard_map.100 = (f32[24,1152]{1,0:T(8,128)S(1)}, bf16[24,1152]{1,0:T(8,128)(2,1)S(1)}, bf16[24,1152]{1,0:T(8,128)(2,1)S(1)}, bf16[24,1152]{1,0:T(8,128)(2,1)S(1)}) custom-call(s32[4]{0:T(128)S(1)} %pad_add_fusion.ids, bf16[96,1152]{1,0:T(8,128)(2,1)S(1)} %get-tuple-element.53.refs_0_, bf16[96,1152]{1,0:T(8,128)(2,1)S(1)} %collective-permute-done.14.refs_1_, ...), custom_call_target="tpu_custom_call" | custom-call | flops 1000000 | bytes 1161232 | tf_op jit(solution)/shard_map/pallas_call | solution.py:298
  43.9 3.4 %collective-permute-start.17 = (bf16[24,1152]{1,0:T(8,128)(2,1)S(1)}, bf16[24,1152]{1,0:T(8,128)(2,1)S(1)}, u32[]{:S(2)}, u32[]{:S(2)}) collective-permute-start(bf16[24,1152]{1,0:T(8,128)(2,1)S(1)} %get-tuple-element.58), channel_id=1, source_target_pairs={{0,8},{4,12},{8,0},{12,4},{16,24},{20,28},{24,16},{28,20},{1,9},{5... | collective-permute-start | bytes 165896 | tf_op jit(solution)/shard_map/ppermute | solution.py:307
  47.2 5.4 %collective-permute-start.18 = (bf16[24,1152]{1,0:T(8,128)(2,1)S(1)}, bf16[24,1152]{1,0:T(8,128)(2,1)S(1)}, u32[]{:S(2)}, u32[]{:S(2)}) collective-permute-start(bf16[24,1152]{1,0:T(8,128)(2,1)S(1)} %get-tuple-element.59), channel_id=1, source_target_pairs={{0,16},{4,20},{8,24},{12,28},{16,0},{20,4},{24,8},{28,12},{1,17},{... | collective-permute-start | bytes 165896 | tf_op jit(solution)/shard_map/ppermute | solution.py:307
  52.6 4.4 %shard_map.97 = (bf16[128,768]{1,0:T(8,128)(2,1)}, bf16[512,768]{1,0:T(8,128)(2,1)S(1)}) custom-call(s32[4]{0:T(128)S(1)} %pad_add_fusion.ids, bf16[128,768]{1,0:T(8,128)(2,1)S(1)} %get-tuple-element.35.refs_0_.g_own, bf16[128,768]{1,0:T(8,128)(2,1)S(1)} %collective-permute-done.refs_1_.g_core, bf16[128,384]{1,0:T(8,128)(2,1)S(1)} %collective-permute-done.1.refs_2_.g_across, ...), custom_call_target="tpu_custom_call" | custom-call | flops 2000000000 | bytes 6979600 | tf_op jit(solution)/shard_map/pallas_call | solution.py:298
  57.0 2.0 %collective-permute-done.19.refs_3_ = bf16[24,1152]{1,0:T(8,128)(2,1)S(1)} collective-permute-done((bf16[24,1152]{1,0:T(8,128)(2,1)S(1)}, bf16[24,1152]{1,0:T(8,128)(2,1)S(1)}, u32[]{:S(2)}, u32[]{:S(2)}) %collective-permute-start.19) | collective-permute-done | bytes 55328 | tf_op jit(solution)/shard_map/ppermute | solution.py:307
  59.0 0.6 shard_map.101
  59.6 2.4 %collective-permute-start.20 = (bf16[12,576]{1,0:T(8,128)(2,1)S(1)}, bf16[12,576]{1,0:T(8,128)(2,1)S(1)}, u32[]{:S(2)}, u32[]{:S(2)}) collective-permute-start(bf16[12,576]{1,0:T(8,128)(2,1)S(1)} %get-tuple-element.62), channel_id=1, source_target_pairs={{0,32},{32,0},{1,33},{33,1},{2,34},{34,2},{3,35},{35,3},{4,36},{36... | collective-permute-start | bytes 41480 | tf_op jit(solution)/shard_map/ppermute | solution.py:307
  62.0 1.5 %collective-permute-start.21 = (bf16[12,576]{1,0:T(8,128)(2,1)S(1)}, bf16[12,576]{1,0:T(8,128)(2,1)S(1)}, u32[]{:S(2)}, u32[]{:S(2)}) collective-permute-start(bf16[12,576]{1,0:T(8,128)(2,1)S(1)} %get-tuple-element.63), channel_id=1, source_target_pairs={{0,4},{4,0},{8,12},{12,8},{16,20},{20,16},{24,28},{28,24},{1,5},{5... | collective-permute-start | bytes 41480 | tf_op jit(solution)/shard_map/ppermute | solution.py:307
  63.5 1.2 %collective-permute-start.22 = (bf16[12,576]{1,0:T(8,128)(2,1)S(1)}, bf16[12,576]{1,0:T(8,128)(2,1)S(1)}, u32[]{:S(2)}, u32[]{:S(2)}) collective-permute-start(bf16[12,576]{1,0:T(8,128)(2,1)S(1)} %get-tuple-element.64), channel_id=1, source_target_pairs={{0,36},{4,32},{8,44},{12,40},{16,52},{20,48},{24,60},{28,56},{32,4... | collective-permute-start | bytes 41480 | tf_op jit(solution)/shard_map/ppermute | solution.py:307
  64.7 3.1 %shard_map.98 = (bf16[128,768]{1,0:T(8,128)(2,1)}, bf16[128,768]{1,0:T(8,128)(2,1)}, bf16[128,768]{1,0:T(8,128)(2,1)}) custom-call(bf16[128,768]{1,0:T(8,128)(2,1)S(1)} %get-tuple-element.38.refs_0_, bf16[128,768]{1,0:T(8,128)(2,1)S(1)} %collective-permute-done.5.refs_1_, bf16[128,768]{1,0:T(8,128)(2,1)S(1)} %collective-permute-done.6.refs_2_, ...), custom_call_target="tpu_custom_call" | custom-call | flops 1000000000 | bytes 8454144 | tf_op jit(solution)/shard_map/pallas_call | solution.py:298
  67.8 1.9 %collective-permute-done.22.refs_3_ = bf16[12,576]{1,0:T(8,128)(2,1)S(1)} collective-permute-done((bf16[12,576]{1,0:T(8,128)(2,1)S(1)}, bf16[12,576]{1,0:T(8,128)(2,1)S(1)}, u32[]{:S(2)}, u32[]{:S(2)}) %collective-permute-start.22) | collective-permute-done | bytes 13856 | tf_op jit(solution)/shard_map/ppermute | solution.py:307
  69.7 0.7 %shard_map.102 = f32[12,3,192]{2,1,0:T(4,128)} custom-call(f32[12,576]{1,0:T(8,128)S(1)} %get-tuple-element.61.refs_0_, bf16[12,576]{1,0:T(8,128)(2,1)S(1)} %collective-permute-done.20.refs_1_, bf16[12,576]{1,0:T(8,128)(2,1)S(1)} %collective-permute-done.21.refs_2_, bf16[12,576]{1,0:T(8,128)(2,1)S(1)} %collective-permute-done.22.refs_3_), custom_call_target="tpu_custom_call" | custom-call | flops 1000000 | bytes 96768 | tf_op jit(solution)/shard_map/pallas_call | solution.py:298
  (28 shorter events, 0.7 us)
Async XLA Ops:
  0.6 8.2 %collective-permute-start.8 = (bf16[128,768]{1,0:T(8,128)(2,1)}, bf16[128,768]{1,0:T(8,128)(2,1)S(1)}, u32[]{:S(2)}, u32[]{:S(2)}) collective-permute-start(bf16[128,768]{1,0:T(8,128)(2,1)} %bitcast.14), channel_id=1, source_target_pairs={{0,2},{2,0},{1,3},{3,1},{4,6},{6,4},{5,7},{7,5},{8,10},{10,8},{9,1... | collective-permute-start | bytes 589832 | tf_op jit(solution)/shard_map/ppermute | solution.py:307
  2.9 15.7 %collective-permute-start.7 = (bf16[128,768]{1,0:T(8,128)(2,1)}, bf16[128,768]{1,0:T(8,128)(2,1)S(1)}, u32[]{:S(2)}, u32[]{:S(2)}) collective-permute-start(bf16[128,768]{1,0:T(8,128)(2,1)} %bitcast.15), channel_id=1, source_target_pairs={{0,1},{1,0},{2,3},{3,2},{4,5},{5,4},{6,7},{7,6},{8,9},{9,8},{10,11... | collective-permute-start | bytes 589832 | tf_op jit(solution)/shard_map/ppermute | solution.py:307
  2.9 15.2 %collective-permute-start.6 = (bf16[128,768]{1,0:T(8,128)(2,1)}, bf16[128,768]{1,0:T(8,128)(2,1)S(1)}, u32[]{:S(2)}, u32[]{:S(2)}) collective-permute-start(bf16[128,768]{1,0:T(8,128)(2,1)} %bitcast.17), channel_id=1, source_target_pairs={{0,2},{2,0},{1,3},{3,1},{4,6},{6,4},{5,7},{7,5},{8,10},{10,8},{9,1... | collective-permute-start | bytes 589832 | tf_op jit(solution)/shard_map/ppermute | solution.py:307
  3.1 15.6 %collective-permute-start.12 = (bf16[128,768]{1,0:T(8,128)(2,1)}, bf16[128,768]{1,0:T(8,128)(2,1)S(1)}, u32[]{:S(2)}, u32[]{:S(2)}) collective-permute-start(bf16[128,768]{1,0:T(8,128)(2,1)} %bitcast.20), channel_id=1, source_target_pairs={{0,2},{2,0},{1,3},{3,1},{4,6},{6,4},{5,7},{7,5},{8,10},{10,8},{9,1... | collective-permute-start | bytes 589832 | tf_op jit(solution)/shard_map/ppermute | solution.py:307
  6.8 11.3 %collective-permute-start.1 = (bf16[128,384]{1,0:T(8,128)(2,1)S(1)}, bf16[128,384]{1,0:T(8,128)(2,1)S(1)}, u32[]{:S(2)}, u32[]{:S(2)}) collective-permute-start(bf16[128,384]{1,0:T(8,128)(2,1)S(1)} %get-tuple-element.36), channel_id=1, source_target_pairs={{0,2},{2,0},{1,3},{3,1},{4,6},{6,4},{5,7},{7,5},{8,10},{10,8},{9,1... | collective-permute-start | bytes 294920 | tf_op jit(solution)/shard_map/ppermute | solution.py:307
  8.8 10.3 %collective-permute-start.9 = (bf16[128,768]{1,0:T(8,128)(2,1)S(1)}, bf16[128,768]{1,0:T(8,128)(2,1)S(1)}, u32[]{:S(2)}, u32[]{:S(2)}) collective-permute-start(bf16[128,768]{1,0:T(8,128)(2,1)S(1)} %collective-permute-done.8.refs_2_), channel_id=1, source_target_pairs={{0,1},{1,0},{2,3},{3,2},{4,5},{5,4},{6,7},{7,6},{8,9},{9,8},{10,11... | collective-permute-start | bytes 589832 | tf_op jit(solution)/shard_map/ppermute | solution.py:307
  18.1 1.7 %collective-permute-start.5 = (bf16[128,768]{1,0:T(8,128)(2,1)}, bf16[128,768]{1,0:T(8,128)(2,1)S(1)}, u32[]{:S(2)}, u32[]{:S(2)}) collective-permute-start(bf16[128,768]{1,0:T(8,128)(2,1)} %bitcast.19), channel_id=1, source_target_pairs={{0,1},{1,0},{2,3},{3,2},{4,5},{5,4},{6,7},{7,6},{8,9},{9,8},{10,11... | collective-permute-start | bytes 589832 | tf_op jit(solution)/shard_map/ppermute | solution.py:307
  18.1 3.1 %collective-permute-start.10 = (bf16[128,768]{1,0:T(8,128)(2,1)S(1)}, bf16[128,768]{1,0:T(8,128)(2,1)S(1)}, u32[]{:S(2)}, u32[]{:S(2)}) collective-permute-start(bf16[128,768]{1,0:T(8,128)(2,1)S(1)} %collective-permute-done.6.refs_2_), channel_id=1, source_target_pairs={{0,1},{1,0},{2,3},{3,2},{4,5},{5,4},{6,7},{7,6},{8,9},{9,8},{10,11... | collective-permute-start | bytes 589832 | tf_op jit(solution)/shard_map/ppermute | solution.py:307
  18.6 3.2 %collective-permute-start.11 = (bf16[128,768]{1,0:T(8,128)(2,1)}, bf16[128,768]{1,0:T(8,128)(2,1)S(1)}, u32[]{:S(2)}, u32[]{:S(2)}) collective-permute-start(bf16[128,768]{1,0:T(8,128)(2,1)} %bitcast.22), channel_id=1, source_target_pairs={{0,1},{1,0},{2,3},{3,2},{4,5},{5,4},{6,7},{7,6},{8,9},{9,8},{10,11... | collective-permute-start | bytes 589832 | tf_op jit(solution)/shard_map/ppermute | solution.py:307
  18.7 3.2 %collective-permute-start.13 = (bf16[128,768]{1,0:T(8,128)(2,1)S(1)}, bf16[128,768]{1,0:T(8,128)(2,1)S(1)}, u32[]{:S(2)}, u32[]{:S(2)}) collective-permute-start(bf16[128,768]{1,0:T(8,128)(2,1)S(1)} %collective-permute-done.12.refs_4_), channel_id=1, source_target_pairs={{0,1},{1,0},{2,3},{3,2},{4,5},{5,4},{6,7},{7,6},{8,9},{9,8},{10,11... | collective-permute-start | bytes 589832 | tf_op jit(solution)/shard_map/ppermute | solution.py:307
  19.1 4.7 %collective-permute-start = (bf16[128,768]{1,0:T(8,128)(2,1)}, bf16[128,768]{1,0:T(8,128)(2,1)S(1)}, u32[]{:S(2)}, u32[]{:S(2)}) collective-permute-start(bf16[128,768]{1,0:T(8,128)(2,1)} %bitcast.24), channel_id=1, source_target_pairs={{0,1},{1,0},{2,3},{3,2},{4,5},{5,4},{6,7},{7,6},{8,9},{9,8},{10,11... | collective-permute-start | bytes 589832 | tf_op jit(solution)/shard_map/ppermute | solution.py:307
  19.8 4.0 %collective-permute-start.2 = (bf16[128,384]{1,0:T(8,128)(2,1)S(1)}, bf16[128,384]{1,0:T(8,128)(2,1)S(1)}, u32[]{:S(2)}, u32[]{:S(2)}) collective-permute-start(bf16[128,384]{1,0:T(8,128)(2,1)S(1)} %collective-permute-done.1.refs_2_.g_across), channel_id=1, source_target_pairs={{0,1},{1,0},{2,3},{3,2},{4,5},{5,4},{6,7},{7,6},{8,9},{9,8},{10,11... | collective-permute-start | bytes 294920 | tf_op jit(solution)/shard_map/ppermute | solution.py:307
  21.9 30.8 %copy-start = (bf16[768,3,768]{2,0,1:T(8,128)(2,1)S(1)}, bf16[768,3,768]{2,0,1:T(8,128)(2,1)}, u32[]{:S(2)}) copy-start(bf16[768,3,768]{2,0,1:T(8,128)(2,1)} %param.8) | copy-start | bytes 10616836
  25.7 9.4 %collective-permute-start.14 = (bf16[96,1152]{1,0:T(8,128)(2,1)S(1)}, bf16[96,1152]{1,0:T(8,128)(2,1)S(1)}, u32[]{:S(2)}, u32[]{:S(2)}) collective-permute-start(bf16[96,1152]{1,0:T(8,128)(2,1)S(1)} %get-tuple-element.54), channel_id=1, source_target_pairs={{0,64},{64,0},{128,192},{192,128},{1,65},{65,1},{129,193},{193,129... | collective-permute-start | bytes 663560 | tf_op jit(solution)/shard_map/ppermute | solution.py:307
  27.3 13.3 %collective-permute-start.15 = (bf16[96,1152]{1,0:T(8,128)(2,1)S(1)}, bf16[96,1152]{1,0:T(8,128)(2,1)S(1)}, u32[]{:S(2)}, u32[]{:S(2)}) collective-permute-start(bf16[96,1152]{1,0:T(8,128)(2,1)S(1)} %get-tuple-element.55), channel_id=1, source_target_pairs={{0,128},{64,192},{128,0},{192,64},{1,129},{65,193},{129,1},{193,65... | collective-permute-start | bytes 663560 | tf_op jit(solution)/shard_map/ppermute | solution.py:307
  30.0 13.1 %collective-permute-start.16 = (bf16[96,1152]{1,0:T(8,128)(2,1)S(1)}, bf16[96,1152]{1,0:T(8,128)(2,1)S(1)}, u32[]{:S(2)}, u32[]{:S(2)}) collective-permute-start(bf16[96,1152]{1,0:T(8,128)(2,1)S(1)} %get-tuple-element.56), channel_id=1, source_target_pairs={{0,192},{64,128},{128,64},{192,0},{1,193},{65,129},{129,65},{193,1... | collective-permute-start | bytes 663560 | tf_op jit(solution)/shard_map/ppermute | solution.py:307
  30.5 4.6 %collective-permute-start.3 = (bf16[128,384]{1,0:T(8,128)(2,1)S(1)}, bf16[128,384]{1,0:T(8,128)(2,1)S(1)}, u32[]{:S(2)}, u32[]{:S(2)}) collective-permute-start(bf16[128,384]{1,0:T(8,128)(2,1)S(1)} %get-tuple-element.37), channel_id=1, source_target_pairs={{0,2},{2,0},{1,3},{3,1},{4,6},{6,4},{5,7},{7,5},{8,10},{10,8},{9,1... | collective-permute-start | bytes 294920 | tf_op jit(solution)/shard_map/ppermute | solution.py:307
  35.1 17.5 %collective-permute-start.4 = (bf16[128,384]{1,0:T(8,128)(2,1)S(1)}, bf16[128,384]{1,0:T(8,128)(2,1)S(1)}, u32[]{:S(2)}, u32[]{:S(2)}) collective-permute-start(bf16[128,384]{1,0:T(8,128)(2,1)S(1)} %collective-permute-done.3.refs_4_), channel_id=1, source_target_pairs={{0,1},{1,0},{2,3},{3,2},{4,5},{5,4},{6,7},{7,6},{8,9},{9,8},{10,11... | collective-permute-start | bytes 294920 | tf_op jit(solution)/shard_map/ppermute | solution.py:307
  43.9 13.1 %collective-permute-start.17 = (bf16[24,1152]{1,0:T(8,128)(2,1)S(1)}, bf16[24,1152]{1,0:T(8,128)(2,1)S(1)}, u32[]{:S(2)}, u32[]{:S(2)}) collective-permute-start(bf16[24,1152]{1,0:T(8,128)(2,1)S(1)} %get-tuple-element.58), channel_id=1, source_target_pairs={{0,8},{4,12},{8,0},{12,4},{16,24},{20,28},{24,16},{28,20},{1,9},{5... | collective-permute-start | bytes 165896 | tf_op jit(solution)/shard_map/ppermute | solution.py:307
  47.2 9.8 %collective-permute-start.18 = (bf16[24,1152]{1,0:T(8,128)(2,1)S(1)}, bf16[24,1152]{1,0:T(8,128)(2,1)S(1)}, u32[]{:S(2)}, u32[]{:S(2)}) collective-permute-start(bf16[24,1152]{1,0:T(8,128)(2,1)S(1)} %get-tuple-element.59), channel_id=1, source_target_pairs={{0,16},{4,20},{8,24},{12,28},{16,0},{20,4},{24,8},{28,12},{1,17},{... | collective-permute-start | bytes 165896 | tf_op jit(solution)/shard_map/ppermute | solution.py:307
  52.6 6.4 %collective-permute-start.19 = (bf16[24,1152]{1,0:T(8,128)(2,1)S(1)}, bf16[24,1152]{1,0:T(8,128)(2,1)S(1)}, u32[]{:S(2)}, u32[]{:S(2)}) collective-permute-start(bf16[24,1152]{1,0:T(8,128)(2,1)S(1)} %get-tuple-element.60), channel_id=1, source_target_pairs={{0,24},{4,28},{8,16},{12,20},{16,8},{20,12},{24,0},{28,4},{1,25},{... | collective-permute-start | bytes 165896 | tf_op jit(solution)/shard_map/ppermute | solution.py:307
  59.6 8.2 %collective-permute-start.20 = (bf16[12,576]{1,0:T(8,128)(2,1)S(1)}, bf16[12,576]{1,0:T(8,128)(2,1)S(1)}, u32[]{:S(2)}, u32[]{:S(2)}) collective-permute-start(bf16[12,576]{1,0:T(8,128)(2,1)S(1)} %get-tuple-element.62), channel_id=1, source_target_pairs={{0,32},{32,0},{1,33},{33,1},{2,34},{34,2},{3,35},{35,3},{4,36},{36... | collective-permute-start | bytes 41480 | tf_op jit(solution)/shard_map/ppermute | solution.py:307
  62.0 5.8 %collective-permute-start.21 = (bf16[12,576]{1,0:T(8,128)(2,1)S(1)}, bf16[12,576]{1,0:T(8,128)(2,1)S(1)}, u32[]{:S(2)}, u32[]{:S(2)}) collective-permute-start(bf16[12,576]{1,0:T(8,128)(2,1)S(1)} %get-tuple-element.63), channel_id=1, source_target_pairs={{0,4},{4,0},{8,12},{12,8},{16,20},{20,16},{24,28},{28,24},{1,5},{5... | collective-permute-start | bytes 41480 | tf_op jit(solution)/shard_map/ppermute | solution.py:307
  63.5 6.2 %collective-permute-start.22 = (bf16[12,576]{1,0:T(8,128)(2,1)S(1)}, bf16[12,576]{1,0:T(8,128)(2,1)S(1)}, u32[]{:S(2)}, u32[]{:S(2)}) collective-permute-start(bf16[12,576]{1,0:T(8,128)(2,1)S(1)} %get-tuple-element.64), channel_id=1, source_target_pairs={{0,36},{4,32},{8,44},{12,40},{16,52},{20,48},{24,60},{28,56},{32,4... | collective-permute-start | bytes 41480 | tf_op jit(solution)/shard_map/ppermute | solution.py:307
